TPU v7x, 32 devices: a whole 2x2x4 slice. The times are simulated.
32 devices in a mesh: dp: 16 (over z, x, core), tp: 2 (over y).
Axes of the slice: x: 2, y: 2, z: 4, core: 2. Of those that a mesh axis runs over, the one named last changes fastest.
Arguments:
- tokens: bfloat16 [8192, 768], P('dp'), may hold values from -6 to 6
- neighbours: bfloat16 [128, 128, 768], P('dp'), may hold values from -6 to 6
- out_grad: bfloat16 [8192, 768], P('dp'), may hold values from -6 to 6
- group_sizes: int32 [16], P('dp'), may hold values from 1 to 4, as said below
- seq_lengths: int32 [16, 4], P('dp'), may hold values from 0 to 512, as said below
- stretch_neighbours: int32 [128, 2], P('dp'), may hold values from 0 to 7, as said below
- norm_gain: float32 [3, 768], replicated, may hold values from 0.5 to 1.5
- norm_bias: float32 [3, 768], replicated, may hold values from -1 to 1
- self_qkv_w: bfloat16 [768, 3, 768], P(None, None, 'tp'), may hold values from -0.3125 to 0.3125
- self_qkv_b: float32 [3, 768], P(None, 'tp'), may hold values from -1 to 1
- self_out_w: bfloat16 [768, 768], P('tp'), may hold values from -0.875 to 0.875
- self_out_b: float32 [768], replicated, may hold values from -1 to 1
- cross_q_w: bfloat16 [768, 768], P(None, 'tp'), may hold values from -0.3125 to 0.3125
- cross_q_b: float32 [768], P('tp'), may hold values from -1 to 1
- cross_kv_w: bfloat16 [768, 2, 768], P(None, None, 'tp'), may hold values from -0.3125 to 0.3125
- cross_v_b: float32 [768], P('tp'), may hold values from -1 to 1
- cross_out_w: bfloat16 [768, 768], P('tp'), may hold values from -0.875 to 0.875
- cross_out_b: float32 [768], replicated, may hold values from -1 to 1
- mlp_in_w: bfloat16 [768, 3072], P(None, 'tp'), may hold values from -0.21875 to 0.21875
- mlp_in_b: float32 [3072], P('tp'), may hold values from -1 to 1
- mlp_out_w: bfloat16 [3072, 768], P('tp'), may hold values from -0.21875 to 0.21875
- mlp_out_b: float32 [768], replicated, may hold values from -1 to 1
Outputs:
- output: bfloat16 [8192, 768], P('dp', 'tp')
- tokens_grad: bfloat16 [8192, 768], P('dp', 'tp')
- neighbours_grad: bfloat16 [128, 128, 768], P('dp', None, 'tp')
- norm_gain_grad: float32 [3, 768], replicated
- norm_bias_grad: float32 [3, 768], replicated
- self_qkv_w_grad: float32 [768, 3, 768], P('dp', None, 'tp')
- self_qkv_b_grad: float32 [3, 768], P(None, 'tp')
- self_out_w_grad: float32 [768, 768], P('tp', 'dp')
- self_out_b_grad: float32 [768], replicated
- cross_q_w_grad: float32 [768, 768], P('dp', 'tp')
- cross_q_b_grad: float32 [768], P('tp')
- cross_kv_w_grad: float32 [768, 2, 768], P('dp', None, 'tp')
- cross_v_b_grad: float32 [768], P('tp')
- cross_out_w_grad: float32 [768, 768], P('tp', 'dp')
- cross_out_b_grad: float32 [768], replicated
- mlp_in_w_grad: float32 [768, 3072], P('dp', 'tp')
- mlp_in_b_grad: float32 [3072], P('tp')
- mlp_out_w_grad: float32 [3072, 768], P('tp', 'dp')
- mlp_out_b_grad: float32 [768], replicated
Inputs may be any that keep to these rules, and one draw needn't show every extreme that they name: `group_sizes`: a power of two; bucket b's padded sequence length is 512 // group_sizes[b]; some device has 1 and some has 4 in every draw. `seq_lengths`: slots at or beyond the device's group size are 0; the others lie between a quarter of the padded length and the padded length; the first slot of every device is exactly its padded length. `stretch_neighbours`: indices into the owning device's own 8 stored neighbours; the two of a block differ.
All inputs are finite; a program needn't handle non-finite values.
Results may differ from a plain program's by a relative error of at most 0.024.
The roundings to bfloat16 on the way count: a program that leaves them out, or rounds other values in their place, can miss the bound.
Values sent between devices are 32-bit elements; how exact they have to be, the bound alone decides.
No kernel may reach another device: no remote copies, remote signals or barrier semaphores. Data moves between devices by JAX's collectives and lax.ppermute only.
A program may use at most 192 MiB of HBM per device.

v0:
```python
from functools import partial
import math

import jax
import jax.numpy as jnp
from jax import lax
from jax.sharding import PartitionSpec as P

HEAD_DIM = 64
STRETCH = 64


def norm_forward(field, gain, shift):
    center = field - jnp.mean(field, axis=-1, keepdims=True)
    spread = jnp.mean(center * center, axis=-1, keepdims=True)
    return center * lax.rsqrt(spread + 1e-05) * gain + shift


def norm_backward(field, gain, shift, gradient):
    result, pullback = jax.vjp(norm_forward, field, gain, shift)
    return pullback(gradient)


def exact_gelu(field):
    return jax.nn.gelu(field, approximate=False)


def rotate(field, position, direction):
    halfway = field.shape[-1] // 2
    frequency = jnp.exp(-math.log(10000.0) * jnp.arange(halfway, dtype=jnp.float32) / halfway)
    angles = position.astype(jnp.float32)[:, None] * frequency[None, :]
    cosine = jnp.cos(angles)[:, None, :]
    sine_part = jnp.sin(angles)[:, None, :] * direction
    first_half = field[..., :halfway]
    second_half = field[..., halfway:]
    return jnp.concatenate(
        [
            first_half * cosine - second_half * sine_part,
            second_half * cosine + first_half * sine_part,
        ],
        axis=-1,
    )


def head_scores(query, key_rows, allowed):
    raw_scores = (
        jnp.einsum("qd,kd->qk", query, key_rows, preferred_element_type=jnp.float32) * 0.125
    )
    return jnp.where(allowed, raw_scores, -1e30)


def head_forward(inputs, allowed):
    query, key_rows, value_rows = inputs
    scores = head_scores(query, key_rows, allowed)
    top_score = jnp.max(scores, axis=-1, keepdims=True)
    expo = jnp.exp(scores - top_score)
    total = jnp.sum(expo, axis=-1, keepdims=True)
    probs = (expo / total).astype(jnp.bfloat16)
    mixed = jnp.einsum("qk,kd->qd", probs, value_rows, preferred_element_type=jnp.float32)
    return (mixed, top_score + jnp.log(total))


def head_backward(inputs, allowed):
    query, key_rows, value_rows, row_lse, grad_mix = inputs
    weights = jnp.exp(head_scores(query, key_rows, allowed) - row_lse)
    grad_weights = jnp.einsum("qd,kd->qk", grad_mix, value_rows, preferred_element_type=jnp.float32)
    delta = jnp.sum(weights * grad_weights, axis=-1, keepdims=True)
    grad_scores = (weights * (grad_weights - delta)).astype(jnp.bfloat16)
    grad_query = (
        jnp.einsum("qk,kd->qd", grad_scores, key_rows, preferred_element_type=jnp.float32) * 0.125
    )
    grad_keys = (
        jnp.einsum("qk,qd->kd", grad_scores, query, preferred_element_type=jnp.float32) * 0.125
    )
    grad_values = jnp.einsum(
        "qk,qd->kd", weights.astype(jnp.bfloat16), grad_mix, preferred_element_type=jnp.float32
    )
    return (grad_query, grad_keys, grad_values)


def softmax_parts(scores):
    top_score = jnp.max(scores, axis=-1, keepdims=True)
    expo = jnp.exp(scores - top_score)
    total = jnp.sum(expo, axis=-1, keepdims=True)
    return (expo / total, top_score + jnp.log(total))


def per_device(
    tokens,
    neighbours,
    out_grad,
    group_sizes,
    seq_lengths,
    stretch_neighbours,
    norm_gain,
    norm_bias,
    self_qkv_w,
    self_qkv_b,
    self_out_w,
    self_out_b,
    cross_q_w,
    cross_q_b,
    cross_kv_w,
    cross_v_b,
    cross_out_w,
    cross_out_b,
    mlp_in_w,
    mlp_in_b,
    mlp_out_w,
    mlp_out_b,
):
    count = tokens.shape[0]
    width = tokens.shape[1]
    local = self_qkv_w.shape[2]
    heads = local // HEAD_DIM
    stretches = stretch_neighbours.shape[0]
    stored = neighbours.shape[0]
    span = neighbours.shape[1]
    padded = count // group_sizes[0]
    row_ids = jnp.arange(count, dtype=jnp.int32)
    position = row_ids % padded
    sequence = row_ids // padded
    slot_ids = jnp.arange(seq_lengths.shape[1], dtype=jnp.int32)
    tok_len = jnp.sum(
        jnp.where(sequence[:, None] == slot_ids[None, :], seq_lengths[0][None, :], 0), axis=1
    )
    allowed = (
        (sequence[:, None] == sequence[None, :])
        & (position[None, :] <= position[:, None])
        & (position[None, :] < tok_len[None, :])
    )
    shifted = position + (STRETCH - 1)
    valid = ((shifted < padded) & (shifted < tok_len)).astype(jnp.float32)[:, None]
    resid = tokens.astype(jnp.float32)
    own_width = width // lax.axis_size("tp")
    own_start = lax.axis_index("tp") * own_width
    ln_one = norm_forward(resid, norm_gain[0], norm_bias[0]).astype(jnp.bfloat16)
    qkv_pre = (
        jnp.einsum("td,dcf->tcf", ln_one, self_qkv_w, preferred_element_type=jnp.float32)
        + self_qkv_b
    )
    query = rotate(qkv_pre[:, 0].reshape(count, heads, HEAD_DIM), position, 1.0).astype(
        jnp.bfloat16
    )
    key_rows = rotate(qkv_pre[:, 1].reshape(count, heads, HEAD_DIM), position, 1.0).astype(
        jnp.bfloat16
    )
    value_rows = qkv_pre[:, 2].reshape(count, heads, HEAD_DIM).astype(jnp.bfloat16)
    head_query = jnp.swapaxes(query, 0, 1)
    head_keys = jnp.swapaxes(key_rows, 0, 1)
    head_values = jnp.swapaxes(value_rows, 0, 1)
    head_mix, self_lse = lax.map(
        partial(head_forward, allowed=allowed), (head_query, head_keys, head_values)
    )
    self_mix = jnp.swapaxes(head_mix, 0, 1).reshape(count, local).astype(jnp.bfloat16)
    attn = (
        lax.psum(jnp.dot(self_mix, self_out_w, preferred_element_type=jnp.float32), "tp")
        + self_out_b
    )
    hidden_one = resid + attn
    ln_two = norm_forward(hidden_one, norm_gain[1], norm_bias[1]).astype(jnp.bfloat16)
    cross_query = (
        jnp.dot(ln_two, cross_q_w, preferred_element_type=jnp.float32) + cross_q_b
    ).astype(jnp.bfloat16)
    flat_store = neighbours.reshape(stored * span, width)
    kv_bias = jnp.stack([jnp.zeros_like(cross_v_b), cross_v_b])
    store_kv = (
        jnp.einsum("nd,dcf->ncf", flat_store, cross_kv_w, preferred_element_type=jnp.float32)
        + kv_bias
    ).astype(jnp.bfloat16)
    block_kv = store_kv.reshape(stored, span, 2, heads, HEAD_DIM)[stretch_neighbours].reshape(
        stretches, 2 * span, 2, heads, HEAD_DIM
    )
    block_keys = block_kv[:, :, 0]
    block_values = block_kv[:, :, 1]
    query_rows = jnp.roll(cross_query, -(STRETCH - 1), axis=0).reshape(
        stretches, STRETCH, heads, HEAD_DIM
    )
    cross_scores = (
        jnp.einsum("cqhd,ckhd->chqk", query_rows, block_keys, preferred_element_type=jnp.float32)
        * 0.125
    )
    cross_weights, cross_lse = softmax_parts(cross_scores)
    cross_probs = cross_weights.astype(jnp.bfloat16)
    cross_rows = jnp.einsum(
        "chqk,ckhd->cqhd", cross_probs, block_values, preferred_element_type=jnp.float32
    ).reshape(count, local)
    cross_mix = jnp.roll(cross_rows * valid, STRETCH - 1, axis=0).astype(jnp.bfloat16)
    cross = (
        lax.psum(jnp.dot(cross_mix, cross_out_w, preferred_element_type=jnp.float32), "tp")
        + cross_out_b
    )
    hidden_two = hidden_one + cross
    ln_three = norm_forward(hidden_two, norm_gain[2], norm_bias[2]).astype(jnp.bfloat16)
    pre_act = jnp.dot(ln_three, mlp_in_w, preferred_element_type=jnp.float32) + mlp_in_b
    act, gelu_pull = jax.vjp(exact_gelu, pre_act)
    act_low = act.astype(jnp.bfloat16)
    mlp = (
        lax.psum(jnp.dot(act_low, mlp_out_w, preferred_element_type=jnp.float32), "tp") + mlp_out_b
    )
    output = lax.dynamic_slice_in_dim(hidden_two + mlp, own_start, own_width, 1).astype(
        jnp.bfloat16
    )
    grad_out = out_grad.astype(jnp.float32)
    mlp_out_b_grad = jnp.sum(grad_out, axis=0)
    mlp_out_w_grad = jnp.einsum("tf,td->fd", act_low, out_grad, preferred_element_type=jnp.float32)
    grad_act = jnp.einsum("td,fd->tf", out_grad, mlp_out_w, preferred_element_type=jnp.float32)
    grad_pre = gelu_pull(grad_act)[0].astype(jnp.bfloat16)
    mlp_in_b_grad = jnp.sum(grad_pre.astype(jnp.float32), axis=0)
    mlp_in_w_grad = jnp.einsum("td,tf->df", ln_three, grad_pre, preferred_element_type=jnp.float32)
    grad_ln_three = lax.psum(
        jnp.einsum("tf,df->td", grad_pre, mlp_in_w, preferred_element_type=jnp.float32), "tp"
    )
    grad_in_three, gain_three, shift_three = norm_backward(
        hidden_two, norm_gain[2], norm_bias[2], grad_ln_three
    )
    grad_two = grad_out + grad_in_three
    grad_cross = grad_two.astype(jnp.bfloat16)
    cross_out_b_grad = jnp.sum(grad_cross.astype(jnp.float32), axis=0)
    cross_out_w_grad = jnp.einsum(
        "tf,td->fd", cross_mix, grad_cross, preferred_element_type=jnp.float32
    )
    grad_cross_mix = jnp.einsum(
        "td,fd->tf", grad_cross, cross_out_w, preferred_element_type=jnp.float32
    ).astype(jnp.bfloat16)
    grad_rows = (
        jnp.roll(grad_cross_mix, -(STRETCH - 1), axis=0) * valid.astype(jnp.bfloat16)
    ).reshape(stretches, STRETCH, heads, HEAD_DIM)
    cross_again = jnp.exp(
        jnp.einsum("cqhd,ckhd->chqk", query_rows, block_keys, preferred_element_type=jnp.float32)
        * 0.125
        - cross_lse
    )
    grad_probs = jnp.einsum(
        "cqhd,ckhd->chqk", grad_rows, block_values, preferred_element_type=jnp.float32
    )
    delta = jnp.sum(cross_again * grad_probs, axis=-1, keepdims=True)
    cross_grad_scores = (cross_again * (grad_probs - delta)).astype(jnp.bfloat16)
    grad_query_rows = (
        jnp.einsum(
            "chqk,ckhd->cqhd", cross_grad_scores, block_keys, preferred_element_type=jnp.float32
        )
        * 0.125
    )
    grad_block_keys = (
        jnp.einsum(
            "chqk,cqhd->ckhd", cross_grad_scores, query_rows, preferred_element_type=jnp.float32
        )
        * 0.125
    )
    grad_block_values = jnp.einsum(
        "chqk,cqhd->ckhd", cross_probs, grad_rows, preferred_element_type=jnp.float32
    )
    grad_query = jnp.roll(grad_query_rows.reshape(count, local), STRETCH - 1, axis=0).astype(
        jnp.bfloat16
    )
    cross_q_b_grad = jnp.sum(grad_query.astype(jnp.float32), axis=0)
    cross_q_w_grad = jnp.einsum("td,tf->df", ln_two, grad_query, preferred_element_type=jnp.float32)
    grad_ln_two_part = jnp.einsum(
        "tf,df->td", grad_query, cross_q_w, preferred_element_type=jnp.float32
    )
    grad_block_kv = jnp.stack([grad_block_keys, grad_block_values], axis=2).reshape(
        stretches * 2, span * 2 * local
    )
    owners = (
        stretch_neighbours.reshape(-1)[None, :] == jnp.arange(stored, dtype=jnp.int32)[:, None]
    ).astype(jnp.float32)
    grad_store = (
        jnp.dot(owners, grad_block_kv, precision=lax.Precision.HIGHEST)
        .reshape(stored * span, 2, local)
        .astype(jnp.bfloat16)
    )
    cross_v_b_grad = jnp.sum(grad_store[:, 1].astype(jnp.float32), axis=0)
    cross_kv_w_grad = jnp.einsum(
        "nd,ncf->dcf", flat_store, grad_store, preferred_element_type=jnp.float32
    )
    store_part = jnp.einsum(
        "ncf,dcf->nd", grad_store, cross_kv_w, preferred_element_type=jnp.float32
    ).reshape(stored, span, width)
    neighbours_grad = lax.psum_scatter(store_part, "tp", scatter_dimension=2, tiled=True).astype(
        jnp.bfloat16
    )
    grad_ln_two = lax.psum(grad_ln_two_part, "tp")
    grad_in_two, gain_two, shift_two = norm_backward(
        hidden_one, norm_gain[1], norm_bias[1], grad_ln_two
    )
    grad_one = grad_two + grad_in_two
    grad_attn = grad_one.astype(jnp.bfloat16)
    self_out_b_grad = jnp.sum(grad_attn.astype(jnp.float32), axis=0)
    self_out_w_grad = jnp.einsum(
        "tf,td->fd", self_mix, grad_attn, preferred_element_type=jnp.float32
    )
    grad_self_mix = jnp.einsum(
        "td,fd->tf", grad_attn, self_out_w, preferred_element_type=jnp.float32
    ).astype(jnp.bfloat16)
    head_grad_mix = jnp.swapaxes(grad_self_mix.reshape(count, heads, HEAD_DIM), 0, 1)
    head_dq, head_dk, head_dv = lax.map(
        partial(head_backward, allowed=allowed),
        (head_query, head_keys, head_values, self_lse, head_grad_mix),
    )
    grad_q_rot = rotate(jnp.swapaxes(head_dq, 0, 1), position, -1.0).reshape(count, local)
    grad_k_rot = rotate(jnp.swapaxes(head_dk, 0, 1), position, -1.0).reshape(count, local)
    grad_v_rows = jnp.swapaxes(head_dv, 0, 1).reshape(count, local)
    grad_qkv = jnp.stack([grad_q_rot, grad_k_rot, grad_v_rows], axis=1).astype(jnp.bfloat16)
    self_qkv_b_grad = jnp.sum(grad_qkv.astype(jnp.float32), axis=0)
    self_qkv_w_grad = jnp.einsum(
        "td,tcf->dcf", ln_one, grad_qkv, preferred_element_type=jnp.float32
    )
    grad_ln_one = lax.psum(
        jnp.einsum("tcf,dcf->td", grad_qkv, self_qkv_w, preferred_element_type=jnp.float32), "tp"
    )
    grad_in_one, gain_one, shift_one = norm_backward(resid, norm_gain[0], norm_bias[0], grad_ln_one)
    tokens_grad = lax.dynamic_slice_in_dim(grad_one + grad_in_one, own_start, own_width, 1).astype(
        jnp.bfloat16
    )
    (
        self_qkv_w_grad,
        self_out_w_grad,
        cross_q_w_grad,
        cross_kv_w_grad,
        cross_out_w_grad,
        mlp_in_w_grad,
        mlp_out_w_grad,
    ) = (
        lax.psum_scatter(self_qkv_w_grad, "dp", scatter_dimension=0, tiled=True),
        lax.psum_scatter(self_out_w_grad, "dp", scatter_dimension=1, tiled=True),
        lax.psum_scatter(cross_q_w_grad, "dp", scatter_dimension=0, tiled=True),
        lax.psum_scatter(cross_kv_w_grad, "dp", scatter_dimension=0, tiled=True),
        lax.psum_scatter(cross_out_w_grad, "dp", scatter_dimension=1, tiled=True),
        lax.psum_scatter(mlp_in_w_grad, "dp", scatter_dimension=0, tiled=True),
        lax.psum_scatter(mlp_out_w_grad, "dp", scatter_dimension=1, tiled=True),
    )
    gain_grads = jnp.stack([gain_one, gain_two, gain_three])
    shift_grads = jnp.stack([shift_one, shift_two, shift_three])
    (
        norm_gain_grad,
        norm_bias_grad,
        self_qkv_b_grad,
        self_out_b_grad,
        cross_q_b_grad,
        cross_v_b_grad,
        cross_out_b_grad,
        mlp_in_b_grad,
        mlp_out_b_grad,
    ) = lax.psum(
        (
            gain_grads,
            shift_grads,
            self_qkv_b_grad,
            self_out_b_grad,
            cross_q_b_grad,
            cross_v_b_grad,
            cross_out_b_grad,
            mlp_in_b_grad,
            mlp_out_b_grad,
        ),
        "dp",
    )
    return (
        output,
        tokens_grad,
        neighbours_grad,
        norm_gain_grad,
        norm_bias_grad,
        self_qkv_w_grad,
        self_qkv_b_grad,
        self_out_w_grad,
        self_out_b_grad,
        cross_q_w_grad,
        cross_q_b_grad,
        cross_kv_w_grad,
        cross_v_b_grad,
        cross_out_w_grad,
        cross_out_b_grad,
        mlp_in_w_grad,
        mlp_in_b_grad,
        mlp_out_w_grad,
        mlp_out_b_grad,
    )


def solution(mesh):
    placed = (
        P("dp", None),
        P("dp", None, None),
        P("dp", None),
        P("dp"),
        P("dp", None),
        P("dp", None),
        P(),
        P(),
        P(None, None, "tp"),
        P(None, "tp"),
        P("tp", None),
        P(),
        P(None, "tp"),
        P("tp"),
        P(None, None, "tp"),
        P("tp"),
        P("tp", None),
        P(),
        P(None, "tp"),
        P("tp"),
        P("tp", None),
        P(),
    )
    return jax.shard_map(
        per_device,
        mesh=mesh,
        in_specs=placed,
        out_specs=(
            P("dp", "tp"),
            P("dp", "tp"),
            P("dp", None, "tp"),
            P(),
            P(),
            P("dp", None, "tp"),
            P(None, "tp"),
            P("tp", "dp"),
            P(),
            P("dp", "tp"),
            P("tp"),
            P("dp", None, "tp"),
            P("tp"),
            P("tp", "dp"),
            P(),
            P("dp", "tp"),
            P("tp"),
            P("tp", "dp"),
            P(),
        ),
        check_vma=False,
    )
```

profile of v0, /device:TPU:0, one launch (start us, length us, event | category | flops | bytes accessed | tf_op | source)
XLA Modules:
  0.0 986.2 jit_solution(2578824090523314707)
XLA Ops:
  11.8 2.8 convolution_add_fusion.1
  20.6 2.4 subtract_convert_fusion.2
  24.2 2.2 copy.158
  28.2 2.2 copy.159
  30.4 20.7 %while.30 = (s32[]{:T(128)}, bf16[6,512,64]{1,2,0:T(8,128)(2,1)S(1)}, f32[6,512,1]{1,2,0:T(1,128)}, bf16[6,512,64]{2,1,0:T(8,128)(2,1)}, bf16[6,512,64]{2,1,0:T(...) while((s32[]{:T(128)}, ...), condition=%wide.region_6.7_spmd.clone.clone, body=%wide.region_3.6_spmd.clone.sunk.clone | while | flops 70254080 | bytes 3701353 | solution.py:152
  51.1 3.1 fusion.123
  55.1 4.3 add_convert_fusion.1
  59.4 2.7 copy.162
  62.1 2.0 copy.197
  65.8 4.0 gather_fusion
  69.8 6.0 copy.165
  75.8 5.6 reshape.384
  81.4 3.8 fusion.120
  85.3 23.3 %all-reduce.11.cloned.1.call-done = f32[512,768]{1,0:T(8,128)} async-done(((f32[512,768]{1,0:T(8,128)}), f32[512,768]{1,0:T(8,128)}) %all-reduce.11.cloned.1.call-update) | async-done | bytes 1572880 | tf_op jit(solution)/shard_map/psum | solution.py:157
  114.5 2.3 copy.181
  116.8 2.8 multiply_reduce_fusion.2
  122.2 2.4 convolution_bitcast_fusion.6
  124.6 2.1 copy.170
  126.6 2.6 reshape.386
  131.3 2.0 fusion.82
  134.4 50.7 %all-reduce.13.cloned.1.call-done = f32[512,768]{1,0:T(8,128)} async-done(((f32[512,768]{1,0:T(8,128)}), f32[512,768]{1,0:T(8,128)}) %all-reduce.13.cloned.1.call-update) | async-done | bytes 1572880 | tf_op jit(solution)/shard_map/psum | solution.py:190
  185.0 2.3 fusion.117
  190.1 10.2 %convert_reduce_fusion = (f32[1536]{0:T(1024)}, bf16[512,1536]{1,0:T(8,128)(2,1)S(1)}, f32[512,1536]{1,0:T(8,128)}) fusion(f32[512,1536]{1,0:T(8,128)S(1)} %convolution_add_fusion, bf16[512,768]{1,0:T(8,128)(2,1)S(1)} %copy-done.17, bf16[1536,768]{1,0:T(8,128)(2,1)S(1)} %copy-done), kind=kOutput, calls=%fused_computation.61 | convolution fusion | flops 1266153984 | bytes 11016192 | tf_op jit(solution)/shard_map/td,fd->tf/dot_general | solution.py:207
  201.5 2.6 fusion.125
  205.5 3.6 multiply_convert_fusion.2
  210.2 2.5 fusion.124
  212.7 43.0 %all-reduce.15.cloned.1.call-done = f32[512,768]{1,0:T(8,128)} async-done(((f32[512,768]{1,0:T(8,128)}), f32[512,768]{1,0:T(8,128)}) %all-reduce.15.cloned.1.call-update) | async-done | bytes 1572880 | tf_op jit(solution)/shard_map/psum | solution.py:211
  255.7 3.2 multiply_reduce_fusion.3
  264.7 3.7 multiply_reduce_fusion.1
  271.0 2.2 multiply_bitcast_fusion
  277.3 3.8 convolution_bitcast_fusion.2
  281.1 3.4 pad_maximum_fusion
  284.5 13.7 %copy.183 = f32[8,256,2,6,64]{4,3,2,1,0:T(8,128)} copy(f32[8,256,2,6,64]{1,4,3,0,2:T(8,128)} %pad_maximum_fusion) | data formatting | bytes 12582912 | tf_op jit(solution)/shard_map/stack | solution.py:262
  298.1 14.9 %reshape.389 = f32[16,98304]{1,0:T(8,128)} reshape(f32[8,256,2,6,64]{4,3,2,1,0:T(8,128)} %copy.183) | data formatting | bytes 12582912 | tf_op jit(solution)/shard_map/reshape | solution.py:262
  313.1 6.3 convolution_convert_fusion
  319.4 2.7 convert_element_type.173
  322.1 4.9 convolution_bitcast_fusion.4
  327.0 5.3 copy.188
  333.7 2.7 multiply_reduce_fusion.4
  341.5 57.1 %while.31 = (s32[]{:T(128)}, f32[6,512,64]{1,2,0:T(8,128)}, f32[6,512,64]{1,2,0:T(8,128)}, bf16[6,512,64]{1,2,0:T(8,128)(2,1)}, bf16[6,512,64]{2,1,0:T(8,128)(2,...) while((s32[]{:T(128)}, f32[6,512,64]{1,2,0:T(8,128)}, ...), condition=%wide.region_25.26_spmd.clone.clone, body=%wide.region_23.25_spmd.clone.sunk.clone | while | flops 171245056 | bytes 12345017 | solution.py:297
  347.3 2.0 fusion.206
  356.8 2.0 fusion.206
  366.3 2.0 fusion.206
  375.8 2.0 fusion.206
  385.3 2.0 fusion.206
  394.9 2.0 fusion.206
  402.2 4.0 convolution_bitcast_fusion.5
  407.7 4.5 convolution_bitcast_fusion.3
  417.1 3.2 fusion.108
  420.4 5.2 fusion.111
  426.7 5.0 fusion.126
  432.7 4.4 fusion.78
  439.5 3.6 fusion.62
  445.9 72.7 %all-reduce.21.cloned.1.call-done = (f32[512,768]{1,0:T(8,128)}, f32[512,768]{1,0:T(8,128)}) async-done(((f32[512,768]{1,0:T(8,128)}, f32[512,768]{1,0:T(8,128)}), (f32[512,768]{1,0:T(8,128)}, f32[512,768]{1,0:T(8,128)})) %all-reduce.21.cloned.1.call-update) | async-done | bytes 3145744 | tf_op jit(solution)/shard_map/psum | solution.py:199
  518.6 2.1 fusion.59
  520.8 61.8 %all-reduce.2 = (f32[3,768]{1,0:T(4,128)}, f32[3,768]{1,0:T(4,128)}, f32[3,384]{1,0:T(4,128)}, f32[768]{0:T(1024)}, f32[384]{0:T(512)}, /*index=5*/f32[384]{0:T(...) all-reduce(f32[3,768]{1,0:T(4,128)S(1)} %pad_maximum_fusion.12, ...), channel_id=1, replica_groups=mesh['dp'=16,'tp'=2] {'dp'}, use_global_device_ids=true, to_apply=%region_33.34 | all-reduce | flops 10368 | bytes 82944 | tf_op jit(solution)/shard_map/psum | solution.py:345
  582.6 2.2 fusion.114
  587.3 2.4 convert_element_type.169
  589.7 37.0 %reduce-scatter.16.cloned.1.call-done = f32[384,48]{0,1:T(8,128)} async-done(((f32[384,768]{0,1:T(8,128)}), f32[384,48]{0,1:T(8,128)}) %reduce-scatter.16.cloned.1.call-update) | async-done | bytes 73744 | tf_op jit(solution)/shard_map/reduce_scatter | solution.py:329
  626.7 61.4 %reduce-scatter.14.cloned.1.call-done = f32[48,384]{1,0:T(8,128)} async-done(((f32[768,384]{1,0:T(8,128)}), f32[48,384]{1,0:T(8,128)}) %reduce-scatter.14.cloned.1.call-update) | async-done | bytes 73744 | tf_op jit(solution)/shard_map/reduce_scatter | solution.py:327
  688.2 61.3 %reduce-scatter.12.cloned.1.call-done = f32[384,48]{0,1:T(8,128)} async-done(((f32[384,768]{0,1:T(8,128)}), f32[384,48]{0,1:T(8,128)}) %reduce-scatter.12.cloned.1.call-update) | async-done | bytes 73744 | tf_op jit(solution)/shard_map/reduce_scatter | solution.py:326
  749.4 79.0 %reduce-scatter.18.cloned.1.call-done = f32[48,1536]{1,0:T(8,128)} async-done(((f32[768,1536]{1,0:T(8,128)}), f32[48,1536]{1,0:T(8,128)}) %reduce-scatter.18.cloned.1.call-update) | async-done | bytes 294928 | tf_op jit(solution)/shard_map/reduce_scatter | solution.py:330
  828.4 79.1 %reduce-scatter.20.cloned.1.call-done = f32[1536,48]{0,1:T(8,128)} async-done(((f32[1536,768]{0,1:T(8,128)}), f32[1536,48]{0,1:T(8,128)}) %reduce-scatter.20.cloned.1.call-update) | async-done | bytes 294928 | tf_op jit(solution)/shard_map/reduce_scatter | solution.py:331
  907.5 71.9 %reduce-scatter.10.cloned.1.call-done = f32[48,3,384]{2,0,1:T(8,128)} async-done(((f32[768,3,384]{2,0,1:T(8,128)}), f32[48,3,384]{2,0,1:T(8,128)}) %reduce-scatter.10.cloned.1.call-update) | async-done | bytes 221200 | tf_op jit(solution)/shard_map/reduce_scatter | solution.py:325
  (436 shorter events, 135.9 us)
Async XLA Ops:
  7.2 182.9 %copy-start = (bf16[1536,768]{1,0:T(8,128)(2,1)S(1)}, bf16[1536,768]{1,0:T(8,128)(2,1)}, u32[]{:S(2)}) copy-start(bf16[1536,768]{1,0:T(8,128)(2,1)} %param.46) | copy-start | bytes 7077892
  7.2 3.0 copy-start.9
  7.2 101.4 %all-reduce.11.cloned.1.call-start = ((), (), s32[]{:S(2)}) async-start(), calls=%async_computation.7 | async-start | bytes 3145728 | tf_op jit(solution)/shard_map/psum | solution.py:157
  8.6 3.1 copy-start.108
  8.7 10.3 %copy-start.29 = (bf16[6,512,64]{1,2,0:T(8,128)(2,1)}, bf16[6,512,64]{1,2,0:T(8,128)(2,1)S(1)}, u32[]{:S(2)}) copy-start(bf16[6,512,64]{1,2,0:T(8,128)(2,1)S(1)} %fusion.122) | copy-start | bytes 1179652
  10.2 4.5 copy-start.68
  11.1 3.5 copy-start.74
  11.8 2.9 copy-start.66
  11.8 2.9 copy-start.97
  24.2 6.2 copy-start.34
  24.2 6.2 copy-start.90
  51.1 3.1 copy-start.32
  51.1 3.8 copy-start.95
  54.2 130.8 %all-reduce.13.cloned.1.call-start = ((), (), s32[]{:S(2)}) async-start(), calls=%async_computation.8 | async-start | bytes 3145728 | tf_op jit(solution)/shard_map/psum | solution.py:190
  81.4 27.2 %copy-start.101 = (f32[768]{0:T(1024)S(1)}, f32[768]{0:T(1024)}, u32[]{:S(2)}) copy-start(f32[768]{0:T(1024)} %param.37) | copy-start | bytes 9220
  119.6 85.2 %copy-start.60 = (f32[8,6,64]{2,1,0:T(8,128)}, f32[8,6,64]{2,1,0:T(8,128)S(1)}, u32[]{:S(2)}) copy-start(f32[8,6,64]{2,1,0:T(8,128)S(1)} %get-tuple-element.443) | copy-start | bytes 36868
  120.7 84.1 %copy-start.64 = (f32[8,6,64]{2,1,0:T(8,128)}, f32[8,6,64]{2,1,0:T(8,128)S(1)}, u32[]{:S(2)}) copy-start(f32[8,6,64]{2,1,0:T(8,128)S(1)} %fusion.50) | copy-start | bytes 36868
  126.6 2.6 copy-start.87
  131.3 53.7 %copy-start.94 = (f32[768]{0:T(1024)S(1)}, f32[768]{0:T(1024)}, u32[]{:S(2)}) copy-start(f32[768]{0:T(1024)} %param.43) | copy-start | bytes 9220
  133.3 122.4 %all-reduce.15.cloned.1.call-start = ((), (), s32[]{:S(2)}) async-start(), calls=%async_computation.9 | async-start | bytes 3145728 | tf_op jit(solution)/shard_map/psum | solution.py:211
  185.0 3.5 copy-start.106
  187.7 71.3 %copy-start.76 = (f32[512]{0:T(512)}, f32[512]{0:T(512)S(1)}, u32[]{:S(2)}) copy-start(f32[512]{0:T(512)S(1)} %fusion.101) | copy-start | bytes 6148
  190.1 10.2 %copy-start.37 = (f32[512,1536]{1,0:T(8,128)}, f32[512,1536]{1,0:T(8,128)S(1)}, u32[]{:S(2)}) copy-start(f32[512,1536]{1,0:T(8,128)S(1)} %convolution_add_fusion) | copy-start | bytes 9437188
  204.1 128.5 %all-reduce.17.cloned.1.call-start = ((), (), s32[]{:S(2)}) async-start(), calls=%async_computation.10 | async-start | bytes 3145728 | tf_op jit(solution)/shard_map/psum | solution.py:283
  212.7 46.2 %copy-start.7 = (f32[512,768]{1,0:T(8,128)S(1)}, f32[512,768]{1,0:T(8,128)}, u32[]{:S(2)}) copy-start(f32[512,768]{1,0:T(8,128)} %copy-done.6) | copy-start | bytes 4718596
  255.7 3.2 copy-start.23
  264.7 3.7 copy-start.35
  264.7 3.7 copy-start.5
  276.8 166.3 %all-reduce.19.cloned.1.call-start = ((), (), s32[]{:S(2)}) async-start(), calls=%async_computation.18 | async-start | bytes 4718592
  277.3 3.8 copy-start.14
  298.1 14.9 %copy-start.102 = (s32[16]{0:T(128)S(1)}, s32[16]{0:T(128)}, u32[]{:S(2)}) copy-start(s32[16]{0:T(128)} %eq.52) | copy-start | bytes 196
  322.1 4.9 copy-start.20
  332.4 186.2 %all-reduce.21.cloned.1.call-start = ((), (), s32[]{:S(2)}) async-start(), calls=%async_computation.19 | async-start | bytes 6291456 | tf_op jit(solution)/shard_map/psum | solution.py:199
  333.7 3.4 copy-start.22
  341.5 58.4 %copy-start.54 = (f32[512,32]{0,1:T(8,128)S(1)}, f32[512,32]{0,1:T(8,128)}, u32[]{:S(2)}) copy-start(f32[512,32]{0,1:T(8,128)} %copy-done.53) | copy-start | bytes 196612
  341.5 58.4 %copy-start.63 = (f32[512,32]{0,1:T(8,128)S(1)}, f32[512,32]{0,1:T(8,128)}, u32[]{:S(2)}) copy-start(f32[512,32]{0,1:T(8,128)} %get-tuple-element.438) | copy-start | bytes 196612
  347.3 3.8 copy-start.31
  356.8 3.8 copy-start.31
  366.3 3.8 copy-start.31
  375.8 3.8 copy-start.31
  385.3 3.8 copy-start.31
  394.8 3.8 copy-start.31
  401.9 4.3 copy-start.48
  402.2 4.1 copy-start.50
  406.2 181.1 %reduce-scatter.8.cloned.1.call-start = ((), (), s32[]{:S(2)}) async-start(), calls=%async_computation.11 | async-start | bytes 4718592 | tf_op jit(solution)/shard_map/reduce_scatter | solution.py:280
  412.2 3.0 copy-start.39
  412.2 3.0 copy-start.44
  412.2 214.5 %reduce-scatter.16.cloned.1.call-start = ((), (), s32[]{:S(2)}) async-start(), calls=%async_computation.15 | async-start | bytes 1253376 | tf_op jit(solution)/shard_map/reduce_scatter | solution.py:329
  415.1 273.0 %reduce-scatter.14.cloned.1.call-start = ((), (), s32[]{:S(2)}) async-start(), calls=%async_computation.14 | async-start | bytes 1253376 | tf_op jit(solution)/shard_map/reduce_scatter | solution.py:327
  417.0 3.4 copy-start.8
  417.0 3.4 copy-start.77
  417.0 3.4 copy-start.100
  417.0 332.4 %reduce-scatter.12.cloned.1.call-start = ((), (), s32[]{:S(2)}) async-start(), calls=%async_computation.13 | async-start | bytes 1253376 | tf_op jit(solution)/shard_map/reduce_scatter | solution.py:326
  420.3 408.2 %reduce-scatter.18.cloned.1.call-start = ((), (), s32[]{:S(2)}) async-start(), calls=%async_computation.16 | async-start | bytes 5013504 | tf_op jit(solution)/shard_map/reduce_scatter | solution.py:330
  425.6 482.0 %reduce-scatter.20.cloned.1.call-start = ((), (), s32[]{:S(2)}) async-start(), calls=%async_computation.17 | async-start | bytes 5013504 | tf_op jit(solution)/shard_map/reduce_scatter | solution.py:331
  431.8 547.7 %reduce-scatter.10.cloned.1.call-start = ((), (), s32[]{:S(2)}) async-start(), calls=%async_computation.12 | async-start | bytes 3760128 | tf_op jit(solution)/shard_map/reduce_scatter | solution.py:325
  437.1 7.5 copy-start.85
  437.1 7.5 copy-start.84
  439.4 5.2 copy-start.49
  444.7 76.1 %copy-start.80 = (f32[768]{0:T(1024)S(1)}, f32[768]{0:T(1024)}, u32[]{:S(2)}) copy-start(f32[768]{0:T(1024)} %get-tuple-element.401) | copy-start | bytes 9220
  444.7 76.1 %copy-start.81 = (f32[768]{0:T(1024)S(1)}, f32[768]{0:T(1024)}, u32[]{:S(2)}) copy-start(f32[768]{0:T(1024)} %get-tuple-element.431) | copy-start | bytes 9220
  444.7 76.1 %copy-start.88 = (f32[1536]{0:T(1024)S(1)}, f32[1536]{0:T(1024)}, u32[]{:S(2)}) copy-start(f32[1536]{0:T(1024)} %get-tuple-element.398) | copy-start | bytes 18436
  444.7 137.8 %copy-start.72 = (f32[512]{0:T(512)S(1)}, f32[512]{0:T(512)}, u32[]{:S(2)}) copy-start(f32[512]{0:T(512)} %copy-done.71) | copy-start | bytes 6148
  586.4 393.0 %copy-start.1 = (bf16[1536,768]{1,0:T(8,128)(2,1)S(1)}, bf16[1536,768]{1,0:T(8,128)(2,1)}, u32[]{:S(2)}) copy-start(bf16[1536,768]{1,0:T(8,128)(2,1)} %param.46) | copy-start | bytes 7077892
  (71 other events, 104.5 us)
Sparse Core Ops, SparseCore 0:
  54.3 54.2 all-reduce.10
  133.5 51.5 all-reduce.12
  204.2 51.5 all-reduce.14
  276.9 51.5 all-reduce.16
  332.5 98.9 all-reduce.18
  433.7 84.8 all-reduce.20
  520.8 43.4 reduce-scatter.7
  568.5 58.1 reduce-scatter.15
  630.9 57.1 reduce-scatter.13
  692.2 57.1 reduce-scatter.11
  753.9 74.5 reduce-scatter.17
  832.7 74.7 reduce-scatter.19
  912.0 67.3 reduce-scatter.9
where the time goes:
time: 995 us; the launch traced here: 986 us
  waiting for transfers between devices  580 us (58%)
  matrix products  152 us (15%)
  local copies, waits for them, and re-layouts  117 us (12%)
  blocking collectives  61.8 us (6%)
  other arithmetic  57.1 us (6%)
  between operations  16.9 us (2%)
    reduce_scatter x1, waiting for transfers between devices, per_device(): lax.psum_scatter(mlp_out_w_grad, 'dp', scatter_dimension=1, tiled=True)  79.1 us
    reduce_scatter x1, waiting for transfers between devices, per_device(): lax.psum_scatter(mlp_in_w_grad, 'dp', scatter_dimension=0, tiled=True)  79 us
    psum x1, waiting for transfers between devices, per_device(): lax.psum(jnp.dot(act_low, mlp_out_w, preferred_element_type=jnp.float32),...  72.7 us
    reduce_scatter x1, waiting for transfers between devices, per_device(): lax.psum_scatter(self_qkv_w_grad, 'dp', scatter_dimension=0, tiled=True)  71.9 us
    psum x1, blocking collectives, per_device(): lax.psum((gain_grads, shift_grads, self_qkv_b_grad, self_out_b_grad, cros...  61.8 us
    reduce_scatter x1, waiting for transfers between devices, per_device(): lax.psum_scatter(cross_q_w_grad, 'dp', scatter_dimension=0, tiled=True)  61.4 us
    reduce_scatter x1, waiting for transfers between devices, per_device(): lax.psum_scatter(self_out_w_grad, 'dp', scatter_dimension=1, tiled=True)  61.3 us
    psum x1, waiting for transfers between devices, per_device(): lax.psum(jnp.dot(cross_mix, cross_out_w, preferred_element_type=jnp.float...  50.7 us
  transfers between devices with their start and end apart: 13, of which 10 were waited for; matrix products, arithmetic and copies ran while one was open for 21% of the time, Pallas kernels for 0%

commit v1 on v0

v1 whole, which is shorter than its diff:
```python
from functools import partial
import math

import jax
import jax.numpy as jnp
from jax import lax
from jax.experimental import pallas as pl
from jax.experimental.pallas import tpu as pltpu
from jax.sharding import PartitionSpec as P

HEAD_DIM = 64
STRETCH = 64
LANES = 128
F32 = jnp.float32
BF16 = jnp.bfloat16
TILE = 128


def dot(left, right):
    return lax.dot_general(left, right, (((1,), (0,)), ((), ())), preferred_element_type=F32)


def dot_t(left, right):
    return lax.dot_general(left, right, (((1,), (1,)), ((), ())), preferred_element_type=F32)


def tdot(left, right):
    return lax.dot_general(left, right, (((0,), (0,)), ((), ())), preferred_element_type=F32)


def norm_stats(field):
    center = field - jnp.mean(field, axis=-1, keepdims=True)
    spread = jnp.mean(center * center, axis=-1, keepdims=True)
    scale = lax.rsqrt(spread + 1e-05)
    return center * scale, scale


def norm_back(xhat, scale, gain, gradient):
    scaled = gradient * gain
    first = jnp.mean(scaled, axis=-1, keepdims=True)
    second = jnp.mean(scaled * xhat, axis=-1, keepdims=True)
    return scale * (scaled - first - xhat * second)


def lane_ids(rows):
    return lax.broadcasted_iota(jnp.int32, (rows, LANES), 1)


def turn(field, cosine, sine, direction):
    lane = lane_ids(field.shape[0])
    ahead = pltpu.roll(field, LANES - HEAD_DIM // 2, 1)
    behind = pltpu.roll(field, HEAD_DIM // 2, 1)
    crossed = jnp.where((lane & (HEAD_DIM - 1)) < HEAD_DIM // 2, -ahead, behind)
    return field * cosine + crossed * (sine * direction)


def two_heads(field):
    low = lane_ids(field.shape[0]) < HEAD_DIM
    zero = jnp.zeros_like(field)
    return jnp.concatenate([jnp.where(low, field, zero), jnp.where(low, zero, field)], axis=0)


def join_heads(field):
    half = field.shape[0] // 2
    return jnp.where(lane_ids(half) < HEAD_DIM, field[:half], field[half:])


def two_columns(columns, first):
    lane = lane_ids(columns.shape[0])
    parts = [
        jnp.sum(jnp.where(lane == first + head, columns, 0.0), axis=-1, keepdims=True)
        for head in range(2)
    ]
    return jnp.concatenate(parts, axis=0)


def put_columns(columns, values, first):
    half = columns.shape[0]
    lane = lane_ids(half)
    columns = jnp.where(lane == first, values[:half], columns)
    return jnp.where(lane == first + 1, values[half:], columns)


def slot_length(ids, info, slots):
    length = jnp.zeros_like(ids)
    for slot in range(slots):
        length = jnp.where(ids >= slot * info[0], info[3 + slot], length)
    return length


def fill_mask(bias_ref, info, slots):
    count = bias_ref.shape[0]
    padded = info[0]
    for start in range(0, count, TILE):
        shape = (TILE, start + TILE)
        rows = lax.broadcasted_iota(jnp.int32, shape, 0) + start
        keys = lax.broadcasted_iota(jnp.int32, shape, 1)
        place = keys & (padded - 1)
        allowed = (
            (keys <= rows)
            & (keys >= rows - (rows & (padded - 1)))
            & (place < slot_length(keys, info, slots))
        )
        bias_ref[start : start + TILE, : start + TILE] = jnp.where(allowed, 0.0, -1e30)


def valid_rows(count, info, slots):
    rows = lax.broadcasted_iota(jnp.int32, (count, LANES), 0)
    shifted = (rows & (info[0] - 1)) + (STRETCH - 1)
    return (shifted < info[0]) & (shifted < slot_length(rows, info, slots))


def join_peer(peer_ref, near_ref, far_ref, core):
    half = near_ref.shape[0]
    peer_ref[pl.ds(pl.multiple_of(core * half, 64), half), :] = near_ref[...].astype(BF16)
    peer_ref[pl.ds(pl.multiple_of((1 - core) * half, 64), half), :] = far_ref[...].astype(BF16)


def self_forward(slots, info, tok, weight, bias, gain, shift, cosine, sine, ln_out, qkv_out, mix_out, lse_out, mask_out):
    count = tok.shape[0]
    pairs = weight.shape[2] // LANES
    fill_mask(mask_out, info, slots)
    step = 256

    def project(index, carry):
        rows = pl.ds(pl.multiple_of(index * step, step), step)
        xhat, _ = norm_stats(tok[rows, :].astype(F32))
        ln = (xhat * gain[...] + shift[...]).astype(BF16)
        ln_out[rows, :] = ln
        for part in range(3):
            made = dot(ln, weight[part]) + bias[part : part + 1, :]
            for pair in range(pairs):
                piece = made[:, pair * LANES : (pair + 1) * LANES]
                if part < 2:
                    piece = turn(piece, cosine[rows, :], sine[rows, :], 1.0)
                qkv_out[part * pairs + pair, rows, :] = piece.astype(BF16)
        return carry

    lax.fori_loop(0, count // step, project, 0)

    def attend(pair, carry):
        columns = pl.ds(pl.multiple_of(pair * LANES, LANES), LANES)
        for start in range(0, count, TILE):
            rows = slice(start, start + TILE)
            span = slice(0, start + TILE)
            query = two_heads(qkv_out[pair, rows, :] * BF16(0.125))
            scores = dot_t(query, qkv_out[pairs + pair, span, :])
            mask = mask_out[rows, span]
            scores = scores + jnp.concatenate([mask, mask], axis=0)
            top = jnp.max(scores, axis=-1, keepdims=True)
            expo = jnp.exp(scores - top)
            total = jnp.sum(expo, axis=-1, keepdims=True)
            probs = (expo * (1.0 / total)).astype(BF16)
            mixed = join_heads(dot(probs, qkv_out[2 * pairs + pair, span, :]))
            mix_out[rows, columns] = mixed.astype(BF16).astype(F32)
            lse_out[rows, :] = put_columns(lse_out[rows, :], top + jnp.log(total), 2 * pair)
        return carry

    lax.fori_loop(0, pairs, attend, 0)


def cross_forward(
    slots, span, info, picks, tok, mix_own, mix_peer, w_own, w_near, w_far, out_bias, gain, shift, q_w, q_b, kv,
    hidden_out, ln_out, query_out, mix_out, lse_out, w_peer, field,
):
    count = tok.shape[0]
    local = q_w.shape[1]
    pairs = local // LANES
    join_peer(w_peer, w_near, w_far, info[2])
    step = 256

    def project(index, carry):
        rows = pl.ds(pl.multiple_of(index * step, step), step)
        attn = dot(mix_own[rows, :].astype(BF16), w_own[...]) + dot(
            mix_peer[rows, :].astype(BF16), w_peer[...]
        )
        hidden = tok[rows, :].astype(F32) + (attn + out_bias[...])
        hidden_out[rows, :] = hidden
        xhat, _ = norm_stats(hidden)
        ln = (xhat * gain[...] + shift[...]).astype(BF16)
        ln_out[rows, :] = ln
        field[rows, :] = dot(ln, q_w[...]) + q_b[...]
        return carry

    lax.fori_loop(0, count // step, project, 0)
    for pair in range(pairs):
        columns = slice(pair * LANES, (pair + 1) * LANES)
        query_out[:, columns] = pltpu.roll(field[:, columns], count - (STRETCH - 1), 0).astype(BF16)

    def block(index, carry):
        rows = pl.ds(pl.multiple_of(index * STRETCH, STRETCH), STRETCH)
        near = pl.ds(pl.multiple_of(picks[index, 0] * span, span), span)
        far = pl.ds(pl.multiple_of(picks[index, 1] * span, span), span)
        lse = jnp.zeros((STRETCH, LANES), F32)
        for pair in range(pairs):
            columns = slice(pair * LANES, (pair + 1) * LANES)
            values = slice(local + pair * LANES, local + (pair + 1) * LANES)
            query = two_heads(query_out[rows, columns] * BF16(0.125))
            keys = jnp.concatenate([kv[near, columns], kv[far, columns]], axis=0)
            vals = jnp.concatenate([kv[near, values], kv[far, values]], axis=0)
            scores = dot_t(query, keys)
            top = jnp.max(scores, axis=-1, keepdims=True)
            expo = jnp.exp(scores - top)
            total = jnp.sum(expo, axis=-1, keepdims=True)
            probs = (expo * (1.0 / total)).astype(BF16)
            field[rows, columns] = join_heads(dot(probs, vals))
            lse = put_columns(lse, top + jnp.log(total), 2 * pair)
        lse_out[rows, :] = lse
        return carry

    lax.fori_loop(0, picks.shape[0], block, 0)
    valid = valid_rows(count, info, slots)
    for pair in range(pairs):
        columns = slice(pair * LANES, (pair + 1) * LANES)
        kept = jnp.where(valid, field[:, columns], 0.0)
        mix_out[:, columns] = pltpu.roll(kept, STRETCH - 1, 0).astype(BF16).astype(F32)


def gelu_parts(field):
    upper = 0.5 * (1.0 + lax.erf(field * (1.0 / math.sqrt(2.0))))
    density = jnp.exp(field * field * -0.5) * (1.0 / math.sqrt(2.0 * math.pi))
    return field * upper, upper + field * density


def feed_forward(
    info, hidden_one, mix_own, mix_peer, w_own, w_near, w_far, out_bias, gain, shift, in_w, in_b, out_w, end_bias, grad,
    hidden_out, ln_out, act_out, pre_out, keep_out, send_out, part_out, bias_out, w_peer,
):
    @pl.when(pl.program_id(0) == 0)
    def _():
        join_peer(w_peer, w_near, w_far, info[2])
        bias_out[...] = jnp.zeros_like(bias_out)

    half = keep_out.shape[1]
    own = pl.ds(pl.multiple_of(info[1] * half, LANES), half)
    peer = pl.ds(pl.multiple_of((1 - info[1]) * half, LANES), half)
    cross = dot(mix_own[...].astype(BF16), w_own[...]) + dot(mix_peer[...].astype(BF16), w_peer[...])
    hidden = hidden_one[...] + (cross + out_bias[...])
    hidden_out[...] = hidden
    xhat, _ = norm_stats(hidden)
    ln = (xhat * gain[...] + shift[...]).astype(BF16)
    ln_out[...] = ln
    act, slope = gelu_parts(dot(ln, in_w[...]) + in_b[...])
    act = act.astype(BF16)
    act_out[...] = act
    grad_pre = (dot_t(grad[...], out_w[...]) * slope).astype(BF16)
    pre_out[...] = grad_pre
    bias_out[...] += jnp.sum(grad_pre.astype(F32), axis=0, keepdims=True)
    part_out[...] = dot_t(grad_pre, in_w[...])
    keep_out[...] = dot(act, out_w[:, own]) + (hidden_out[:, own] + end_bias[:, own])
    send_out[...] = dot(act, out_w[:, peer])


def cross_backward(
    slots, span, info, picks, part_own, part_peer, hidden, out_grad, gain, out_w, query, kv, lse,
    grad_out, low_out, query_out, query_low, store_out, gain_out, shift_out, bias_out, q_bias_out, v_bias_out,
    rows_grad, field, store,
):
    count = hidden.shape[0]
    local = query.shape[1]
    pairs = local // LANES
    step = 256
    gain_out[...] = jnp.zeros_like(gain_out)
    shift_out[...] = jnp.zeros_like(shift_out)
    bias_out[...] = jnp.zeros_like(bias_out)
    store[...] = jnp.zeros_like(store)

    def project(index, carry):
        rows = pl.ds(pl.multiple_of(index * step, step), step)
        gradient = part_own[rows, :] + part_peer[rows, :]
        xhat, scale = norm_stats(hidden[rows, :])
        gain_out[...] += jnp.sum(gradient * xhat, axis=0, keepdims=True)
        shift_out[...] += jnp.sum(gradient, axis=0, keepdims=True)
        two = out_grad[rows, :].astype(F32) + norm_back(xhat, scale, gain[...], gradient)
        grad_out[rows, :] = two
        low = two.astype(BF16)
        low_out[rows, :] = low
        bias_out[...] += jnp.sum(low.astype(F32), axis=0, keepdims=True)
        field[rows, :] = dot_t(low, out_w[...])
        return carry

    lax.fori_loop(0, count // step, project, 0)
    valid = valid_rows(count, info, slots)
    for pair in range(pairs):
        columns = slice(pair * LANES, (pair + 1) * LANES)
        moved = pltpu.roll(field[:, columns].astype(BF16).astype(F32), count - (STRETCH - 1), 0)
        rows_grad[:, columns] = jnp.where(valid, moved, 0.0).astype(BF16)

    def block(index, carry):
        rows = pl.ds(pl.multiple_of(index * STRETCH, STRETCH), STRETCH)
        near = pl.ds(pl.multiple_of(picks[index, 0] * span, span), span)
        far = pl.ds(pl.multiple_of(picks[index, 1] * span, span), span)
        logs = lse[rows, :]
        for pair in range(pairs):
            columns = slice(pair * LANES, (pair + 1) * LANES)
            values = slice(local + pair * LANES, local + (pair + 1) * LANES)
            query_two = two_heads(query[rows, columns] * BF16(0.125))
            grad_two = two_heads(rows_grad[rows, columns])
            keys = jnp.concatenate([kv[near, columns], kv[far, columns]], axis=0)
            vals = jnp.concatenate([kv[near, values], kv[far, values]], axis=0)
            probs = jnp.exp(dot_t(query_two, keys) - two_columns(logs, 2 * pair))
            grad_probs = dot_t(grad_two, vals)
            delta = jnp.sum(probs * grad_probs, axis=-1, keepdims=True)
            grad_scores = (probs * (grad_probs - delta)).astype(BF16)
            field[rows, columns] = join_heads(dot(grad_scores, keys)) * 0.125
            grad_keys = tdot(grad_scores, query_two)
            grad_vals = tdot(probs.astype(BF16), grad_two)
            store[near, columns] += grad_keys[:span]
            store[far, columns] += grad_keys[span:]
            store[near, values] += grad_vals[:span]
            store[far, values] += grad_vals[span:]
        return carry

    lax.fori_loop(0, picks.shape[0], block, 0)
    for pair in range(pairs):
        columns = slice(pair * LANES, (pair + 1) * LANES)
        low = pltpu.roll(field[:, columns], STRETCH - 1, 0).astype(BF16)
        query_low[:, columns] = low
        query_out[:, columns] = low.astype(F32)
        q_bias_out[:, columns] = jnp.sum(low.astype(F32), axis=0, keepdims=True)

    v_bias_out[...] = jnp.zeros_like(v_bias_out)

    def flush(index, carry):
        rows = pl.ds(pl.multiple_of(index * span, span), span)
        low = store[rows, :].astype(BF16)
        store_out[rows, :] = low
        v_bias_out[...] += jnp.sum(low[:, local:].astype(F32), axis=0, keepdims=True)
        return carry

    lax.fori_loop(0, store.shape[0] // span, flush, 0)


def self_backward(
    info, query_own, query_peer, q_w, q_near, q_far, hidden, grad_two, gain_two, out_w, qkv, lse, mask, cosine, sine, w,
    tok, gain_one,
    low_out, qkv_out, keep_out, send_out, sums_out, q_bias_out, q_peer, one, mix_grad, key_grad, value_grad, part,
):
    count = tok.shape[0]
    local = out_w.shape[0]
    pairs = local // LANES
    step = 256
    join_peer(q_peer, q_near, q_far, info[2])
    sums_out[...] = jnp.zeros_like(sums_out)
    half = keep_out.shape[1]
    own = pl.ds(pl.multiple_of(info[1] * half, LANES), half)
    peer = pl.ds(pl.multiple_of((1 - info[1]) * half, LANES), half)

    def project(index, carry):
        rows = pl.ds(pl.multiple_of(index * step, step), step)
        gradient = dot_t(query_own[rows, :], q_w[...]) + dot_t(
            query_peer[rows, :].astype(BF16), q_peer[...]
        )
        xhat, scale = norm_stats(hidden[rows, :])
        sums_out[0:1, :] += jnp.sum(gradient * xhat, axis=0, keepdims=True)
        sums_out[1:2, :] += jnp.sum(gradient, axis=0, keepdims=True)
        grad_one = grad_two[rows, :] + norm_back(xhat, scale, gain_two[...], gradient)
        one[rows, :] = grad_one
        low = grad_one.astype(BF16)
        low_out[rows, :] = low
        sums_out[2:3, :] += jnp.sum(low.astype(F32), axis=0, keepdims=True)
        mixed = dot_t(low, out_w[...])
        for pair in range(pairs):
            mix_grad[pair, rows, :] = mixed[:, pair * LANES : (pair + 1) * LANES].astype(BF16)
        return carry

    lax.fori_loop(0, count // step, project, 0)

    def attend(pair, carry):
        key_grad[...] = jnp.zeros_like(key_grad)
        value_grad[...] = jnp.zeros_like(value_grad)
        for start in range(0, count, TILE):
            rows = slice(start, start + TILE)
            until = slice(0, start + TILE)
            query = two_heads(qkv[pair, rows, :] * BF16(0.125))
            keys = qkv[pairs + pair, until, :]
            vals = qkv[2 * pairs + pair, until, :]
            grad_mix = two_heads(mix_grad[pair, rows, :])
            allowed = mask[rows, until]
            scores = dot_t(query, keys) + jnp.concatenate([allowed, allowed], axis=0)
            probs = jnp.exp(scores - two_columns(lse[rows, :], 2 * pair))
            grad_probs = dot_t(grad_mix, vals)
            delta = jnp.sum(probs * grad_probs, axis=-1, keepdims=True)
            grad_scores = (probs * (grad_probs - delta)).astype(BF16)
            grad_query = join_heads(dot(grad_scores, keys)) * 0.125
            back = turn(grad_query, cosine[rows, :], sine[rows, :], -1.0)
            qkv_out[pair, rows, :] = back.astype(BF16)
            key_grad[until, :] += tdot(grad_scores, query)
            value_grad[until, :] += tdot(probs.astype(BF16), grad_mix)
        for start in range(0, count, TILE):
            rows = slice(start, start + TILE)
            back = turn(key_grad[rows, :], cosine[rows, :], sine[rows, :], -1.0)
            qkv_out[pairs + pair, rows, :] = back.astype(BF16)
            qkv_out[2 * pairs + pair, rows, :] = value_grad[rows, :].astype(BF16)
        return carry

    lax.fori_loop(0, pairs, attend, 0)

    for piece in range(3 * pairs):
        q_bias_out[:, piece * LANES : (piece + 1) * LANES] = jnp.sum(
            qkv_out[piece].astype(F32), axis=0, keepdims=True
        )

    def finish(index, carry):
        rows = pl.ds(pl.multiple_of(index * step, step), step)
        gradient = jnp.zeros((step, tok.shape[1]), F32)
        for part_at in range(3):
            joined = jnp.concatenate(
                [qkv_out[part_at * pairs + pair, rows, :] for pair in range(pairs)], axis=1
            )
            gradient = gradient + dot_t(joined, w[part_at])
        xhat, scale = norm_stats(tok[rows, :].astype(F32))
        sums_out[3:4, :] += jnp.sum(gradient * xhat, axis=0, keepdims=True)
        sums_out[4:5, :] += jnp.sum(gradient, axis=0, keepdims=True)
        part[...] = norm_back(xhat, scale, gain_one[...], gradient)
        keep_out[rows, :] = part[:, own] + one[rows, own]
        send_out[rows, :] = part[:, peer]
        return carry

    lax.fori_loop(0, count // step, finish, 0)


def whole(count):
    return [pl.BlockSpec(memory_space=pltpu.VMEM)] * count


def scalars(count):
    return [pl.BlockSpec(memory_space=pltpu.SMEM)] * count


def shape(dims, kind=F32):
    return jax.ShapeDtypeStruct(dims, kind)


def call(body, name, small, big, outs, scratch=()):
    return pl.pallas_call(
        body,
        name=name,
        out_shape=outs,
        in_specs=scalars(len(small)) + whole(len(big)),
        out_specs=whole(len(outs)),
        scratch_shapes=scratch,
    )(*small, *big)


def per_device(
    tokens,
    neighbours,
    out_grad,
    group_sizes,
    seq_lengths,
    stretch_neighbours,
    norm_gain,
    norm_bias,
    self_qkv_w,
    self_qkv_b,
    self_out_w,
    self_out_b,
    cross_q_w,
    cross_q_b,
    cross_kv_w,
    cross_v_b,
    cross_out_w,
    cross_out_b,
    mlp_in_w,
    mlp_in_b,
    mlp_out_w,
    mlp_out_b,
):
    count, width = tokens.shape
    local = self_qkv_w.shape[2]
    hidden = mlp_in_w.shape[1]
    pairs = local // LANES
    stored, span = neighbours.shape[:2]
    slots = seq_lengths.shape[1]
    dp_size = lax.axis_size("dp")
    tp_at = lax.axis_index("tp")
    dp_at = lax.axis_index("dp")
    core = dp_at % 2

    def swap(value):
        return lax.ppermute(value, "tp", [(0, 1), (1, 0)])

    def across(value, bit):
        return lax.ppermute(value, "dp", [(at, at ^ bit) for at in range(dp_size)])

    def fetch(weight):
        half = weight.shape[0] // 2
        mine = lax.dynamic_slice_in_dim(weight, core * half, half, 0).astype(F32)
        near = swap(mine)
        return near, across(near, 1)

    def row(value):
        return value.reshape(1, -1)

    padded = count // group_sizes[0]
    info = jnp.concatenate(
        [jnp.stack([padded, tp_at.astype(jnp.int32), core.astype(jnp.int32)]), seq_lengths[0]]
    )
    position = (jnp.arange(count, dtype=jnp.int32) % padded).astype(F32)
    halfway = HEAD_DIM // 2
    frequency = jnp.exp(-math.log(10000.0) * jnp.arange(halfway, dtype=F32) / halfway)
    angles = position[:, None] * jnp.tile(frequency, LANES // halfway)[None, :]
    cosine = jnp.cos(angles)
    sine = jnp.sin(angles)

    so_near, so_far = fetch(self_out_w)
    co_near, co_far = fetch(cross_out_w)
    cq_near, cq_far = fetch(cross_q_w)

    qkv_w = jnp.swapaxes(self_qkv_w, 0, 1)
    ln_one, qkv, self_mix, self_lse, mask = call(
        partial(self_forward, slots),
        "self_forward",
        (info,),
        (tokens, qkv_w, self_qkv_b, norm_gain[0:1], norm_bias[0:1], cosine, sine),
        (
            shape((count, width), BF16),
            shape((3 * pairs, count, LANES), BF16),
            shape((count, local)),
            shape((count, LANES)),
            shape((count, count)),
        ),
    )
    self_mix_peer = swap(self_mix)

    kv_w = jnp.swapaxes(cross_kv_w, 0, 1).reshape(2, width, local)
    flat_store = neighbours.reshape(stored * span, width)
    kv_bias = jnp.concatenate([jnp.zeros_like(cross_v_b), cross_v_b])
    joined_kv = jnp.concatenate([kv_w[0], kv_w[1]], axis=1)
    store_kv = (dot(flat_store, joined_kv) + kv_bias).astype(BF16)

    hidden_one, ln_two, cross_query, cross_mix, cross_lse = call(
        partial(cross_forward, slots, span),
        "cross_forward",
        (info, stretch_neighbours),
        (
            tokens,
            self_mix,
            self_mix_peer,
            self_out_w,
            so_near,
            so_far,
            row(self_out_b),
            norm_gain[1:2],
            norm_bias[1:2],
            cross_q_w,
            row(cross_q_b),
            store_kv,
        ),
        (
            shape((count, width)),
            shape((count, width), BF16),
            shape((count, local), BF16),
            shape((count, local)),
            shape((count, LANES)),
        ),
        [pltpu.VMEM((local, width), BF16), pltpu.VMEM((count, local), F32)],
    )
    cross_mix_peer = swap(cross_mix)

    step = 256
    rows = lambda wide: pl.BlockSpec((step, wide), lambda i: (i, 0))
    kept = pl.BlockSpec(memory_space=pltpu.VMEM)
    own_width = width // 2
    hidden_two, ln_three, act, grad_pre, out_keep, out_send, part_three, mlp_in_b_grad = pl.pallas_call(
        feed_forward,
        name="feed_forward",
        grid=(count // step,),
        in_specs=[pl.BlockSpec(memory_space=pltpu.SMEM), rows(width), rows(local), rows(local)]
        + [kept] * 10
        + [rows(width)],
        out_specs=[
            rows(width),
            rows(width),
            rows(hidden),
            rows(hidden),
            rows(own_width),
            rows(own_width),
            rows(width),
            pl.BlockSpec((1, hidden), lambda i: (0, 0)),
        ],
        out_shape=[
            shape((count, width)),
            shape((count, width), BF16),
            shape((count, hidden), BF16),
            shape((count, hidden), BF16),
            shape((count, own_width)),
            shape((count, own_width)),
            shape((count, width)),
            shape((1, hidden)),
        ],
        scratch_shapes=[pltpu.VMEM((local, width), BF16)],
    )(
        info,
        hidden_one,
        cross_mix,
        cross_mix_peer,
        cross_out_w,
        co_near,
        co_far,
        row(cross_out_b),
        norm_gain[2:3],
        norm_bias[2:3],
        mlp_in_w,
        row(mlp_in_b),
        mlp_out_w,
        row(mlp_out_b),
        out_grad,
    )
    part_three_peer = swap(part_three)
    out_back = swap(out_send)
    output = (out_keep + out_back).astype(BF16)

    mlp_out_w_grad = tdot(out_grad, act)
    mlp_in_w_grad = tdot(ln_three, grad_pre)
    mlp_out_b_grad = jnp.sum(out_grad.astype(F32), axis=0, keepdims=True)

    (
        grad_two,
        grad_cross,
        grad_query,
        grad_query_low,
        grad_store,
        gain_three,
        shift_three,
        cross_out_b_grad,
        cross_q_b_grad,
        cross_v_b_grad,
    ) = call(
        partial(cross_backward, slots, span),
        "cross_backward",
        (info, stretch_neighbours),
        (
            part_three,
            part_three_peer,
            hidden_two,
            out_grad,
            norm_gain[2:3],
            cross_out_w,
            cross_query,
            store_kv,
            cross_lse,
        ),
        (
            shape((count, width)),
            shape((count, width), BF16),
            shape((count, local)),
            shape((count, local), BF16),
            shape((stored * span, 2 * local), BF16),
            shape((1, width)),
            shape((1, width)),
            shape((1, width)),
            shape((1, local)),
            shape((1, local)),
        ),
        [
            pltpu.VMEM((count, local), BF16),
            pltpu.VMEM((count, local), F32),
            pltpu.VMEM((stored * span, 2 * local), F32),
        ],
    )
    grad_query_peer = swap(grad_query)

    own_kv = lax.dynamic_slice_in_dim(joined_kv, tp_at * own_width, own_width, 0)
    peer_kv = lax.dynamic_slice_in_dim(joined_kv, (1 - tp_at) * own_width, own_width, 0)
    store_back = swap(dot_t(grad_store, peer_kv))
    neighbours_grad = (dot_t(grad_store, own_kv) + store_back).astype(BF16)
    cross_out_w_grad = tdot(grad_cross, cross_mix.astype(BF16))
    cross_q_w_grad = tdot(ln_two, grad_query_low)
    cross_kv_w_grad = tdot(flat_store, grad_store)

    grad_attn, grad_qkv, tok_keep, tok_send, sums, self_qkv_b_grad = call(
        self_backward,
        "self_backward",
        (info,),
        (
            grad_query_low,
            grad_query_peer,
            cross_q_w,
            cq_near,
            cq_far,
            hidden_one,
            grad_two,
            norm_gain[1:2],
            self_out_w,
            qkv,
            self_lse,
            mask,
            cosine,
            sine,
            qkv_w,
            tokens,
            norm_gain[0:1],
        ),
        (
            shape((count, width), BF16),
            shape((3 * pairs, count, LANES), BF16),
            shape((count, own_width)),
            shape((count, own_width)),
            shape((8, width)),
            shape((1, 3 * local)),
        ),
        [
            pltpu.VMEM((width, local), BF16),
            pltpu.VMEM((count, width), F32),
            pltpu.VMEM((pairs, count, LANES), BF16),
            pltpu.VMEM((count, LANES), F32),
            pltpu.VMEM((count, LANES), F32),
            pltpu.VMEM((256, width), F32),
        ],
    )
    tokens_grad = (tok_keep + swap(tok_send)).astype(BF16)
    self_out_w_grad = tdot(grad_attn, self_mix.astype(BF16))
    self_qkv_w_grad = jnp.concatenate([tdot(ln_one, grad_qkv[piece]) for piece in range(3 * pairs)], axis=1)

    def scatter(value):
        value = value.reshape(dp_size, width // dp_size, value.shape[1])
        bit = 1
        while bit < dp_size:
            value = value.reshape(-1, 2, *value.shape[1:])
            mine = (dp_at // bit) % 2
            sent = lax.dynamic_index_in_dim(value, 1 - mine, 1, keepdims=False)
            held = lax.dynamic_index_in_dim(value, mine, 1, keepdims=False)
            value = held + across(sent, bit)
            bit *= 2
        return value[0]

    mlp_out_w_grad = scatter(mlp_out_w_grad)
    mlp_in_w_grad = scatter(mlp_in_w_grad)
    cross_out_w_grad = scatter(cross_out_w_grad)
    cross_q_w_grad = scatter(cross_q_w_grad)
    cross_kv_w_grad = scatter(cross_kv_w_grad)
    self_out_w_grad = scatter(self_out_w_grad)
    self_qkv_w_grad = scatter(self_qkv_w_grad)

    def total(value):
        bit = 1
        while bit < dp_size:
            value = value + across(value, bit)
            bit *= 2
        return value

    shared = jnp.concatenate(
        [sums[3:5], 0.5 * sums[0:3], 0.5 * gain_three, 0.5 * shift_three, 0.5 * cross_out_b_grad, 0.5 * mlp_out_b_grad],
        axis=0,
    )
    shared = shared + swap(shared)
    alone = jnp.concatenate(
        [self_qkv_b_grad, cross_q_b_grad, cross_v_b_grad, mlp_in_b_grad], axis=1
    )
    alone_size = alone.shape[1]
    alone_rows = -(-alone_size // width)
    alone = jnp.pad(alone, ((0, 0), (0, alone_rows * width - alone_size))).reshape(alone_rows, width)
    summed = total(jnp.concatenate([shared, alone], axis=0))
    alone = summed[9:].reshape(-1)
    norm_gain_grad = jnp.stack([summed[0], summed[2], summed[5]])
    norm_bias_grad = jnp.stack([summed[1], summed[3], summed[6]])
    return (
        output,
        tokens_grad,
        neighbours_grad.reshape(stored, span, own_width),
        norm_gain_grad,
        norm_bias_grad,
        self_qkv_w_grad.reshape(-1, 3, local),
        alone[: 3 * local].reshape(3, local),
        self_out_w_grad.T,
        summed[4],
        cross_q_w_grad,
        alone[3 * local : 4 * local],
        cross_kv_w_grad.reshape(-1, 2, local),
        alone[4 * local : 5 * local],
        cross_out_w_grad.T,
        summed[7],
        mlp_in_w_grad,
        alone[5 * local : 5 * local + hidden],
        mlp_out_w_grad.T,
        summed[8],
    )


def solution(mesh):
    placed = (
        P("dp", None),
        P("dp", None, None),
        P("dp", None),
        P("dp"),
        P("dp", None),
        P("dp", None),
        P(),
        P(),
        P(None, None, "tp"),
        P(None, "tp"),
        P("tp", None),
        P(),
        P(None, "tp"),
        P("tp"),
        P(None, None, "tp"),
        P("tp"),
        P("tp", None),
        P(),
        P(None, "tp"),
        P("tp"),
        P("tp", None),
        P(),
    )
    return jax.shard_map(
        per_device,
        mesh=mesh,
        in_specs=placed,
        out_specs=(
            P("dp", "tp"),
            P("dp", "tp"),
            P("dp", None, "tp"),
            P(),
            P(),
            P("dp", None, "tp"),
            P(None, "tp"),
            P("tp", "dp"),
            P(),
            P("dp", "tp"),
            P("tp"),
            P("dp", None, "tp"),
            P("tp"),
            P("tp", "dp"),
            P(),
            P("dp", "tp"),
            P("tp"),
            P("tp", "dp"),
            P(),
        ),
        check_vma=False,
    )
```

time: 995 us -> 443 us (0.45)
  waiting for transfers between devices: 580 us -> 216 us
  matrix products: 152 us -> 36.7 us
  local copies, waits for them, and re-layouts: 117 us -> 37 us
  Pallas kernels: 0 us -> 73.3 us
  blocking collectives: 61.8 us -> 0 us
  starting transfers between devices: 1.54 us -> 49.6 us
  other arithmetic: 57.1 us -> 26.9 us
  between operations: 16.9 us -> 2.28 us
    reduce_scatter x7 -> x0, waiting for transfers between devices: 390 us -> none  [the longest x1 79.1 us: per_device(): lax.psum_scatter(mlp_out_w_grad, 'dp', scatter_dimension=1, tiled=True)]
    ppermute x0 -> x46, waiting for transfers between devices: none -> 216 us  [the longest x35 129 us: across(): return lax.ppermute(value, 'dp', [(at, at ^ bit) for at in range(dp_size)])]
    psum x5 -> x0, waiting for transfers between devices: 190 us -> none  [the longest x1 72.7 us: per_device(): lax.psum(jnp.dot(act_low, mlp_out_w, preferred_element_type=jnp.float32),...]
    dot_general x70 -> x18, matrix products: 152 us -> 36.7 us  [the longest x15 28.7 us: tdot(): lax.dot_general(left, right, (((0,), (0,)), ((), ())), preferred_element_...]
    pallas_call x0 -> x5, Pallas kernels: none -> 73.3 us  [the longest x4 59.6 us: call(): pl.pallas_call(body, name=name, out_shape=outs, in_specs=scalars(len(smal...]
    psum x1 -> x0, blocking collectives: 61.8 us -> none  [per_device(): lax.psum((gain_grads, shift_grads, self_qkv_b_grad, self_out_b_grad, cros...]
    ppermute x0 -> x46, starting transfers between devices: none -> 49.6 us  [the longest x35 36.4 us: across(): return lax.ppermute(value, 'dp', [(at, at ^ bit) for at in range(dp_size)])]
    reduce_sum x25 -> x1, other arithmetic: 28.7 us -> 0.15 us  [per_device(): mlp_out_b_grad = jnp.sum(out_grad.astype(F32), axis=0, keepdims=True)]
  transfers between devices with their start and end apart: 13 -> 46, of which waited for: 10 -> 23; matrix products, arithmetic and copies ran while one was open for 21% -> 20% of each run, Pallas kernels for 0% -> 17%
where the time goes in v1:
time: 443 us; the launch traced here: 442 us
  waiting for transfers between devices  216 us (49%)
  Pallas kernels  73.3 us (17%)
  starting transfers between devices  49.6 us (11%)
  local copies, waits for them, and re-layouts  37 us (8%)
  matrix products  36.7 us (8%)
  other arithmetic  26.9 us (6%)
    ppermute x35, waiting for transfers between devices, across(): return lax.ppermute(value, 'dp', [(at, at ^ bit) for at in range(dp_size)])  129 us
    ppermute x11, waiting for transfers between devices, swap(): return lax.ppermute(value, 'tp', [(0, 1), (1, 0)])  86.6 us
    pallas_call x4, Pallas kernels, call(): pl.pallas_call(body, name=name, out_shape=outs, in_specs=scalars(len(smal...  59.6 us
    ppermute x35, starting transfers between devices, across(): return lax.ppermute(value, 'dp', [(at, at ^ bit) for at in range(dp_size)])  36.4 us
    dot_general x15, matrix products, tdot(): lax.dot_general(left, right, (((0,), (0,)), ((), ())), preferred_element_...  28.7 us
    pallas_call x1, Pallas kernels, per_device(): pl.pallas_call(feed_forward, name='feed_forward', grid=(count // step,),...  13.6 us
    ppermute x11, starting transfers between devices, swap(): return lax.ppermute(value, 'tp', [(0, 1), (1, 0)])  13.2 us
    add x23, other arithmetic, scatter(): value = held + across(sent, bit)  13.2 us
  transfers between devices with their start and end apart: 46, of which 23 were waited for; matrix products, arithmetic and copies ran while one was open for 20% of the time, Pallas kernels for 17%

profile of v1, /device:TPU:0, one launch (start us, length us, event | category | flops | bytes accessed | tf_op | source)
XLA Modules:
  0.0 441.6 jit_solution(4722484906061367764)
XLA Ops:
  0.7 1.9 dynamic-slice_convert_fusion.2
  2.6 3.0 collective-permute-start.1
  10.6 1.8 multiply_sine_fusion
  12.4 10.6 %self_forward.1 = (bf16[512,768]{1,0:T(8,128)(2,1)}, bf16[9,512,128]{2,1,0:T(8,128)(2,1)}, f32[512,384]{1,0:T(8,128)}, f32[512,128]{1,0:T(8,128)}, f32[512,512]{1,0:T(8,128)}) custom-call(s32[7]{0:T(128)} %pad_add_fusion.info, bf16[512,768]{1,0:T(8,128)(2,1)} %tok.5, bf16[3,768,384]{2,1,0:T(8,128)(2,1)} %bitcast.206, f32[3,384]{1,0:T(4,128)} %bias.1, ...), custom_call_target="tpu_custom_call" | custom-call | tf_op jit(solution)/shard_map/self_forward/pallas_call | solution.py:436
  23.9 2.0 collective-permute-start.4
  28.7 2.5 fusion.kv
  31.2 12.5 %collective-permute-done.mix_peer = f32[512,384]{1,0:T(8,128)} collective-permute-done((f32[512,384]{1,0:T(8,128)}, f32[512,384]{1,0:T(8,128)}, u32[]{:S(2)}, u32[]{:S(2)}) %collective-permute-start) | collective-permute-done | bytes 786464 | tf_op jit(solution)/shard_map/ppermute | solution.py:482
  44.6 13.8 %cross_forward.1 = (f32[512,768]{1,0:T(8,128)}, bf16[512,768]{1,0:T(8,128)(2,1)}, bf16[512,384]{1,0:T(8,128)(2,1)}, f32[512,384]{1,0:T(8,128)}, f32[512,128]{1,0:T(8,128)}) custom-call(s32[7]{0:T(128)} %pad_add_fusion.info, s32[8,2]{1,0:T(8,128)} %copy.59.picks, bf16[512,768]{1,0:T(8,128)(2,1)} %tok.5, f32[512,384]{1,0:T(8,128)} %get-tuple-element.53.mix_own, ...), custom_call_target="tpu_custom_call" | custom-call | tf_op jit(solution)/shard_map/cross_forward/pallas_call | solution.py:436
  58.5 2.0 collective-permute-start.9
  62.6 25.5 %collective-permute-done.9.q_near = f32[384,384]{1,0:T(8,128)} collective-permute-done((f32[384,384]{1,0:T(8,128)S(1)}, f32[384,384]{1,0:T(8,128)}, u32[]{:S(2)}, u32[]{:S(2)}) %collective-permute-start.9) | collective-permute-done | bytes 589856 | tf_op jit(solution)/shard_map/ppermute | solution.py:482
  89.0 13.6 %feed_forward.1 = (f32[512,768]{1,0:T(8,128)}, bf16[512,768]{1,0:T(8,128)(2,1)}, bf16[512,1536]{1,0:T(8,128)(2,1)}, bf16[512,1536]{1,0:T(8,128)(2,1)}, f32[512,3...) custom-call(s32[7]{0:T(128)} %pad_add_fusion.info, ...), custom_call_target="tpu_custom_call" | custom-call | tf_op jit(solution)/shard_map/feed_forward/pallas_call | solution.py:566
  103.2 1.5 collective-permute-start.7
  104.7 3.1 fusion.44
  107.8 1.7 dynamic-slice_bitcast_fusion.1
  112.6 1.7 dynamic-slice_bitcast_fusion
  115.5 7.8 %collective-permute-done.6 = f32[512,384]{1,0:T(8,128)S(1)} collective-permute-done((f32[512,384]{1,0:T(8,128)}, f32[512,384]{1,0:T(8,128)S(1)}, u32[]{:S(2)}, u32[]{:S(2)}) %collective-permute-start.6) | collective-permute-done | bytes 786464 | tf_op jit(solution)/shard_map/ppermute | solution.py:482
  124.1 32.4 %collective-permute-done.7.part_peer = f32[512,768]{1,0:T(8,128)S(1)} collective-permute-done((f32[512,768]{1,0:T(8,128)}, f32[512,768]{1,0:T(8,128)S(1)}, u32[]{:S(2)}, u32[]{:S(2)}) %collective-permute-start.7) | collective-permute-done | bytes 1572896 | tf_op jit(solution)/shard_map/ppermute | solution.py:482
  157.7 17.4 %cross_backward.1 = (f32[512,768]{1,0:T(8,128)}, bf16[512,768]{1,0:T(8,128)(2,1)}, f32[512,384]{1,0:T(8,128)}, bf16[512,384]{1,0:T(8,128)(2,1)}, bf16[1024,768]{...) custom-call(s32[7]{0:T(128)} %pad_add_fusion.info, ...), custom_call_target="tpu_custom_call" | custom-call | tf_op jit(solution)/shard_map/cross_backward/pallas_call | solution.py:436
  175.7 3.0 fusion.43
  178.8 2.1 fusion.4
  185.0 1.5 collective-permute-start.12
  187.5 8.3 %collective-permute-done.8.query_peer = f32[512,384]{1,0:T(8,128)S(1)} collective-permute-done((f32[512,384]{1,0:T(8,128)}, f32[512,384]{1,0:T(8,128)S(1)}, u32[]{:S(2)}, u32[]{:S(2)}) %collective-permute-start.8) | collective-permute-done | bytes 786464 | tf_op jit(solution)/shard_map/ppermute | solution.py:482
  195.8 1.5 collective-permute-start.27
  197.3 17.8 %self_backward.1 = (bf16[512,768]{1,0:T(8,128)(2,1)}, bf16[9,512,128]{2,1,0:T(8,128)(2,1)}, f32[512,384]{1,0:T(8,128)}, f32[512,384]{1,0:T(8,128)}, f32[8,768]{1,0:T(8,128)}, /*index=5*/f32[1,1152]{1,0:T(1,128)}) custom-call(s32[7]{0:T(128)} %pad_add_fusion.info, bf16[512,384]{1,0:T(8,128)(2,1)} %get-tuple-element.62.query_own, f32[512,384]{1,0:T(8,128)} %copy-done.33, ...), custom_call_target="tpu_custom_call" | custom-call | tf_op jit(solution)/shard_map/self_backward/pallas_call | solution.py:436
  215.1 2.0 convolution_dynamic-update-slice_fusion.8
  217.1 2.0 convolution_dynamic-update-slice_fusion.7
  219.1 2.0 convolution_dynamic-update-slice_fusion.6
  221.0 2.0 convolution_dynamic-update-slice_fusion.5
  223.1 2.0 convolution_dynamic-update-slice_fusion.4
  225.1 2.0 convolution_dynamic-update-slice_fusion.3
  227.1 2.0 convolution_dynamic-update-slice_fusion.2
  229.1 2.0 convolution_dynamic-update-slice_fusion.1
  231.1 2.0 convolution_dynamic-update-slice_fusion
  233.1 5.2 %copy.61 = f32[768,1152]{1,0:T(8,128)} copy(f32[768,1152]{0,1:T(8,128)} %convolution_dynamic-update-slice_fusion) | data formatting | bytes 7077888 | tf_op jit(solution)/shard_map/concatenate | solution.py:715
  238.3 2.1 fusion.8
  243.5 2.8 bitcast_add_fusion.1
  246.8 2.3 bitcast_add_fusion
  254.6 2.9 collective-permute-done.15
  257.5 1.6 collective-permute-start.16
  259.9 1.8 collective-permute-done.16
  261.7 2.7 collective-permute-start.17
  265.0 1.7 collective-permute-done.17
  266.7 1.6 collective-permute-start.28
  272.2 1.8 collective-permute-start.36
  275.0 2.6 collective-permute-done.36
  277.6 3.6 collective-permute-start.29
  281.2 3.9 collective-permute-done.29
  287.0 4.1 collective-permute-done.37
  293.0 1.8 bitcast_add_fusion.5
  297.1 3.3 add_convert_fusion.1
  301.3 2.0 add_convert_fusion.2
  303.3 49.0 %collective-permute-done.23 = f32[4,48,384]{2,1,0:T(8,128)S(1)} collective-permute-done((f32[4,48,384]{2,1,0:T(8,128)S(1)}, f32[4,48,384]{2,1,0:T(8,128)S(1)}, u32[]{:S(2)}, u32[]{:S(2)}) %collective-permute-start.23) | collective-permute-done | bytes 294944 | tf_op jit(solution)/shard_map/ppermute | solution.py:485
  352.8 11.6 %collective-permute-done.31 = f32[4,48,768]{2,1,0:T(8,128)S(1)} collective-permute-done((f32[4,48,768]{2,1,0:T(8,128)S(1)}, f32[4,48,768]{2,1,0:T(8,128)S(1)}, u32[]{:S(2)}, u32[]{:S(2)}) %collective-permute-start.31) | collective-permute-done | bytes 589856 | tf_op jit(solution)/shard_map/ppermute | solution.py:485
  365.2 2.8 collective-permute-start.32
  368.0 3.0 collective-permute-done.25
  373.4 3.4 collective-permute-done.32
  378.5 1.8 collective-permute-start.44
  380.3 10.8 %collective-permute-done.33 = f32[1,48,768]{2,1,0:T(8,128)S(1)} collective-permute-done((f32[1,48,768]{2,1,0:T(8,128)S(1)}, f32[1,48,768]{2,1,0:T(8,128)S(1)}, u32[]{:S(2)}, u32[]{:S(2)}) %collective-permute-start.33) | collective-permute-done | bytes 147488 | tf_op jit(solution)/shard_map/ppermute | solution.py:485
  391.9 2.2 bitcast_add_fusion.2
  396.6 3.4 collective-permute-start.41
  400.0 10.6 %collective-permute-done.44 = f32[2,48,1536]{2,1,0:T(8,128)} collective-permute-done((f32[2,48,1536]{2,1,0:T(8,128)}, f32[2,48,1536]{2,1,0:T(8,128)}, u32[]{:S(2)}, u32[]{:S(2)}) %collective-permute-start.44) | collective-permute-done | bytes 589856 | tf_op jit(solution)/shard_map/ppermute | solution.py:485
  412.9 3.6 collective-permute-start.20
  417.3 13.3 %collective-permute-done.20 = f32[2,48,1152]{2,1,0:T(8,128)S(1)} collective-permute-done((f32[2,48,1152]{2,1,0:T(8,128)S(1)}, f32[2,48,1152]{2,1,0:T(8,128)S(1)}, u32[]{:S(2)}, u32[]{:S(2)}) %collective-permute-start.20) | collective-permute-done | bytes 442400 | tf_op jit(solution)/shard_map/ppermute | solution.py:485
  431.6 9.2 %collective-permute-done.21 = f32[1,48,1152]{2,1,0:T(8,128)S(1)} collective-permute-done((f32[1,48,1152]{2,1,0:T(8,128)S(1)}, f32[1,48,1152]{2,1,0:T(8,128)S(1)}, u32[]{:S(2)}, u32[]{:S(2)}) %collective-permute-start.21) | collective-permute-done | bytes 221216 | tf_op jit(solution)/shard_map/ppermute | solution.py:485
  (273 shorter events, 59.8 us)
Async XLA Ops:
  0.7 28.0 %copy-start = (bf16[8,128,768]{2,1,0:T(8,128)(2,1)S(1)}, bf16[8,128,768]{2,1,0:T(8,128)(2,1)}, u32[]{:S(2)}) copy-start(bf16[8,128,768]{2,1,0:T(8,128)(2,1)} %param.23) | copy-start | bytes 4718596
  2.6 23.5 %collective-permute-start.1 = (f32[192,768]{1,0:T(8,128)}, f32[192,768]{1,0:T(8,128)}, u32[]{:S(2)}, u32[]{:S(2)}) collective-permute-start(f32[192,768]{1,0:T(8,128)} %dynamic-slice_convert_fusion.2), channel_id=1, source_target_pairs={{0,1},{1,0},{2,3},{3,2},{4,5},{5,4},{6,7},{7,6},{8,9},{9,8},{10,11... | collective-permute-start | bytes 1769480 | tf_op jit(solution)/shard_map/ppermute | solution.py:482
  12.4 10.6 %copy-start.13 = (bf16[384,768]{1,0:T(8,128)(2,1)S(1)}, bf16[384,768]{1,0:T(8,128)(2,1)}, u32[]{:S(2)}) copy-start(bf16[384,768]{1,0:T(8,128)(2,1)} %out_w.4) | copy-start | bytes 1769476
  12.4 13.5 %copy-start.32 = (bf16[768,2,384]{2,1,0:T(2,128)(2,1)S(1)}, bf16[768,2,384]{2,1,0:T(2,128)(2,1)}, u32[]{:S(2)}) copy-start(bf16[768,2,384]{2,1,0:T(2,128)(2,1)} %param.36) | copy-start | bytes 3538948
  23.0 20.7 %collective-permute-start = (f32[512,384]{1,0:T(8,128)}, f32[512,384]{1,0:T(8,128)}, u32[]{:S(2)}, u32[]{:S(2)}) collective-permute-start(f32[512,384]{1,0:T(8,128)} %get-tuple-element.53.mix_own), channel_id=1, source_target_pairs={{0,1},{1,0},{2,3},{3,2},{4,5},{5,4},{6,7},{7,6},{8,9},{9,8},{10,11... | collective-permute-start | bytes 2359304 | tf_op jit(solution)/shard_map/ppermute | solution.py:482
  23.9 36.7 %collective-permute-start.4 = (f32[192,768]{1,0:T(8,128)}, f32[192,768]{1,0:T(8,128)}, u32[]{:S(2)}, u32[]{:S(2)}) collective-permute-start(f32[192,768]{1,0:T(8,128)} %dynamic-slice_convert_fusion.1), channel_id=1, source_target_pairs={{0,1},{1,0},{2,3},{3,2},{4,5},{5,4},{6,7},{7,6},{8,9},{9,8},{10,11... | collective-permute-start | bytes 1769480 | tf_op jit(solution)/shard_map/ppermute | solution.py:482
  26.1 17.6 %collective-permute-start.2 = (f32[192,768]{1,0:T(8,128)}, f32[192,768]{1,0:T(8,128)S(1)}, u32[]{:S(2)}, u32[]{:S(2)}) collective-permute-start(f32[192,768]{1,0:T(8,128)} %collective-permute-done.1.w_near), channel_id=1, source_target_pairs={{0,2},{2,0},{4,6},{6,4},{8,10},{10,8},{12,14},{14,12},{16,18},{18,... | collective-permute-start | bytes 1769480 | tf_op jit(solution)/shard_map/ppermute | solution.py:485
  26.7 4.5 %copy-start.19 = (bf16[768,384]{1,0:T(8,128)(2,1)}, bf16[768,384]{1,0:T(8,128)(2,1)S(1)}, u32[]{:S(2)}) copy-start(bf16[768,384]{1,0:T(8,128)(2,1)S(1)} %get-tuple-element.148) | copy-start | bytes 1769476
  44.6 13.9 %copy-start.14 = (bf16[768,384]{1,0:T(8,128)(2,1)S(1)}, bf16[768,384]{1,0:T(8,128)(2,1)}, u32[]{:S(2)}) copy-start(bf16[768,384]{1,0:T(8,128)(2,1)} %q_w.3) | copy-start | bytes 1769476
  44.6 16.0 %copy-start.45 = (f32[768]{0:T(1024)S(1)}, f32[768]{0:T(1024)}, u32[]{:S(2)}) copy-start(f32[768]{0:T(1024)} %param.39) | copy-start | bytes 9220
  44.6 16.6 %copy-start.41 = (f32[1536]{0:T(1024)S(1)}, f32[1536]{0:T(1024)}, u32[]{:S(2)}) copy-start(f32[1536]{0:T(1024)} %param.41) | copy-start | bytes 18436
  44.6 17.2 %copy-start.46 = (f32[768]{0:T(1024)S(1)}, f32[768]{0:T(1024)}, u32[]{:S(2)}) copy-start(f32[768]{0:T(1024)} %param.43) | copy-start | bytes 9220
  58.4 29.8 %collective-permute-start.3 = (f32[512,384]{1,0:T(8,128)}, f32[512,384]{1,0:T(8,128)}, u32[]{:S(2)}, u32[]{:S(2)}) collective-permute-start(f32[512,384]{1,0:T(8,128)} %get-tuple-element.55.mix_own), channel_id=1, source_target_pairs={{0,1},{1,0},{2,3},{3,2},{4,5},{5,4},{6,7},{7,6},{8,9},{9,8},{10,11... | collective-permute-start | bytes 2359304 | tf_op jit(solution)/shard_map/ppermute | solution.py:482
  58.5 29.6 %collective-permute-start.9 = (f32[384,384]{1,0:T(8,128)S(1)}, f32[384,384]{1,0:T(8,128)}, u32[]{:S(2)}, u32[]{:S(2)}) collective-permute-start(f32[384,384]{1,0:T(8,128)S(1)} %dynamic-slice_convert_fusion), channel_id=1, source_target_pairs={{0,1},{1,0},{2,3},{3,2},{4,5},{5,4},{6,7},{7,6},{8,9},{9,8},{10,11... | collective-permute-start | bytes 1769480 | tf_op jit(solution)/shard_map/ppermute | solution.py:482
  60.6 27.5 %collective-permute-start.5 = (f32[192,768]{1,0:T(8,128)}, f32[192,768]{1,0:T(8,128)S(1)}, u32[]{:S(2)}, u32[]{:S(2)}) collective-permute-start(f32[192,768]{1,0:T(8,128)} %collective-permute-done.4.w_near), channel_id=1, source_target_pairs={{0,2},{2,0},{4,6},{6,4},{8,10},{10,8},{12,14},{14,12},{16,18},{18,... | collective-permute-start | bytes 1769480 | tf_op jit(solution)/shard_map/ppermute | solution.py:485
  88.1 99.4 %collective-permute-start.10 = (f32[384,384]{1,0:T(8,128)}, f32[384,384]{1,0:T(8,128)}, u32[]{:S(2)}, u32[]{:S(2)}) collective-permute-start(f32[384,384]{1,0:T(8,128)} %collective-permute-done.9.q_near), channel_id=1, source_target_pairs={{0,2},{2,0},{4,6},{6,4},{8,10},{10,8},{12,14},{14,12},{16,18},{18,... | collective-permute-start | bytes 1769480 | tf_op jit(solution)/shard_map/ppermute | solution.py:485
  102.6 20.7 %collective-permute-start.6 = (f32[512,384]{1,0:T(8,128)}, f32[512,384]{1,0:T(8,128)S(1)}, u32[]{:S(2)}, u32[]{:S(2)}) collective-permute-start(f32[512,384]{1,0:T(8,128)} %get-tuple-element.57), channel_id=1, source_target_pairs={{0,1},{1,0},{2,3},{3,2},{4,5},{5,4},{6,7},{7,6},{8,9},{9,8},{10,11... | collective-permute-start | bytes 2359304 | tf_op jit(solution)/shard_map/ppermute | solution.py:482
  103.2 53.3 %collective-permute-start.7 = (f32[512,768]{1,0:T(8,128)}, f32[512,768]{1,0:T(8,128)S(1)}, u32[]{:S(2)}, u32[]{:S(2)}) collective-permute-start(f32[512,768]{1,0:T(8,128)} %get-tuple-element.58.part_own), channel_id=1, source_target_pairs={{0,1},{1,0},{2,3},{3,2},{4,5},{5,4},{6,7},{7,6},{8,9},{9,8},{10,11... | collective-permute-start | bytes 4718600 | tf_op jit(solution)/shard_map/ppermute | solution.py:482
  110.9 131.7 %collective-permute-start.38 = (f32[8,48,1536]{2,1,0:T(8,128)}, f32[8,48,1536]{2,1,0:T(8,128)}, u32[]{:S(2)}, u32[]{:S(2)}) collective-permute-start(f32[8,48,1536]{2,1,0:T(8,128)} %dynamic-slice_bitcast_fusion.1), channel_id=1, source_target_pairs={{0,2},{2,0},{4,6},{6,4},{8,10},{10,8},{12,14},{14,12},{16,18},{18,... | collective-permute-start | bytes 7077896 | tf_op jit(solution)/shard_map/ppermute | solution.py:485
  112.6 10.7 %copy-start.36 = (f32[512,384]{1,0:T(8,128)S(1)}, f32[512,384]{1,0:T(8,128)}, u32[]{:S(2)}) copy-start(f32[512,384]{1,0:T(8,128)} %get-tuple-element.56) | copy-start | bytes 2359300
  175.1 20.7 %collective-permute-start.8 = (f32[512,384]{1,0:T(8,128)}, f32[512,384]{1,0:T(8,128)S(1)}, u32[]{:S(2)}, u32[]{:S(2)}) collective-permute-start(f32[512,384]{1,0:T(8,128)} %get-tuple-element.63), channel_id=1, source_target_pairs={{0,1},{1,0},{2,3},{3,2},{4,5},{5,4},{6,7},{7,6},{8,9},{9,8},{10,11... | collective-permute-start | bytes 2359304 | tf_op jit(solution)/shard_map/ppermute | solution.py:482
  181.6 2.6 collective-permute-start.26
  183.0 2.1 collective-permute-start.34
  184.2 62.0 %collective-permute-start.42 = (f32[8,48,1536]{2,1,0:T(8,128)}, f32[8,48,1536]{2,1,0:T(8,128)}, u32[]{:S(2)}, u32[]{:S(2)}) collective-permute-start(f32[8,48,1536]{2,1,0:T(8,128)} %dynamic-slice_bitcast_fusion), channel_id=1, source_target_pairs={{0,2},{2,0},{4,6},{6,4},{8,10},{10,8},{12,14},{14,12},{16,18},{18,... | collective-permute-start | bytes 7077896 | tf_op jit(solution)/shard_map/ppermute | solution.py:485
  184.8 12.5 %copy-start.23 = (f32[8,48,384]{2,1,0:T(8,128)}, f32[8,48,384]{2,1,0:T(8,128)S(1)}, u32[]{:S(2)}) copy-start(f32[8,48,384]{2,1,0:T(8,128)S(1)} %bitcast_add_fusion.11) | copy-start | bytes 1769476
  185.0 110.9 %collective-permute-start.12 = (f32[1024,384]{1,0:T(8,128)}, f32[1024,384]{1,0:T(8,128)}, u32[]{:S(2)}, u32[]{:S(2)}) collective-permute-start(f32[1024,384]{1,0:T(8,128)} %fusion.4), channel_id=1, source_target_pairs={{0,1},{1,0},{2,3},{3,2},{4,5},{5,4},{6,7},{7,6},{8,9},{9,8},{10,11... | collective-permute-start | bytes 4718600 | tf_op jit(solution)/shard_map/ppermute | solution.py:482
  186.6 10.7 %copy-start.25 = (f32[8,48,384]{2,1,0:T(8,128)}, f32[8,48,384]{2,1,0:T(8,128)S(1)}, u32[]{:S(2)}) copy-start(f32[8,48,384]{2,1,0:T(8,128)S(1)} %bitcast_add_fusion.9) | copy-start | bytes 1769476
  187.5 104.3 %collective-permute-start.30 = (f32[8,48,768]{2,1,0:T(8,128)}, f32[8,48,768]{2,1,0:T(8,128)}, u32[]{:S(2)}, u32[]{:S(2)}) collective-permute-start(f32[8,48,768]{2,1,0:T(8,128)} %dynamic-slice_bitcast_fusion.5), channel_id=1, source_target_pairs={{0,2},{2,0},{4,6},{6,4},{8,10},{10,8},{12,14},{14,12},{16,18},{18,... | collective-permute-start | bytes 3538952 | tf_op jit(solution)/shard_map/ppermute | solution.py:485
  195.8 57.3 %collective-permute-start.27 = (f32[4,48,384]{2,1,0:T(8,128)S(1)}, f32[4,48,384]{2,1,0:T(8,128)S(1)}, u32[]{:S(2)}, u32[]{:S(2)}) collective-permute-start(f32[4,48,384]{2,1,0:T(8,128)S(1)} %dynamic-slice_bitcast_fusion.16), channel_id=1, source_target_pairs={{0,4},{2,6},{4,0},{6,2},{8,12},{10,14},{12,8},{14,10},{16,20},{18,... | collective-permute-start | bytes 884744 | tf_op jit(solution)/shard_map/ppermute | solution.py:485
  197.3 17.8 %copy-start.2 = (bf16[512,768]{1,0:T(8,128)(2,1)S(1)}, bf16[512,768]{1,0:T(8,128)(2,1)}, u32[]{:S(2)}) copy-start(bf16[512,768]{1,0:T(8,128)(2,1)} %get-tuple-element.79) | copy-start | bytes 2359300
  238.3 8.5 %slice-start = ((s8[4718592]{0:T(1024)(128)(4,1)}), s8[4194304]{0:T(1024)(128)(4,1)S(1)}, s32[]{:S(2)}) async-start(s8[4718592]{0:T(1024)(128)(4,1)} %bitcast.195), calls=%async_computation | async-start | bytes 8388608
  241.3 5.5 %slice-start.1 = ((s8[4718592]{0:T(1024)(128)(4,1)}), s8[524288]{0:T(1024)(128)(4,1)S(1)}, s32[]{:S(2)}) async-start(s8[4718592]{0:T(1024)(128)(4,1)} %bitcast.195), calls=%async_computation.1 | async-start | bytes 1048576
  242.6 10.7 %collective-permute-start.35 = (f32[4,48,384]{2,1,0:T(8,128)}, f32[4,48,384]{2,1,0:T(8,128)S(1)}, u32[]{:S(2)}, u32[]{:S(2)}) collective-permute-start(f32[4,48,384]{2,1,0:T(8,128)} %dynamic-slice_bitcast_fusion.14), channel_id=1, source_target_pairs={{0,4},{2,6},{4,0},{6,2},{8,12},{10,14},{12,8},{14,10},{16,20},{18,... | collective-permute-start | bytes 884744 | tf_op jit(solution)/shard_map/ppermute | solution.py:485
  246.3 4.2 collective-permute-start.13
  250.5 1.3 collective-permute-start.14
  251.8 48.6 %collective-permute-start.11 = (f32[512,384]{1,0:T(8,128)}, f32[512,384]{1,0:T(8,128)}, u32[]{:S(2)}, u32[]{:S(2)}) collective-permute-start(f32[512,384]{1,0:T(8,128)} %get-tuple-element.69), channel_id=1, source_target_pairs={{0,1},{1,0},{2,3},{3,2},{4,5},{5,4},{6,7},{7,6},{8,9},{9,8},{10,11... | collective-permute-start | bytes 2359304 | tf_op jit(solution)/shard_map/ppermute | solution.py:482
  253.1 138.8 %collective-permute-start.18 = (f32[8,48,1152]{2,1,0:T(8,128)}, f32[8,48,1152]{2,1,0:T(8,128)}, u32[]{:S(2)}, u32[]{:S(2)}) collective-permute-start(f32[8,48,1152]{2,1,0:T(8,128)} %dynamic-slice_bitcast_fusion.2), channel_id=1, source_target_pairs={{0,2},{2,0},{4,6},{6,4},{8,10},{10,8},{12,14},{14,12},{16,18},{18,... | collective-permute-start | bytes 5308424 | tf_op jit(solution)/shard_map/ppermute | solution.py:485
  253.4 4.2 collective-permute-start.15
  257.5 4.1 collective-permute-start.16
  261.7 5.0 %collective-permute-start.17 = (f32[14,768]{1,0:T(8,128)S(1)}, f32[14,768]{1,0:T(8,128)S(1)}, u32[]{:S(2)}, u32[]{:S(2)}) collective-permute-start(f32[14,768]{1,0:T(8,128)S(1)} %add.293), channel_id=1, source_target_pairs={{0,16},{2,18},{4,20},{6,22},{8,24},{10,26},{12,28},{14,30},{16,0},... | collective-permute-start | bytes 129032 | tf_op jit(solution)/shard_map/ppermute | solution.py:485
  266.7 5.5 %collective-permute-start.28 = (f32[2,48,384]{2,1,0:T(8,128)}, f32[2,48,384]{2,1,0:T(8,128)}, u32[]{:S(2)}, u32[]{:S(2)}) collective-permute-start(f32[2,48,384]{2,1,0:T(8,128)} %dynamic-slice_bitcast_fusion.19), channel_id=1, source_target_pairs={{0,8},{2,10},{4,12},{6,14},{8,0},{10,2},{12,4},{14,6},{16,24},{18,... | collective-permute-start | bytes 442376 | tf_op jit(solution)/shard_map/ppermute | solution.py:485
  270.8 21.0 %copy-start.30 = (f32[4,48,1536]{2,1,0:T(8,128)S(1)}, f32[4,48,1536]{2,1,0:T(8,128)}, u32[]{:S(2)}) copy-start(f32[4,48,1536]{2,1,0:T(8,128)} %dynamic-slice_bitcast_fusion.4) | copy-start | bytes 3538948
  272.2 5.4 %collective-permute-start.36 = (f32[2,48,384]{2,1,0:T(8,128)}, f32[2,48,384]{2,1,0:T(8,128)S(1)}, u32[]{:S(2)}, u32[]{:S(2)}) collective-permute-start(f32[2,48,384]{2,1,0:T(8,128)} %dynamic-slice_bitcast_fusion.18), channel_id=1, source_target_pairs={{0,8},{2,10},{4,12},{6,14},{8,0},{10,2},{12,4},{14,6},{16,24},{18,... | collective-permute-start | bytes 442376 | tf_op jit(solution)/shard_map/ppermute | solution.py:485
  277.6 7.5 %collective-permute-start.29 = (f32[1,48,384]{2,1,0:T(8,128)S(1)}, f32[1,48,384]{2,1,0:T(8,128)S(1)}, u32[]{:S(2)}, u32[]{:S(2)}) collective-permute-start(f32[1,48,384]{2,1,0:T(8,128)S(1)} %constant_dynamic-slice_fusion.4), channel_id=1, source_target_pairs={{0,16},{2,18},{4,20},{6,22},{8,24},{10,26},{12,28},{14,30},{16,0},... | collective-permute-start | bytes 221192 | tf_op jit(solution)/shard_map/ppermute | solution.py:485
  285.1 6.0 %collective-permute-start.37 = (f32[1,48,384]{2,1,0:T(8,128)S(1)}, f32[1,48,384]{2,1,0:T(8,128)S(1)}, u32[]{:S(2)}, u32[]{:S(2)}) collective-permute-start(f32[1,48,384]{2,1,0:T(8,128)S(1)} %constant_dynamic-slice_fusion.2), channel_id=1, source_target_pairs={{0,16},{2,18},{4,20},{6,22},{8,24},{10,26},{12,28},{14,30},{16,0},... | collective-permute-start | bytes 221192 | tf_op jit(solution)/shard_map/ppermute | solution.py:485
  291.1 3.7 collective-permute-start.22
  291.8 79.8 %collective-permute-start.39 = (f32[4,48,1536]{2,1,0:T(8,128)S(1)}, f32[4,48,1536]{2,1,0:T(8,128)S(1)}, u32[]{:S(2)}, u32[]{:S(2)}) collective-permute-start(f32[4,48,1536]{2,1,0:T(8,128)S(1)} %copy-done.30), channel_id=1, source_target_pairs={{0,4},{2,6},{4,0},{6,2},{8,12},{10,14},{12,8},{14,10},{16,20},{18,... | collective-permute-start | bytes 3538952 | tf_op jit(solution)/shard_map/ppermute | solution.py:485
  294.8 77.1 %collective-permute-start.43 = (f32[4,48,1536]{2,1,0:T(8,128)S(1)}, f32[4,48,1536]{2,1,0:T(8,128)S(1)}, u32[]{:S(2)}, u32[]{:S(2)}) collective-permute-start(f32[4,48,1536]{2,1,0:T(8,128)S(1)} %copy-done.31), channel_id=1, source_target_pairs={{0,4},{2,6},{4,0},{6,2},{8,12},{10,14},{12,8},{14,10},{16,20},{18,... | collective-permute-start | bytes 3538952 | tf_op jit(solution)/shard_map/ppermute | solution.py:485
  295.9 5.4 %copy-start.35 = (f32[512,384]{1,0:T(8,128)S(1)}, f32[512,384]{1,0:T(8,128)}, u32[]{:S(2)}) copy-start(f32[512,384]{1,0:T(8,128)} %get-tuple-element.68) | copy-start | bytes 2359300
  295.9 56.3 %collective-permute-start.23 = (f32[4,48,384]{2,1,0:T(8,128)S(1)}, f32[4,48,384]{2,1,0:T(8,128)S(1)}, u32[]{:S(2)}, u32[]{:S(2)}) collective-permute-start(f32[4,48,384]{2,1,0:T(8,128)S(1)} %dynamic-slice_bitcast_fusion.17), channel_id=1, source_target_pairs={{0,4},{2,6},{4,0},{6,2},{8,12},{10,14},{12,8},{14,10},{16,20},{18,... | collective-permute-start | bytes 884744 | tf_op jit(solution)/shard_map/ppermute | solution.py:485
  300.4 64.0 %collective-permute-start.31 = (f32[4,48,768]{2,1,0:T(8,128)S(1)}, f32[4,48,768]{2,1,0:T(8,128)S(1)}, u32[]{:S(2)}, u32[]{:S(2)}) collective-permute-start(f32[4,48,768]{2,1,0:T(8,128)S(1)} %dynamic-slice_bitcast_fusion.10), channel_id=1, source_target_pairs={{0,4},{2,6},{4,0},{6,2},{8,12},{10,14},{12,8},{14,10},{16,20},{18,... | collective-permute-start | bytes 1769480 | tf_op jit(solution)/shard_map/ppermute | solution.py:485
  352.3 19.3 %copy-start.11 = (f32[8,48,1536]{2,1,0:T(8,128)S(1)}, f32[8,48,1536]{2,1,0:T(8,128)}, u32[]{:S(2)}) copy-start(f32[8,48,1536]{2,1,0:T(8,128)} %copy-done.10) | copy-start | bytes 7077892
  352.3 12.2 %collective-permute-start.24 = (f32[2,48,384]{2,1,0:T(8,128)S(1)}, f32[2,48,384]{2,1,0:T(8,128)S(1)}, u32[]{:S(2)}, u32[]{:S(2)}) collective-permute-start(f32[2,48,384]{2,1,0:T(8,128)S(1)} %dynamic-slice_bitcast_fusion.20), channel_id=1, source_target_pairs={{0,8},{2,10},{4,12},{6,14},{8,0},{10,2},{12,4},{14,6},{16,24},{18,... | collective-permute-start | bytes 442376 | tf_op jit(solution)/shard_map/ppermute | solution.py:485
  364.6 6.4 %collective-permute-start.25 = (f32[1,48,384]{2,1,0:T(8,128)S(1)}, f32[1,48,384]{2,1,0:T(8,128)S(1)}, u32[]{:S(2)}, u32[]{:S(2)}) collective-permute-start(f32[1,48,384]{2,1,0:T(8,128)S(1)} %constant_dynamic-slice_fusion.5), channel_id=1, source_target_pairs={{0,16},{2,18},{4,20},{6,22},{8,24},{10,26},{12,28},{14,30},{16,0},... | collective-permute-start | bytes 221192 | tf_op jit(solution)/shard_map/ppermute | solution.py:485
  365.2 11.6 %collective-permute-start.32 = (f32[2,48,768]{2,1,0:T(8,128)S(1)}, f32[2,48,768]{2,1,0:T(8,128)S(1)}, u32[]{:S(2)}, u32[]{:S(2)}) collective-permute-start(f32[2,48,768]{2,1,0:T(8,128)S(1)} %dynamic-slice_bitcast_fusion.15), channel_id=1, source_target_pairs={{0,8},{2,10},{4,12},{6,14},{8,0},{10,2},{12,4},{14,6},{16,24},{18,... | collective-permute-start | bytes 884744 | tf_op jit(solution)/shard_map/ppermute | solution.py:485
  371.8 23.6 %collective-permute-start.40 = (f32[2,48,1536]{2,1,0:T(8,128)S(1)}, f32[2,48,1536]{2,1,0:T(8,128)}, u32[]{:S(2)}, u32[]{:S(2)}) collective-permute-start(f32[2,48,1536]{2,1,0:T(8,128)S(1)} %dynamic-slice_bitcast_fusion.8), channel_id=1, source_target_pairs={{0,8},{2,10},{4,12},{6,14},{8,0},{10,2},{12,4},{14,6},{16,24},{18,... | collective-permute-start | bytes 1769480 | tf_op jit(solution)/shard_map/ppermute | solution.py:485
  376.9 14.3 %collective-permute-start.33 = (f32[1,48,768]{2,1,0:T(8,128)S(1)}, f32[1,48,768]{2,1,0:T(8,128)S(1)}, u32[]{:S(2)}, u32[]{:S(2)}) collective-permute-start(f32[1,48,768]{2,1,0:T(8,128)S(1)} %constant_dynamic-slice_fusion.3), channel_id=1, source_target_pairs={{0,16},{2,18},{4,20},{6,22},{8,24},{10,26},{12,28},{14,30},{16,0},... | collective-permute-start | bytes 442376 | tf_op jit(solution)/shard_map/ppermute | solution.py:485
  378.5 32.1 %collective-permute-start.44 = (f32[2,48,1536]{2,1,0:T(8,128)}, f32[2,48,1536]{2,1,0:T(8,128)}, u32[]{:S(2)}, u32[]{:S(2)}) collective-permute-start(f32[2,48,1536]{2,1,0:T(8,128)} %dynamic-slice_bitcast_fusion.7), channel_id=1, source_target_pairs={{0,8},{2,10},{4,12},{6,14},{8,0},{10,2},{12,4},{14,6},{16,24},{18,... | collective-permute-start | bytes 1769480 | tf_op jit(solution)/shard_map/ppermute | solution.py:485
  394.2 18.5 %collective-permute-start.19 = (f32[4,48,1152]{2,1,0:T(8,128)S(1)}, f32[4,48,1152]{2,1,0:T(8,128)S(1)}, u32[]{:S(2)}, u32[]{:S(2)}) collective-permute-start(f32[4,48,1152]{2,1,0:T(8,128)S(1)} %dynamic-slice_bitcast_fusion.6), channel_id=1, source_target_pairs={{0,4},{2,6},{4,0},{6,2},{8,12},{10,14},{12,8},{14,10},{16,20},{18,... | collective-permute-start | bytes 2654216 | tf_op jit(solution)/shard_map/ppermute | solution.py:485
  396.6 20.0 %collective-permute-start.41 = (f32[1,48,1536]{2,1,0:T(8,128)S(1)}, f32[1,48,1536]{2,1,0:T(8,128)S(1)}, u32[]{:S(2)}, u32[]{:S(2)}) collective-permute-start(f32[1,48,1536]{2,1,0:T(8,128)S(1)} %constant_dynamic-slice_fusion.1), channel_id=1, source_target_pairs={{0,16},{2,18},{4,20},{6,22},{8,24},{10,26},{12,28},{14,30},{16,0},... | collective-permute-start | bytes 884744 | tf_op jit(solution)/shard_map/ppermute | solution.py:485
  411.8 19.0 %collective-permute-start.45 = (f32[1,48,1536]{2,1,0:T(8,128)S(1)}, f32[1,48,1536]{2,1,0:T(8,128)S(1)}, u32[]{:S(2)}, u32[]{:S(2)}) collective-permute-start(f32[1,48,1536]{2,1,0:T(8,128)S(1)} %constant_dynamic-slice_fusion), channel_id=1, source_target_pairs={{0,16},{2,18},{4,20},{6,22},{8,24},{10,26},{12,28},{14,30},{16,0},... | collective-permute-start | bytes 884744 | tf_op jit(solution)/shard_map/ppermute | solution.py:485
  412.9 17.7 %collective-permute-start.20 = (f32[2,48,1152]{2,1,0:T(8,128)S(1)}, f32[2,48,1152]{2,1,0:T(8,128)S(1)}, u32[]{:S(2)}, u32[]{:S(2)}) collective-permute-start(f32[2,48,1152]{2,1,0:T(8,128)S(1)} %dynamic-slice_bitcast_fusion.13), channel_id=1, source_target_pairs={{0,8},{2,10},{4,12},{6,14},{8,0},{10,2},{12,4},{14,6},{16,24},{18,... | collective-permute-start | bytes 1327112 | tf_op jit(solution)/shard_map/ppermute | solution.py:485
  430.6 10.9 %copy-start.1 = (bf16[8,128,768]{2,1,0:T(8,128)(2,1)S(1)}, bf16[8,128,768]{2,1,0:T(8,128)(2,1)}, u32[]{:S(2)}) copy-start(bf16[8,128,768]{2,1,0:T(8,128)(2,1)} %param.23) | copy-start | bytes 4718596
  430.7 10.0 %collective-permute-start.21 = (f32[1,48,1152]{2,1,0:T(8,128)S(1)}, f32[1,48,1152]{2,1,0:T(8,128)S(1)}, u32[]{:S(2)}, u32[]{:S(2)}) collective-permute-start(f32[1,48,1152]{2,1,0:T(8,128)S(1)} %constant_dynamic-slice_fusion.6), channel_id=1, source_target_pairs={{0,16},{2,18},{4,20},{6,22},{8,24},{10,26},{12,28},{14,30},{16,0},... | collective-permute-start | bytes 663560 | tf_op jit(solution)/shard_map/ppermute | solution.py:485
  (39 other events, 99.6 us)

commit v2 on v1

--- a/solution.py
+++ b/solution.py
@@ -111,21 +111,22 @@
 
 
 def join_peer(peer_ref, near_ref, far_ref, core):
-    half = near_ref.shape[0]
+    half = peer_ref.shape[0] // 2
     peer_ref[pl.ds(pl.multiple_of(core * half, 64), half), :] = near_ref[...].astype(BF16)
     peer_ref[pl.ds(pl.multiple_of((1 - core) * half, 64), half), :] = far_ref[...].astype(BF16)
 
 
-def self_forward(slots, info, tok, weight, bias, gain, shift, cosine, sine, ln_out, qkv_out, mix_out, lse_out, mask_out):
+def self_forward(slots, info, tok, weight, bias, gains, shifts, cosine, sine, ln_out, qkv_out, mix_out, lse_out, mask_out):
     count = tok.shape[0]
     pairs = weight.shape[2] // LANES
+    gain, shift = gains[0:1, :], shifts[0:1, :]
     fill_mask(mask_out, info, slots)
     step = 256
 
     def project(index, carry):
         rows = pl.ds(pl.multiple_of(index * step, step), step)
         xhat, _ = norm_stats(tok[rows, :].astype(F32))
-        ln = (xhat * gain[...] + shift[...]).astype(BF16)
+        ln = (xhat * gain + shift).astype(BF16)
         ln_out[rows, :] = ln
         for part in range(3):
             made = dot(ln, weight[part]) + bias[part : part + 1, :]
@@ -160,12 +161,13 @@
 
 
 def cross_forward(
-    slots, span, info, picks, tok, mix_own, mix_peer, w_own, w_near, w_far, out_bias, gain, shift, q_w, q_b, kv,
+    slots, span, info, picks, tok, mix_own, mix_peer, w_own, w_near, w_far, out_bias, gains, shifts, q_w, q_b, kv,
     hidden_out, ln_out, query_out, mix_out, lse_out, w_peer, field,
 ):
     count = tok.shape[0]
     local = q_w.shape[1]
     pairs = local // LANES
+    gain, shift = gains[1:2, :], shifts[1:2, :]
     join_peer(w_peer, w_near, w_far, info[2])
     step = 256
 
@@ -177,7 +179,7 @@
         hidden = tok[rows, :].astype(F32) + (attn + out_bias[...])
         hidden_out[rows, :] = hidden
         xhat, _ = norm_stats(hidden)
-        ln = (xhat * gain[...] + shift[...]).astype(BF16)
+        ln = (xhat * gain + shift).astype(BF16)
         ln_out[rows, :] = ln
         field[rows, :] = dot(ln, q_w[...]) + q_b[...]
         return carry
@@ -223,7 +225,7 @@
 
 
 def feed_forward(
-    info, hidden_one, mix_own, mix_peer, w_own, w_near, w_far, out_bias, gain, shift, in_w, in_b, out_w, end_bias, grad,
+    info, hidden_one, mix_own, mix_peer, w_own, w_near, w_far, out_bias, gains, shifts, in_w, in_b, out_w, end_bias, grad,
     hidden_out, ln_out, act_out, pre_out, keep_out, send_out, part_out, bias_out, w_peer,
 ):
     @pl.when(pl.program_id(0) == 0)
@@ -238,7 +240,7 @@
     hidden = hidden_one[...] + (cross + out_bias[...])
     hidden_out[...] = hidden
     xhat, _ = norm_stats(hidden)
-    ln = (xhat * gain[...] + shift[...]).astype(BF16)
+    ln = (xhat * gains[2:3, :] + shifts[2:3, :]).astype(BF16)
     ln_out[...] = ln
     act, slope = gelu_parts(dot(ln, in_w[...]) + in_b[...])
     act = act.astype(BF16)
@@ -252,30 +254,32 @@
 
 
 def cross_backward(
-    slots, span, info, picks, part_own, part_peer, hidden, out_grad, gain, out_w, query, kv, lse,
-    grad_out, low_out, query_out, query_low, store_out, gain_out, shift_out, bias_out, q_bias_out, v_bias_out,
-    rows_grad, field, store,
+    slots, span, order, info, picks, part_own, part_peer, hidden, out_grad, gains, out_w, query, kv, lse,
+    mix, ln, flat_store,
+    grad_out, query_out, query_low, store_out, sums_out, q_bias_out, v_bias_out, keep_out, send_one, send_two,
+    rows_grad, field, store, low_out, turned, ordered,
 ):
     count = hidden.shape[0]
     local = query.shape[1]
     pairs = local // LANES
     step = 256
-    gain_out[...] = jnp.zeros_like(gain_out)
-    shift_out[...] = jnp.zeros_like(shift_out)
-    bias_out[...] = jnp.zeros_like(bias_out)
+    gain = gains[2:3, :]
+    sums_out[...] = jnp.zeros_like(sums_out)
     store[...] = jnp.zeros_like(store)
 
     def project(index, carry):
         rows = pl.ds(pl.multiple_of(index * step, step), step)
         gradient = part_own[rows, :] + part_peer[rows, :]
         xhat, scale = norm_stats(hidden[rows, :])
-        gain_out[...] += jnp.sum(gradient * xhat, axis=0, keepdims=True)
-        shift_out[...] += jnp.sum(gradient, axis=0, keepdims=True)
-        two = out_grad[rows, :].astype(F32) + norm_back(xhat, scale, gain[...], gradient)
+        sums_out[0:1, :] += jnp.sum(gradient * xhat, axis=0, keepdims=True)
+        sums_out[1:2, :] += jnp.sum(gradient, axis=0, keepdims=True)
+        cotangent = out_grad[rows, :].astype(F32)
+        sums_out[3:4, :] += jnp.sum(cotangent, axis=0, keepdims=True)
+        two = cotangent + norm_back(xhat, scale, gain, gradient)
         grad_out[rows, :] = two
         low = two.astype(BF16)
         low_out[rows, :] = low
-        bias_out[...] += jnp.sum(low.astype(F32), axis=0, keepdims=True)
+        sums_out[2:3, :] += jnp.sum(low.astype(F32), axis=0, keepdims=True)
         field[rows, :] = dot_t(low, out_w[...])
         return carry
 
@@ -329,17 +333,21 @@
         return carry
 
     lax.fori_loop(0, store.shape[0] // span, flush, 0)
+    terms = ((low_out, mix), (ln, query_low), (flat_store, store_out))
+    fill_grads(order, info[3 + slots], terms, keep_out, (send_one, send_two), turned, ordered)
 
 
 def self_backward(
-    info, query_own, query_peer, q_w, q_near, q_far, hidden, grad_two, gain_two, out_w, qkv, lse, mask, cosine, sine, w,
-    tok, gain_one,
-    low_out, qkv_out, keep_out, send_out, sums_out, q_bias_out, q_peer, one, mix_grad, key_grad, value_grad, part,
+    slots, order, info, query_own, query_peer, q_w, q_near, q_far, hidden, grad_two, gains, out_w, qkv, lse, mask, cosine, sine, w,
+    tok, cross_sums, q_bias, v_bias, in_bias, out_send, mix, ln,
+    keep_out, send_out, sums_out, grads_keep, grads_one, grads_two,
+    q_peer, one, mix_grad, key_grad, value_grad, part, low_out, qkv_out, turned, ordered,
 ):
     count = tok.shape[0]
     local = out_w.shape[0]
     pairs = local // LANES
     step = 256
+    gain_one, gain_two = gains[0:1, :], gains[1:2, :]
     join_peer(q_peer, q_near, q_far, info[2])
     sums_out[...] = jnp.zeros_like(sums_out)
     half = keep_out.shape[1]
@@ -348,17 +356,17 @@
 
     def project(index, carry):
         rows = pl.ds(pl.multiple_of(index * step, step), step)
-        gradient = dot_t(query_own[rows, :], q_w[...]) + dot_t(
+        gradient = dot_t(query_own[rows, :], q_w[...]) + dot(
             query_peer[rows, :].astype(BF16), q_peer[...]
         )
         xhat, scale = norm_stats(hidden[rows, :])
-        sums_out[0:1, :] += jnp.sum(gradient * xhat, axis=0, keepdims=True)
-        sums_out[1:2, :] += jnp.sum(gradient, axis=0, keepdims=True)
-        grad_one = grad_two[rows, :] + norm_back(xhat, scale, gain_two[...], gradient)
+        sums_out[2:3, :] += jnp.sum(gradient * xhat, axis=0, keepdims=True)
+        sums_out[3:4, :] += jnp.sum(gradient, axis=0, keepdims=True)
+        grad_one = grad_two[rows, :] + norm_back(xhat, scale, gain_two, gradient)
         one[rows, :] = grad_one
         low = grad_one.astype(BF16)
         low_out[rows, :] = low
-        sums_out[2:3, :] += jnp.sum(low.astype(F32), axis=0, keepdims=True)
+        sums_out[4:5, :] += jnp.sum(low.astype(F32), axis=0, keepdims=True)
         mixed = dot_t(low, out_w[...])
         for pair in range(pairs):
             mix_grad[pair, rows, :] = mixed[:, pair * LANES : (pair + 1) * LANES].astype(BF16)
@@ -396,10 +404,27 @@
 
     lax.fori_loop(0, pairs, attend, 0)
 
-    for piece in range(3 * pairs):
-        q_bias_out[:, piece * LANES : (piece + 1) * LANES] = jnp.sum(
-            qkv_out[piece].astype(F32), axis=0, keepdims=True
+    sums_out[5:9, :] = cross_sums[0:4, :]
+
+    def place(piece, columns):
+        start = (piece % 2) * local
+        sums_out[9 + piece // 2 : 10 + piece // 2, start : start + local] = columns
+
+    for part_at in range(3):
+        place(
+            part_at,
+            jnp.concatenate(
+                [
+                    jnp.sum(qkv_out[part_at * pairs + pair].astype(F32), axis=0, keepdims=True)
+                    for pair in range(pairs)
+                ],
+                axis=1,
+            ),
         )
+    place(3, q_bias[...])
+    place(4, v_bias[...])
+    for piece in range(in_bias.shape[1] // local):
+        place(5 + piece, in_bias[:, piece * local : (piece + 1) * local])
 
     def finish(index, carry):
         rows = pl.ds(pl.multiple_of(index * step, step), step)
@@ -410,14 +435,81 @@
             )
             gradient = gradient + dot_t(joined, w[part_at])
         xhat, scale = norm_stats(tok[rows, :].astype(F32))
-        sums_out[3:4, :] += jnp.sum(gradient * xhat, axis=0, keepdims=True)
-        sums_out[4:5, :] += jnp.sum(gradient, axis=0, keepdims=True)
-        part[...] = norm_back(xhat, scale, gain_one[...], gradient)
+        sums_out[0:1, :] += jnp.sum(gradient * xhat, axis=0, keepdims=True)
+        sums_out[1:2, :] += jnp.sum(gradient, axis=0, keepdims=True)
+        part[...] = norm_back(xhat, scale, gain_one, gradient)
         keep_out[rows, :] = part[:, own] + one[rows, own]
-        send_out[rows, :] = part[:, peer]
+        send_out[rows, :half] = part[:, peer]
+        send_out[rows, half:] = out_send[rows, :]
         return carry
 
     lax.fori_loop(0, count // step, finish, 0)
+    terms = ((low_out, mix), (ln, qkv_out))
+    fill_grads(order, info[3 + slots], terms, grads_keep, (grads_one, grads_two), turned, ordered)
+
+
+def slice_at(place, order):
+    last = len(order) - 1
+    return sum(bit * ((place >> (last - at)) & 1) for at, bit in enumerate(order))
+
+
+def fill_grads(order, me, terms, keep_out, send_outs, turned, ordered):
+    width = turned.shape[0]
+    half = width // 2
+    share = send_outs[0].shape[1]
+    column = 0
+    for left, right in terms:
+        count = left.shape[0]
+        if order is None:
+            ordered[:, :count] = left[...].T
+        else:
+            parts = 1 << len(order)
+            slab = width // parts
+            turned[:, :count] = left[...].T
+
+            def move(place, carry, count=count):
+                source = pl.multiple_of((me ^ slice_at(place, order)) * slab, 16)
+                target = pl.multiple_of(place * slab, 16)
+                ordered[pl.ds(target, slab), :count] = turned[pl.ds(source, slab), :count]
+                return carry
+
+            lax.fori_loop(0, parts, move, 0)
+        pieces = right.shape[0] if len(right.shape) == 3 else right.shape[1] // LANES
+        group = 3
+        wide = group * LANES
+        for index in range(pieces // group):
+            if len(right.shape) == 3:
+                field = jnp.concatenate([right[index * group + at] for at in range(group)], axis=1)
+            else:
+                field = right[:, index * wide : (index + 1) * wide]
+            field = field.astype(BF16)
+            keep_out[:, column : column + wide] = dot(ordered[:half, :count], field)
+            at = column % share
+            send_outs[column // share][:, at : at + wide] = dot(ordered[half:, :count], field)
+            column += wide
+
+
+def weight_grads(order, me_at, info, *refs):
+    products = (len(refs) - 7) // 2
+    lefts, rights = refs[:products], refs[products : 2 * products]
+    keep_out, *send_outs = refs[2 * products : -2]
+    fill_grads(order, info[me_at], zip(lefts, rights), keep_out, send_outs, *refs[-2:])
+
+
+def add_halves(pieces, joined, split, *refs):
+    kept, came = refs[:2], refs[2 : 2 + 2 * pieces]
+    outs = refs[2 + 2 * pieces + (2 if joined else 0) :]
+    share = came[0].shape[1]
+    for side in range(2):
+        for piece in range(pieces):
+            start = piece * share
+            value = kept[side][:, start : start + share] + came[2 * piece + side][...]
+            if start < split:
+                outs[side][:, start : start + share] = value
+            else:
+                outs[2 + side][:, start - split : start - split + share] = value
+        if joined:
+            outs[side][:, pieces * share :] = refs[2 + 2 * pieces + side][...]
 
 
 def whole(count):
@@ -432,7 +524,15 @@
     return jax.ShapeDtypeStruct(dims, kind)
 
 
-def call(body, name, small, big, outs, scratch=()):
+def after(value, *others):
+    return lax.optimization_barrier((value, *others))[0]
+
+
+def work(flops):
+    return pl.CostEstimate(flops=flops, bytes_accessed=1, transcendentals=0)
+
+
+def call(body, name, small, big, outs, scratch=(), flops=0):
     return pl.pallas_call(
         body,
         name=name,
@@ -440,6 +540,7 @@
         in_specs=scalars(len(small)) + whole(len(big)),
         out_specs=whole(len(outs)),
         scratch_shapes=scratch,
+        cost_estimate=work(flops),
     )(*small, *big)
 
 
@@ -474,6 +575,7 @@
     stored, span = neighbours.shape[:2]
     slots = seq_lengths.shape[1]
     dp_size = lax.axis_size("dp")
+    slab = width // dp_size
     tp_at = lax.axis_index("tp")
     dp_at = lax.axis_index("dp")
     core = dp_at % 2
@@ -484,18 +586,24 @@
     def across(value, bit):
         return lax.ppermute(value, "dp", [(at, at ^ bit) for at in range(dp_size)])
 
-    def fetch(weight):
+    def mine(weight):
         half = weight.shape[0] // 2
-        mine = lax.dynamic_slice_in_dim(weight, core * half, half, 0).astype(F32)
-        near = swap(mine)
-        return near, across(near, 1)
+        return lax.dynamic_slice_in_dim(weight, core * half, half, 0).astype(F32)
+
+    def mine_turned(weight):
+        half = weight.shape[1] // 2
+        return lax.dynamic_slice_in_dim(weight, core * half, half, 1).T.astype(F32)
 
     def row(value):
         return value.reshape(1, -1)
 
     padded = count // group_sizes[0]
     info = jnp.concatenate(
-        [jnp.stack([padded, tp_at.astype(jnp.int32), core.astype(jnp.int32)]), seq_lengths[0]]
+        [
+            jnp.stack([padded, tp_at.astype(jnp.int32), core.astype(jnp.int32)]),
+            seq_lengths[0],
+            dp_at.astype(jnp.int32)[None],
+        ]
     )
     position = (jnp.arange(count, dtype=jnp.int32) % padded).astype(F32)
     halfway = HEAD_DIM // 2
@@ -504,16 +612,69 @@
     cosine = jnp.cos(angles)
     sine = jnp.sin(angles)
 
-    so_near, so_far = fetch(self_out_w)
-    co_near, co_far = fetch(cross_out_w)
-    cq_near, cq_far = fetch(cross_q_w)
-
+    bits = [1 << at for at in range(dp_size.bit_length() - 1)]
+    order = bits if slab % 16 == 0 else None
+
+    def add_sent(name, kept, came, joined=(), split=None):
+        rows, total = kept.shape[0] // 2, kept.shape[1]
+        split = split or total
+        steps = 4
+        block = rows // steps
+
+        def sides(value):
+            wide = value.shape[1]
+            return [
+                pl.BlockSpec((block, wide), lambda i: (i, 0)),
+                pl.BlockSpec((block, wide), lambda i: (i + steps, 0)),
+            ]
+
+        straight = lambda wide: pl.BlockSpec((block, wide), lambda i: (i, 0))
+        first = split + sum(value.shape[1] for value in joined[:1])
+        wides = [first, first] + ([total - split] * 2 if split < total else [])
+        return pl.pallas_call(
+            partial(add_halves, len(came), bool(joined), split),
+            name=name,
+            grid=(steps,),
+            in_specs=[spec for value in (kept, *came) for spec in sides(value)]
+            + [straight(value.shape[1]) for value in joined],
+            out_specs=[straight(wide) for wide in wides],
+            out_shape=[shape((rows, wide)) for wide in wides],
+            cost_estimate=work(0),
+        )(*[value for value in (kept, *came) for _ in range(2)], *joined)
+
+    def sorted_halves(kept, *sent):
+        if order is not None:
+            return kept, sent
+        value = jnp.concatenate([kept, jnp.concatenate(sent, axis=1)], axis=0)
+        places = jnp.array([slice_at(place, bits) for place in range(dp_size)], jnp.int32) ^ dp_at
+        value = jnp.take(value.reshape(dp_size, slab, -1), places, axis=0).reshape(value.shape)
+        return value[: width // 2], jnp.split(value[width // 2 :], len(sent), axis=1)
+
+    def core_halve(halves, gate=None):
+        kept, sent = halves
+        came = jnp.concatenate([across(piece, 1) for piece in sent], axis=1)
+        return merge(kept if gate is None else after(kept, *gate), came)
+
+    def grads_of(total, shares):
+        return (shape((width // 2, total)),) + (shape((width // 2, total // shares)),) * shares
+
+    def turning(most):
+        return [pltpu.VMEM((width, most), BF16), pltpu.VMEM((width, most), BF16)]
+
+    def merge(kept, arrived):
+        half = kept.shape[0] // 2
+        return kept[:half] + arrived[:half], kept[half:] + arrived[half:]
+
+    def halve(kept, sent, bit):
+        return merge(kept, across(sent, bit))
+
+    so_near = swap(mine(self_out_w))
     qkv_w = jnp.swapaxes(self_qkv_w, 0, 1)
     ln_one, qkv, self_mix, self_lse, mask = call(
         partial(self_forward, slots),
         "self_forward",
         (info,),
-        (tokens, qkv_w, self_qkv_b, norm_gain[0:1], norm_bias[0:1], cosine, sine),
+        (tokens, qkv_w, self_qkv_b, norm_gain, norm_bias, cosine, sine),
         (
             shape((count, width), BF16),
             shape((3 * pairs, count, LANES), BF16),
@@ -521,8 +682,10 @@
             shape((count, LANES)),
             shape((count, count)),
         ),
+        flops=11_000_000_000,
     )
     self_mix_peer = swap(self_mix)
+    so_far = across(so_near, 1)
 
     kv_w = jnp.swapaxes(cross_kv_w, 0, 1).reshape(2, width, local)
     flat_store = neighbours.reshape(stored * span, width)
@@ -530,6 +693,7 @@
     joined_kv = jnp.concatenate([kv_w[0], kv_w[1]], axis=1)
     store_kv = (dot(flat_store, joined_kv) + kv_bias).astype(BF16)
 
+    co_near = swap(after(mine(cross_out_w), self_mix_peer))
     hidden_one, ln_two, cross_query, cross_mix, cross_lse = call(
         partial(cross_forward, slots, span),
         "cross_forward",
@@ -542,8 +706,8 @@
             so_near,
             so_far,
             row(self_out_b),
-            norm_gain[1:2],
-            norm_bias[1:2],
+            norm_gain,
+            norm_bias,
             cross_q_w,
             row(cross_q_b),
             store_kv,
@@ -556,8 +720,11 @@
             shape((count, LANES)),
         ),
         [pltpu.VMEM((local, width), BF16), pltpu.VMEM((count, local), F32)],
+        flops=14_000_000_000,
     )
     cross_mix_peer = swap(cross_mix)
+    co_far = across(co_near, 1)
+    cq_near = swap(after(mine_turned(cross_q_w), cross_mix_peer))
 
     step = 256
     rows = lambda wide: pl.BlockSpec((step, wide), lambda i: (i, 0))
@@ -591,6 +758,7 @@
             shape((1, hidden)),
         ],
         scratch_shapes=[pltpu.VMEM((local, width), BF16)],
+        cost_estimate=work(14_000_000_000),
     )(
         info,
         hidden_one,
@@ -600,8 +768,8 @@
         co_near,
         co_far,
         row(cross_out_b),
-        norm_gain[2:3],
-        norm_bias[2:3],
+        norm_gain,
+        norm_bias,
         mlp_in_w,
         row(mlp_in_b),
         mlp_out_w,
@@ -609,69 +777,80 @@
         out_grad,
     )
     part_three_peer = swap(part_three)
-    out_back = swap(out_send)
-    output = (out_keep + out_back).astype(BF16)
-
-    mlp_out_w_grad = tdot(out_grad, act)
-    mlp_in_w_grad = tdot(ln_three, grad_pre)
-    mlp_out_b_grad = jnp.sum(out_grad.astype(F32), axis=0, keepdims=True)
-
+    cq_far = across(cq_near, 1)
+    mlp = sorted_halves(
+        *call(
+            partial(weight_grads, order, 3 + slots),
+            "mlp_grads",
+            (info,),
+            (after(out_grad, cq_near), ln_three, act, grad_pre),
+            grads_of(2 * hidden, 4),
+            turning(count),
+            flops=0,
+        )
+    )
+    came_mlp = [across(piece, 1) for piece in mlp[1]]
+    *first, late_kept, late_sent = add_sent("add_mlp", mlp[0], came_mlp, split=3 * hidden // 2)
     (
         grad_two,
-        grad_cross,
         grad_query,
         grad_query_low,
         grad_store,
-        gain_three,
-        shift_three,
-        cross_out_b_grad,
+        cross_sums,
         cross_q_b_grad,
         cross_v_b_grad,
+        *cross_halves,
     ) = call(
-        partial(cross_backward, slots, span),
+        partial(cross_backward, slots, span, order),
         "cross_backward",
         (info, stretch_neighbours),
         (
             part_three,
             part_three_peer,
-            hidden_two,
+            after(hidden_two, first[1]),
             out_grad,
-            norm_gain[2:3],
+            norm_gain,
             cross_out_w,
             cross_query,
             store_kv,
             cross_lse,
+            cross_mix,
+            ln_two,
+            flat_store,
         ),
         (
             shape((count, width)),
-            shape((count, width), BF16),
             shape((count, local)),
             shape((count, local), BF16),
             shape((stored * span, 2 * local), BF16),
-            shape((1, width)),
-            shape((1, width)),
-            shape((1, width)),
+            shape((8, width)),
             shape((1, local)),
             shape((1, local)),
+            *grads_of(4 * local, 2),
         ),
         [
             pltpu.VMEM((count, local), BF16),
             pltpu.VMEM((count, local), F32),
             pltpu.VMEM((stored * span, 2 * local), F32),
+            pltpu.VMEM((count, width), BF16),
+            *turning(max(count, stored * span)),
         ],
+        flops=17_000_000_000,
     )
     grad_query_peer = swap(grad_query)
+    first = halve(*first, bits[1])
 
     own_kv = lax.dynamic_slice_in_dim(joined_kv, tp_at * own_width, own_width, 0)
     peer_kv = lax.dynamic_slice_in_dim(joined_kv, (1 - tp_at) * own_width, own_width, 0)
-    store_back = swap(dot_t(grad_store, peer_kv))
-    neighbours_grad = (dot_t(grad_store, own_kv) + store_back).astype(BF16)
-    cross_out_w_grad = tdot(grad_cross, cross_mix.astype(BF16))
-    cross_q_w_grad = tdot(ln_two, grad_query_low)
-    cross_kv_w_grad = tdot(flat_store, grad_store)
-
-    grad_attn, grad_qkv, tok_keep, tok_send, sums, self_qkv_b_grad = call(
-        self_backward,
+    store_send = dot_t(grad_store, peer_kv)
+    store_keep = dot_t(grad_store, own_kv)
+    cross = sorted_halves(*cross_halves)
+    came_cross = [across(piece, 1) for piece in cross[1]]
+    third = add_sent("add_cross", cross[0], came_cross, (late_kept, late_sent))
+    store_back = swap(after(store_send, third[1]))
+
+    tok_keep, both_send, sums, *self_halves = call(
+        partial(self_backward, slots, order),
         "self_backward",
         (info,),
         (
@@ -681,8 +860,8 @@
             cq_near,
             cq_far,
             hidden_one,
-            grad_two,
-            norm_gain[1:2],
+            after(grad_two, third[1], first[1]),
+            norm_gain,
             self_out_w,
             qkv,
             self_lse,
@@ -691,91 +870,85 @@
             sine,
             qkv_w,
             tokens,
-            norm_gain[0:1],
+            cross_sums,
+            cross_q_b_grad,
+            cross_v_b_grad,
+            mlp_in_b_grad,
+            out_send,
+            self_mix,
+            ln_one,
         ),
         (
-            shape((count, width), BF16),
-            shape((3 * pairs, count, LANES), BF16),
             shape((count, own_width)),
-            shape((count, own_width)),
-            shape((8, width)),
-            shape((1, 3 * local)),
+            shape((count, width)),
+            shape((16, width)),
+            *grads_of(4 * local, 2),
         ),
         [
-            pltpu.VMEM((width, local), BF16),
+            pltpu.VMEM((local, width), BF16),
             pltpu.VMEM((count, width), F32),
             pltpu.VMEM((pairs, count, LANES), BF16),
             pltpu.VMEM((count, LANES), F32),
             pltpu.VMEM((count, LANES), F32),
             pltpu.VMEM((256, width), F32),
+            pltpu.VMEM((count, width), BF16),
+            pltpu.VMEM((3 * pairs, count, LANES), BF16),
+            *turning(count),
         ],
+        flops=40_000_000_000,
     )
-    tokens_grad = (tok_keep + swap(tok_send)).astype(BF16)
-    self_out_w_grad = tdot(grad_attn, self_mix.astype(BF16))
-    self_qkv_w_grad = jnp.concatenate([tdot(ln_one, grad_qkv[piece]) for piece in range(3 * pairs)], axis=1)
-
-    def scatter(value):
-        value = value.reshape(dp_size, width // dp_size, value.shape[1])
-        bit = 1
-        while bit < dp_size:
-            value = value.reshape(-1, 2, *value.shape[1:])
-            mine = (dp_at // bit) % 2
-            sent = lax.dynamic_index_in_dim(value, 1 - mine, 1, keepdims=False)
-            held = lax.dynamic_index_in_dim(value, mine, 1, keepdims=False)
-            value = held + across(sent, bit)
-            bit *= 2
-        return value[0]
-
-    mlp_out_w_grad = scatter(mlp_out_w_grad)
-    mlp_in_w_grad = scatter(mlp_in_w_grad)
-    cross_out_w_grad = scatter(cross_out_w_grad)
-    cross_q_w_grad = scatter(cross_q_w_grad)
-    cross_kv_w_grad = scatter(cross_kv_w_grad)
-    self_out_w_grad = scatter(self_out_w_grad)
-    self_qkv_w_grad = scatter(self_qkv_w_grad)
-
-    def total(value):
-        bit = 1
-        while bit < dp_size:
-            value = value + across(value, bit)
-            bit *= 2
-        return value
-
-    shared = jnp.concatenate(
-        [sums[3:5], 0.5 * sums[0:3], 0.5 * gain_three, 0.5 * shift_three, 0.5 * cross_out_b_grad, 0.5 * mlp_out_b_grad],
-        axis=0,
-    )
+    back = swap(both_send)
+    tokens_grad = (tok_keep + back[:, :own_width]).astype(BF16)
+    output = (out_keep + back[:, own_width:]).astype(BF16)
+    neighbours_grad = (store_keep + store_back).astype(BF16)
+
+    first_came = across(first[1], bits[2])
+    third_came = across(third[1], bits[1])
+    fourth = core_halve(sorted_halves(*self_halves), (first_came, third_came, store_back))
+    first = merge(first[0], first_came)
+    third = merge(third[0], third_came)
+    sums, *first = lax.optimization_barrier((sums, *first, fourth[1]))[:3]
+
+    def finish(parts, order):
+        for bit in order[:-1]:
+            parts = halve(*parts, bit)
+        return parts[0] + across(parts[1], order[-1])
+
+    mlp_grads = finish(first, bits[3:])
+    third = finish(third, bits[2:])
+    self_grads = finish(fourth, bits[1:])
+    cross_grads = third[:, : 4 * local]
+    mlp_out_w_grad = mlp_grads[:, :hidden]
+    mlp_in_w_grad = jnp.concatenate([mlp_grads[:, hidden:], third[:, 4 * local :]], axis=1)
+
+    bit = 1
+    while bit < dp_size:
+        sums = sums + across(sums, bit)
+        bit *= 2
+    shared = 0.5 * sums[2:9]
+    shared = jnp.concatenate([sums[0:2], shared], axis=0)
     shared = shared + swap(shared)
-    alone = jnp.concatenate(
-        [self_qkv_b_grad, cross_q_b_grad, cross_v_b_grad, mlp_in_b_grad], axis=1
-    )
-    alone_size = alone.shape[1]
-    alone_rows = -(-alone_size // width)
-    alone = jnp.pad(alone, ((0, 0), (0, alone_rows * width - alone_size))).reshape(alone_rows, width)
-    summed = total(jnp.concatenate([shared, alone], axis=0))
-    alone = summed[9:].reshape(-1)
-    norm_gain_grad = jnp.stack([summed[0], summed[2], summed[5]])
-    norm_bias_grad = jnp.stack([summed[1], summed[3], summed[6]])
+    alone = sums[9:].reshape(-1)
     return (
         output,
         tokens_grad,
         neighbours_grad.reshape(stored, span, own_width),
-        norm_gain_grad,
-        norm_bias_grad,
-        self_qkv_w_grad.reshape(-1, 3, local),
+        jnp.stack([shared[0], shared[2], shared[5]]),
+        jnp.stack([shared[1], shared[3], shared[6]]),
+        self_grads[:, local:].reshape(-1, 3, local),
         alone[: 3 * local].reshape(3, local),
-        self_out_w_grad.T,
-        summed[4],
-        cross_q_w_grad,
+        self_grads[:, :local].T,
+        shared[4],
+        cross_grads[:, local : 2 * local],
         alone[3 * local : 4 * local],
-        cross_kv_w_grad.reshape(-1, 2, local),
+        cross_grads[:, 2 * local :].reshape(-1, 2, local),
         alone[4 * local : 5 * local],
-        cross_out_w_grad.T,
-        summed[7],
+        cross_grads[:, :local].T,
+        shared[7],
         mlp_in_w_grad,
         alone[5 * local : 5 * local + hidden],
         mlp_out_w_grad.T,
-        summed[8],
+        shared[8],
     )
 
 

time: 443 us -> 289 us (0.65)
  waiting for transfers between devices: 216 us -> 109 us
  Pallas kernels: 73.3 us -> 102 us
  matrix products: 36.7 us -> 9.07 us
  local copies, waits for them, and re-layouts: 37 us -> 17.6 us
  starting transfers between devices: 49.6 us -> 30.3 us
  other arithmetic: 26.9 us -> 18.4 us
    ppermute x35 -> x24, waiting for transfers between devices: 129 us -> 59.6 us  [across(): return lax.ppermute(value, 'dp', [(at, at ^ bit) for at in range(dp_size)])]
    ppermute x11 -> x10, waiting for transfers between devices: 86.6 us -> 49.1 us  [swap(): return lax.ppermute(value, 'tp', [(0, 1), (1, 0)])]
    dot_general x15 -> x0, matrix products: 28.7 us -> none  [tdot(): lax.dot_general(left, right, (((0,), (0,)), ((), ())), preferred_element_...]
    ppermute x35 -> x24, starting transfers between devices: 36.4 us -> 18.5 us  [across(): return lax.ppermute(value, 'dp', [(at, at ^ bit) for at in range(dp_size)])]
    pallas_call x4 -> x5, Pallas kernels: 59.6 us -> 77.5 us  [call(): pl.pallas_call(body, name=name, out_shape=outs, in_specs=scalars(len(smal...]
    squeeze x28 -> x0, local copies, waits for them, and re-layouts: 12.8 us -> none  [scatter(): sent = lax.dynamic_index_in_dim(value, 1 - mine, 1, keepdims=False)]
    pallas_call x0 -> x2, Pallas kernels: none -> 11.1 us  [add_sent(): pl.pallas_call(partial(add_halves, len(came), bool(joined), split), name=...]
    unnamed x117 -> x66, local copies, waits for them, and re-layouts: 9.76 us -> 6.93 us
  transfers between devices with their start and end apart: 46 -> 34, of which waited for: 23 -> 17; matrix products, arithmetic and copies ran while one was open for 20% -> 12% of each run, Pallas kernels for 17% -> 35%
where the time goes in v2:
time: 289 us; the launch traced here: 288 us
  waiting for transfers between devices  109 us (38%)
  Pallas kernels  102 us (35%)
  starting transfers between devices  30.3 us (10%)
  other arithmetic  18.4 us (6%)
  local copies, waits for them, and re-layouts  17.6 us (6%)
  matrix products  9.07 us (3%)
    pallas_call x5, Pallas kernels, call(): pl.pallas_call(body, name=name, out_shape=outs, in_specs=scalars(len(smal...  77.5 us
    ppermute x24, waiting for transfers between devices, across(): return lax.ppermute(value, 'dp', [(at, at ^ bit) for at in range(dp_size)])  59.6 us
    ppermute x10, waiting for transfers between devices, swap(): return lax.ppermute(value, 'tp', [(0, 1), (1, 0)])  49.1 us
    ppermute x24, starting transfers between devices, across(): return lax.ppermute(value, 'dp', [(at, at ^ bit) for at in range(dp_size)])  18.5 us
    pallas_call x1, Pallas kernels, per_device(): pl.pallas_call(feed_forward, name='feed_forward', grid=(count // step,),...  13.7 us
    ppermute x10, starting transfers between devices, swap(): return lax.ppermute(value, 'tp', [(0, 1), (1, 0)])  11.8 us
    pallas_call x2, Pallas kernels, add_sent(): pl.pallas_call(partial(add_halves, len(came), bool(joined), split), name=...  11.1 us
    add x7, other arithmetic, merge(): return (kept[:half] + arrived[:half], kept[half:] + arrived[half:])  9.82 us
  transfers between devices with their start and end apart: 34, of which 17 were waited for; matrix products, arithmetic and copies ran while one was open for 12% of the time, Pallas kernels for 35%

profile of v2, /device:TPU:0, one launch (start us, length us, event | category | flops | bytes accessed | tf_op | source)
XLA Modules:
  0.0 288.1 jit_solution(14138272825730513038)
XLA Ops:
  0.7 1.0 dynamic-slice_convert_fusion.1
  1.7 3.1 %collective-permute-start.1 = (f32[192,768]{1,0:T(8,128)S(1)}, f32[192,768]{1,0:T(8,128)}, u32[]{:S(2)}, u32[]{:S(2)}) collective-permute-start(f32[192,768]{1,0:T(8,128)S(1)} %dynamic-slice_convert_fusion.1), channel_id=1, source_target_pairs={{0,1},{1,0},{2,3},{3,2},{4,5},{5,4},{6,7},{7,6},{8,9},{9,8},{10,11... | collective-permute-start | bytes 1769480 | tf_op jit(solution)/shard_map/ppermute | solution.py:584
  5.7 1.8 multiply_sine_fusion
  7.5 1.2 concatenate.18.info
  8.7 10.5 %self_forward.1 = (bf16[512,768]{1,0:T(8,128)(2,1)}, bf16[9,512,128]{2,1,0:T(8,128)(2,1)}, f32[512,384]{1,0:T(8,128)}, f32[512,128]{1,0:T(8,128)}, f32[512,512]{1,0:T(8,128)}) custom-call(s32[8]{0:T(128)} %concatenate.18.info, bf16[512,768]{1,0:T(8,128)(2,1)} %tok.5, bf16[3,768,384]{2,1,0:T(8,128)(2,1)} %bitcast.39, f32[3,384]{1,0:T(4,128)} %bias.1, ...), custom_call_target="tpu_custom_call" | custom-call | flops 11000000512 | bytes 1 | tf_op jit(solution)/shard_map/self_forward/pallas_call | solution.py:536
  22.0 1.5 copy-done.26
  23.5 2.6 fusion.kv
  26.2 12.5 %collective-permute-done.mix_peer = f32[512,384]{1,0:T(8,128)} collective-permute-done((f32[512,384]{1,0:T(8,128)}, f32[512,384]{1,0:T(8,128)}, u32[]{:S(2)}, u32[]{:S(2)}) %collective-permute-start) | collective-permute-done | bytes 786464 | tf_op jit(solution)/shard_map/ppermute | solution.py:584
  38.9 0.9 copy-done.30
  39.8 13.8 %cross_forward.1 = (f32[512,768]{1,0:T(8,128)}, bf16[512,768]{1,0:T(8,128)(2,1)}, bf16[512,384]{1,0:T(8,128)(2,1)}, f32[512,384]{1,0:T(8,128)}, f32[512,128]{1,0:T(8,128)}) custom-call(s32[8]{0:T(128)} %concatenate.18.info, s32[8,2]{1,0:T(8,128)} %copy.49.picks, bf16[512,768]{1,0:T(8,128)(2,1)} %tok.5, f32[512,384]{1,0:T(8,128)} %get-tuple-element.74.mix_own.mix, ...), custom_call_target="tpu_custom_call" | custom-call | flops 14000000000 | bytes 1 | tf_op jit(solution)/shard_map/cross_forward/pallas_call | solution.py:536
  53.6 1.7 collective-permute-start.3
  57.5 14.4 %collective-permute-done.3.mix_peer = f32[512,384]{1,0:T(8,128)S(1)} collective-permute-done((f32[512,384]{1,0:T(8,128)}, f32[512,384]{1,0:T(8,128)S(1)}, u32[]{:S(2)}, u32[]{:S(2)}) %collective-permute-start.3) | collective-permute-done | bytes 786464 | tf_op jit(solution)/shard_map/ppermute | solution.py:584
  71.9 1.5 collective-permute-start.7
  73.4 13.7 %feed_forward.1 = (f32[512,768]{1,0:T(8,128)}, bf16[512,768]{1,0:T(8,128)(2,1)}, bf16[512,1536]{1,0:T(8,128)(2,1)}, bf16[512,1536]{1,0:T(8,128)(2,1)}, f32[512,3...) custom-call(s32[8]{0:T(128)} %concatenate.18.info, ...), custom_call_target="tpu_custom_call" | custom-call | flops 14000000000 | bytes 1 | tf_op jit(solution)/shard_map/feed_forward/pallas_call | solution.py:733
  87.0 0.9 collective-permute-start.6
  87.9 9.3 %mlp_grads.1 = (f32[384,3072]{1,0:T(8,128)}, f32[384,768]{1,0:T(8,128)}, f32[384,768]{1,0:T(8,128)}, f32[384,768]{1,0:T(8,128)}, f32[384,768]{1,0:T(8,128)}) custom-call(s32[8]{0:T(128)} %concatenate.18.info, bf16[512,768]{1,0:T(8,128)(2,1)} %out_grad.1, bf16[512,768]{1,0:T(8,128)(2,1)} %get-tuple-element.83.refs_1_, ...), custom_call_target="tpu_custom_call" | custom-call | bytes 1 | tf_op jit(solution)/shard_map/mlp_grads/pallas_call | solution.py:536
  98.3 2.0 collective-permute-done.10.refs_6_.refs_7_
  100.3 1.7 collective-permute-done.11.refs_8_.refs_9_
  102.0 1.7 collective-permute-done.8.refs_2_.refs_3_
  103.7 1.8 collective-permute-done.9.refs_4_.refs_5_
  105.5 6.1 %add_mlp.1 = (f32[192,2304]{1,0:T(8,128)}, f32[192,2304]{1,0:T(8,128)}, f32[192,768]{1,0:T(8,128)}, f32[192,768]{1,0:T(8,128)}) custom-call(f32[384,3072]{1,0:T(8,128)} %get-tuple-element.86.refs_0_.refs_1_, f32[384,3072]{1,0:T(8,128)} %get-tuple-element.86.refs_0_.refs_1_, f32[384,768]{1,0:T(8,128)} %copy-done.3, f32[384,768]{1,0:T(8,128)} %copy-done.3, ...), custom_call_target="tpu_custom_call" | custom-call | bytes 1 | tf_op jit(solution)/shard_map/add_mlp/pallas_call | solution.py:634
  111.6 1.6 collective-permute-start.16
  113.2 7.8 %collective-permute-done.6.part_peer = f32[512,768]{1,0:T(8,128)} collective-permute-done((f32[512,768]{1,0:T(8,128)}, f32[512,768]{1,0:T(8,128)}, u32[]{:S(2)}, u32[]{:S(2)}) %collective-permute-start.6) | collective-permute-done | bytes 1572896 | tf_op jit(solution)/shard_map/ppermute | solution.py:584
  121.0 21.9 %cross_backward.1 = (f32[512,768]{1,0:T(8,128)}, f32[512,384]{1,0:T(8,128)}, bf16[512,384]{1,0:T(8,128)(2,1)}, bf16[1024,768]{1,0:T(8,128)(2,1)}, f32[8,768]{1,0...) custom-call(s32[8]{0:T(128)} %concatenate.18.info, ...), custom_call_target="tpu_custom_call" | custom-call | flops 16999999488 | bytes 1 | tf_op jit(solution)/shard_map/cross_backward/pallas_call | solution.py:536
  143.5 1.1 collective-permute-start.12
  144.6 3.6 %fusion.6 = f32[1024,384]{1,0:T(8,128)} fusion(bf16[1024,768]{1,0:T(8,128)(2,1)} %get-tuple-element.118, s32[]{:T(128)S(6)} %select_n.40, bf16[768,384]{1,0:T(8,128)(2,1)S(1)} %copy-done.9, bf16[768,384]{1,0:T(8,128)(2,1)S(1)} %copy-done.11), kind=kOutput, calls=%fused_computation.21 | convolution fusion | flops 605159424 | bytes 4325380 | tf_op jit(solution)/shard_map/dot_general | solution.py:24
  148.2 1.0 copy-done.5
  149.6 5.0 %add_cross.1 = (f32[192,2304]{1,0:T(8,128)}, f32[192,2304]{1,0:T(8,128)}) custom-call(f32[384,1536]{1,0:T(8,128)} %get-tuple-element.99.refs_0_.refs_1_, f32[384,1536]{1,0:T(8,128)} %get-tuple-element.99.refs_0_.refs_1_, f32[384,768]{1,0:T(8,128)} %copy-done.5, f32[384,768]{1,0:T(8,128)} %copy-done.5, f32[384,768]{1,0:T(8,128)} %copy-done.6, ...), custom_call_target="tpu_custom_call" | custom-call | bytes 1 | tf_op jit(solution)/shard_map/add_cross/pallas_call | solution.py:634
  154.6 1.5 collective-permute-start.20
  156.1 0.9 collective-permute-start.18
  157.0 3.1 %slice_add_fusion.4 = (f32[96,2304]{1,0:T(8,128)S(1)}, f32[96,2304]{1,0:T(8,128)}) fusion(f32[192,2304]{1,0:T(8,128)} %collective-permute-done.16, f32[192,2304]{1,0:T(8,128)} %get-tuple-element.105), kind=kLoop, calls=%fused_computation.13 | loop fusion | flops 442368 | bytes 5308416 | tf_op jit(solution)/shard_map/add | solution.py:666
  160.2 1.6 collective-permute-start.19
  161.7 2.5 collective-permute-done.12.query_peer
  164.3 22.0 %self_backward.1 = (f32[512,384]{1,0:T(8,128)}, f32[512,768]{1,0:T(8,128)}, f32[16,768]{1,0:T(8,128)}, f32[384,1536]{1,0:T(8,128)}, f32[384,768]{1,0:T(8,128)}, /*index=5*/f32[384,768]{1,0:T(8,128)}) custom-call(s32[8]{0:T(128)} %concatenate.18.info, bf16[512,384]{1,0:T(8,128)(2,1)} %get-tuple-element.96.query_own, ...), custom_call_target="tpu_custom_call" | custom-call | flops 40000000000 | bytes 1 | tf_op jit(solution)/shard_map/self_backward/pallas_call | solution.py:536
  186.8 1.0 slice_add_fusion.12
  187.9 9.5 %collective-permute-done.18 = f32[1024,384]{1,0:T(8,128)S(1)} collective-permute-done((f32[1024,384]{1,0:T(8,128)}, f32[1024,384]{1,0:T(8,128)S(1)}, u32[]{:S(2)}, u32[]{:S(2)}) %collective-permute-start.18) | collective-permute-done | bytes 1572896 | tf_op jit(solution)/shard_map/ppermute | solution.py:584
  197.6 1.5 copy-done.7
  199.2 1.8 slice_add_fusion
  201.0 1.2 collective-permute-done.23
  202.2 1.5 collective-permute-start.24
  203.8 1.1 collective-permute-start.17
  204.9 1.5 collective-permute-done.24
  206.4 1.6 collective-permute-start.25
  208.0 2.9 %add_convert_fusion.1 = bf16[1024,384]{1,0:T(8,128)(2,1)} fusion(f32[1024,384]{1,0:T(8,128)S(1)} %collective-permute-done.18, bf16[1024,768]{1,0:T(8,128)(2,1)S(1)} %copy-done, s32[]{:T(128)S(6)} %select_n.39, bf16[768,384]{1,0:T(8,128)(2,1)} %copy-done.8, bf16[768,384]{1,0:T(8,128)(2,1)} %copy-done.10), kind=kOutput, calls=%fused_computation.1 | convolution fusion | flops 605945856 | bytes 5111812 | tf_op jit(solution)/shard_map/dot_general | solution.py:24
  211.0 1.5 collective-permute-start.28
  212.4 2.6 collective-permute-start.33
  215.4 2.6 slice_add_fusion.3
  218.5 17.2 %collective-permute-done.26 = f32[16,768]{1,0:T(8,128)S(1)} collective-permute-done((f32[16,768]{1,0:T(8,128)S(1)}, f32[16,768]{1,0:T(8,128)S(1)}, u32[]{:S(2)}, u32[]{:S(2)}) %collective-permute-start.26) | collective-permute-done | bytes 49184 | tf_op jit(solution)/shard_map/ppermute | solution.py:587
  235.7 1.2 collective-permute-start.27
  238.7 2.4 collective-permute-done.27
  242.4 2.9 %fusion.1 = (bf16[512,384]{1,0:T(8,128)(2,1)}, bf16[512,384]{1,0:T(8,128)(2,1)}) fusion(f32[512,384]{1,0:T(8,128)} %get-tuple-element.117, f32[512,768]{1,0:T(8,128)} %collective-permute-done.17, f32[512,384]{1,0:T(8,128)} %get-tuple-element.78), kind=kLoop, calls=%fused_computation.16 | loop fusion | flops 786432 | bytes 3932160 | tf_op jit(solution)/shard_map/convert_element_type | solution.py:901
  245.4 0.7 slice_bitcast_fusion.2
  246.1 2.0 collective-permute-done.31
  248.1 1.1 slice_add_fusion.10
  249.2 0.7 collective-permute-start.32
  250.1 1.8 collective-permute-start.29
  251.8 17.1 %collective-permute-done.32 = f32[48,2304]{1,0:T(8,128)S(1)} collective-permute-done((f32[48,2304]{1,0:T(8,128)S(1)}, f32[48,2304]{1,0:T(8,128)S(1)}, u32[]{:S(2)}, u32[]{:S(2)}) %collective-permute-start.32) | collective-permute-done | bytes 442400 | tf_op jit(solution)/shard_map/ppermute | solution.py:587
  268.9 1.1 fusion.8
  270.0 2.5 collective-permute-done.29
  272.6 1.1 collective-permute-start.30
  274.3 0.7 reshape.108
  275.1 0.7 pad_maximum_fusion.2
  275.8 10.9 %collective-permute-done.30 = f32[48,1536]{1,0:T(8,128)S(1)} collective-permute-done((f32[48,1536]{1,0:T(8,128)S(1)}, f32[48,1536]{1,0:T(8,128)S(1)}, u32[]{:S(2)}, u32[]{:S(2)}) %collective-permute-start.30) | collective-permute-done | bytes 294944 | tf_op jit(solution)/shard_map/ppermute | solution.py:587
  287.4 0.7 copy.59
  (135 shorter events, 14.0 us)
Async XLA Ops:
  1.7 20.1 %collective-permute-start.1 = (f32[192,768]{1,0:T(8,128)S(1)}, f32[192,768]{1,0:T(8,128)}, u32[]{:S(2)}, u32[]{:S(2)}) collective-permute-start(f32[192,768]{1,0:T(8,128)S(1)} %dynamic-slice_convert_fusion.1), channel_id=1, source_target_pairs={{0,1},{1,0},{2,3},{3,2},{4,5},{5,4},{6,7},{7,6},{8,9},{9,8},{10,11... | collective-permute-start | bytes 1769480 | tf_op jit(solution)/shard_map/ppermute | solution.py:584
  8.7 10.6 %copy-start.15 = (bf16[768,2,384]{2,1,0:T(2,128)(2,1)S(1)}, bf16[768,2,384]{2,1,0:T(2,128)(2,1)}, u32[]{:S(2)}) copy-start(bf16[768,2,384]{2,1,0:T(2,128)(2,1)} %param.36) | copy-start | bytes 3538948
  19.2 1.4 copy-start.20
  19.2 1.9 copy-start.23
  19.2 2.5 copy-start.24
  19.2 2.5 copy-start.17
  19.2 19.4 %collective-permute-start = (f32[512,384]{1,0:T(8,128)}, f32[512,384]{1,0:T(8,128)}, u32[]{:S(2)}, u32[]{:S(2)}) collective-permute-start(f32[512,384]{1,0:T(8,128)} %get-tuple-element.74.mix_own.mix), channel_id=1, source_target_pairs={{0,1},{1,0},{2,3},{3,2},{4,5},{5,4},{6,7},{7,6},{8,9},{9,8},{10,11... | collective-permute-start | bytes 2359304 | tf_op jit(solution)/shard_map/ppermute | solution.py:584
  21.7 1.8 copy-start.26
  21.8 17.1 %collective-permute-start.2 = (f32[192,768]{1,0:T(8,128)}, f32[192,768]{1,0:T(8,128)S(1)}, u32[]{:S(2)}, u32[]{:S(2)}) collective-permute-start(f32[192,768]{1,0:T(8,128)} %collective-permute-done.1.w_near), channel_id=1, source_target_pairs={{0,2},{2,0},{4,6},{6,4},{8,10},{10,8},{12,14},{14,12},{16,18},{18,... | collective-permute-start | bytes 1769480 | tf_op jit(solution)/shard_map/ppermute | solution.py:587
  22.0 4.1 %copy-start.8 = (bf16[768,384]{1,0:T(8,128)(2,1)}, bf16[768,384]{1,0:T(8,128)(2,1)S(1)}, u32[]{:S(2)}) copy-start(bf16[768,384]{1,0:T(8,128)(2,1)S(1)} %get-tuple-element.182) | copy-start | bytes 1769476
  22.0 4.1 %copy-start.10 = (bf16[768,384]{1,0:T(8,128)(2,1)}, bf16[768,384]{1,0:T(8,128)(2,1)S(1)}, u32[]{:S(2)}) copy-start(bf16[768,384]{1,0:T(8,128)(2,1)S(1)} %get-tuple-element.183) | copy-start | bytes 1769476
  26.1 29.2 %copy-start.19 = (f32[1536]{0:T(1024)S(1)}, f32[1536]{0:T(1024)}, u32[]{:S(2)}) copy-start(f32[1536]{0:T(1024)} %param.41) | copy-start | bytes 18436
  26.1 29.9 %copy-start.21 = (f32[768]{0:T(1024)S(1)}, f32[768]{0:T(1024)}, u32[]{:S(2)}) copy-start(f32[768]{0:T(1024)} %param.39) | copy-start | bytes 9220
  26.1 30.4 %copy-start.22 = (f32[768]{0:T(1024)S(1)}, f32[768]{0:T(1024)}, u32[]{:S(2)}) copy-start(f32[768]{0:T(1024)} %param.43) | copy-start | bytes 9220
  26.1 31.0 %copy-start.16 = (bf16[768,384]{1,0:T(8,128)(2,1)S(1)}, bf16[768,384]{1,0:T(8,128)(2,1)}, u32[]{:S(2)}) copy-start(bf16[768,384]{1,0:T(8,128)(2,1)} %q_w.3) | copy-start | bytes 1769476
  38.6 16.7 %collective-permute-start.4 = (f32[192,768]{1,0:T(8,128)S(1)}, f32[192,768]{1,0:T(8,128)S(1)}, u32[]{:S(2)}, u32[]{:S(2)}) collective-permute-start(f32[192,768]{1,0:T(8,128)S(1)} %dynamic-slice_convert_fusion), channel_id=1, source_target_pairs={{0,1},{1,0},{2,3},{3,2},{4,5},{5,4},{6,7},{7,6},{8,9},{9,8},{10,11... | collective-permute-start | bytes 1769480 | tf_op jit(solution)/shard_map/ppermute | solution.py:584
  53.6 18.3 %collective-permute-start.3 = (f32[512,384]{1,0:T(8,128)}, f32[512,384]{1,0:T(8,128)S(1)}, u32[]{:S(2)}, u32[]{:S(2)}) collective-permute-start(f32[512,384]{1,0:T(8,128)} %get-tuple-element.76.mix_own.mix), channel_id=1, source_target_pairs={{0,1},{1,0},{2,3},{3,2},{4,5},{5,4},{6,7},{7,6},{8,9},{9,8},{10,11... | collective-permute-start | bytes 2359304 | tf_op jit(solution)/shard_map/ppermute | solution.py:584
  55.3 18.1 %copy-start.29 = (f32[192,768]{1,0:T(8,128)}, f32[192,768]{1,0:T(8,128)S(1)}, u32[]{:S(2)}) copy-start(f32[192,768]{1,0:T(8,128)S(1)} %collective-permute-done.4.w_near) | copy-start | bytes 1769476
  55.3 18.1 %collective-permute-start.5 = (f32[192,768]{1,0:T(8,128)S(1)}, f32[192,768]{1,0:T(8,128)}, u32[]{:S(2)}, u32[]{:S(2)}) collective-permute-start(f32[192,768]{1,0:T(8,128)S(1)} %collective-permute-done.4.w_near), channel_id=1, source_target_pairs={{0,2},{2,0},{4,6},{6,4},{8,10},{10,8},{12,14},{14,12},{16,18},{18,... | collective-permute-start | bytes 1769480 | tf_op jit(solution)/shard_map/ppermute | solution.py:587
  71.9 1.5 copy-start.27
  71.9 16.0 %collective-permute-start.7 = (f32[192,768]{1,0:T(8,128)S(1)}, f32[192,768]{1,0:T(8,128)S(1)}, u32[]{:S(2)}, u32[]{:S(2)}) collective-permute-start(f32[192,768]{1,0:T(8,128)S(1)} %convert_bitcast_fusion), channel_id=1, source_target_pairs={{0,1},{1,0},{2,3},{3,2},{4,5},{5,4},{6,7},{7,6},{8,9},{9,8},{10,11... | collective-permute-start | bytes 1769480 | tf_op jit(solution)/shard_map/ppermute | solution.py:584
  87.0 34.0 %collective-permute-start.6 = (f32[512,768]{1,0:T(8,128)}, f32[512,768]{1,0:T(8,128)}, u32[]{:S(2)}, u32[]{:S(2)}) collective-permute-start(f32[512,768]{1,0:T(8,128)} %get-tuple-element.79.part_own), channel_id=1, source_target_pairs={{0,1},{1,0},{2,3},{3,2},{4,5},{5,4},{6,7},{7,6},{8,9},{9,8},{10,11... | collective-permute-start | bytes 4718600 | tf_op jit(solution)/shard_map/ppermute | solution.py:584
  87.9 9.4 %copy-start.28 = (f32[192,768]{1,0:T(8,128)}, f32[192,768]{1,0:T(8,128)S(1)}, u32[]{:S(2)}) copy-start(f32[192,768]{1,0:T(8,128)S(1)} %collective-permute-done.7.q_near) | copy-start | bytes 1769476
  97.3 3.1 %collective-permute-start.10 = (f32[384,768]{1,0:T(8,128)}, f32[384,768]{1,0:T(8,128)S(1)}, u32[]{:S(2)}, u32[]{:S(2)}) collective-permute-start(f32[384,768]{1,0:T(8,128)} %get-tuple-element.89), channel_id=1, source_target_pairs={{0,2},{2,0},{4,6},{6,4},{8,10},{10,8},{12,14},{14,12},{16,18},{18,... | collective-permute-start | bytes 3538952 | tf_op jit(solution)/shard_map/ppermute | solution.py:587
  97.3 4.7 %collective-permute-start.11 = (f32[384,768]{1,0:T(8,128)}, f32[384,768]{1,0:T(8,128)S(1)}, u32[]{:S(2)}, u32[]{:S(2)}) collective-permute-start(f32[384,768]{1,0:T(8,128)} %get-tuple-element.90), channel_id=1, source_target_pairs={{0,2},{2,0},{4,6},{6,4},{8,10},{10,8},{12,14},{14,12},{16,18},{18,... | collective-permute-start | bytes 3538952 | tf_op jit(solution)/shard_map/ppermute | solution.py:587
  97.8 5.9 %collective-permute-start.8 = (f32[384,768]{1,0:T(8,128)}, f32[384,768]{1,0:T(8,128)S(1)}, u32[]{:S(2)}, u32[]{:S(2)}) collective-permute-start(f32[384,768]{1,0:T(8,128)} %get-tuple-element.87), channel_id=1, source_target_pairs={{0,2},{2,0},{4,6},{6,4},{8,10},{10,8},{12,14},{14,12},{16,18},{18,... | collective-permute-start | bytes 3538952 | tf_op jit(solution)/shard_map/ppermute | solution.py:587
  97.9 7.7 %collective-permute-start.9 = (f32[384,768]{1,0:T(8,128)}, f32[384,768]{1,0:T(8,128)}, u32[]{:S(2)}, u32[]{:S(2)}) collective-permute-start(f32[384,768]{1,0:T(8,128)} %get-tuple-element.88), channel_id=1, source_target_pairs={{0,2},{2,0},{4,6},{6,4},{8,10},{10,8},{12,14},{14,12},{16,18},{18,... | collective-permute-start | bytes 3538952 | tf_op jit(solution)/shard_map/ppermute | solution.py:587
  100.3 5.2 %copy-start.1 = (f32[384,768]{1,0:T(8,128)}, f32[384,768]{1,0:T(8,128)S(1)}, u32[]{:S(2)}) copy-start(f32[384,768]{1,0:T(8,128)S(1)} %collective-permute-done.10.refs_6_.refs_7_) | copy-start | bytes 3538948
  102.0 3.5 %copy-start.2 = (f32[384,768]{1,0:T(8,128)}, f32[384,768]{1,0:T(8,128)S(1)}, u32[]{:S(2)}) copy-start(f32[384,768]{1,0:T(8,128)S(1)} %collective-permute-done.11.refs_8_.refs_9_) | copy-start | bytes 3538948
  103.7 1.8 copy-start.3
  111.6 45.4 %collective-permute-start.16 = (f32[192,2304]{1,0:T(8,128)}, f32[192,2304]{1,0:T(8,128)}, u32[]{:S(2)}, u32[]{:S(2)}) collective-permute-start(f32[192,2304]{1,0:T(8,128)} %get-tuple-element.91), channel_id=1, source_target_pairs={{0,4},{2,6},{4,0},{6,2},{8,12},{10,14},{12,8},{14,10},{16,20},{18,... | collective-permute-start | bytes 5308424 | tf_op jit(solution)/shard_map/ppermute | solution.py:587
  121.0 23.6 %copy-start.9 = (bf16[768,384]{1,0:T(8,128)(2,1)S(1)}, bf16[768,384]{1,0:T(8,128)(2,1)}, u32[]{:S(2)}) copy-start(bf16[768,384]{1,0:T(8,128)(2,1)} %copy-done.8) | copy-start | bytes 1769476
  121.0 23.6 %copy-start.11 = (bf16[768,384]{1,0:T(8,128)(2,1)S(1)}, bf16[768,384]{1,0:T(8,128)(2,1)}, u32[]{:S(2)}) copy-start(bf16[768,384]{1,0:T(8,128)(2,1)} %copy-done.10) | copy-start | bytes 1769476
  143.0 5.2 %collective-permute-start.14 = (f32[384,768]{1,0:T(8,128)}, f32[384,768]{1,0:T(8,128)S(1)}, u32[]{:S(2)}, u32[]{:S(2)}) collective-permute-start(f32[384,768]{1,0:T(8,128)} %get-tuple-element.100), channel_id=1, source_target_pairs={{0,2},{2,0},{4,6},{6,4},{8,10},{10,8},{12,14},{14,12},{16,18},{18,... | collective-permute-start | bytes 3538952 | tf_op jit(solution)/shard_map/ppermute | solution.py:587
  143.0 5.2 %collective-permute-start.15 = (f32[384,768]{1,0:T(8,128)}, f32[384,768]{1,0:T(8,128)S(1)}, u32[]{:S(2)}, u32[]{:S(2)}) collective-permute-start(f32[384,768]{1,0:T(8,128)} %get-tuple-element.101), channel_id=1, source_target_pairs={{0,2},{2,0},{4,6},{6,4},{8,10},{10,8},{12,14},{14,12},{16,18},{18,... | collective-permute-start | bytes 3538952 | tf_op jit(solution)/shard_map/ppermute | solution.py:587
  143.5 18.3 %collective-permute-start.13 = (f32[192,768]{1,0:T(8,128)}, f32[192,768]{1,0:T(8,128)}, u32[]{:S(2)}, u32[]{:S(2)}) collective-permute-start(f32[192,768]{1,0:T(8,128)} %copy-done.28), channel_id=1, source_target_pairs={{0,2},{2,0},{4,6},{6,4},{8,10},{10,8},{12,14},{14,12},{16,18},{18,... | collective-permute-start | bytes 1769480 | tf_op jit(solution)/shard_map/ppermute | solution.py:587
  143.5 20.7 %collective-permute-start.12 = (f32[512,384]{1,0:T(8,128)}, f32[512,384]{1,0:T(8,128)}, u32[]{:S(2)}, u32[]{:S(2)}) collective-permute-start(f32[512,384]{1,0:T(8,128)} %get-tuple-element.97), channel_id=1, source_target_pairs={{0,1},{1,0},{2,3},{3,2},{4,5},{5,4},{6,7},{7,6},{8,9},{9,8},{10,11... | collective-permute-start | bytes 2359304 | tf_op jit(solution)/shard_map/ppermute | solution.py:584
  148.2 1.0 copy-start.5
  148.2 1.4 copy-start.6
  154.6 42.7 %collective-permute-start.20 = (f32[192,2304]{1,0:T(8,128)}, f32[192,2304]{1,0:T(8,128)}, u32[]{:S(2)}, u32[]{:S(2)}) collective-permute-start(f32[192,2304]{1,0:T(8,128)} %get-tuple-element.104), channel_id=1, source_target_pairs={{0,4},{2,6},{4,0},{6,2},{8,12},{10,14},{12,8},{14,10},{16,20},{18,... | collective-permute-start | bytes 5308424 | tf_op jit(solution)/shard_map/ppermute | solution.py:587
  156.1 41.2 %collective-permute-start.18 = (f32[1024,384]{1,0:T(8,128)}, f32[1024,384]{1,0:T(8,128)S(1)}, u32[]{:S(2)}, u32[]{:S(2)}) collective-permute-start(f32[1024,384]{1,0:T(8,128)} %fusion.6), channel_id=1, source_target_pairs={{0,1},{1,0},{2,3},{3,2},{4,5},{5,4},{6,7},{7,6},{8,9},{9,8},{10,11... | collective-permute-start | bytes 4718600 | tf_op jit(solution)/shard_map/ppermute | solution.py:584
  160.2 26.7 %collective-permute-start.19 = (f32[96,2304]{1,0:T(8,128)}, f32[96,2304]{1,0:T(8,128)S(1)}, u32[]{:S(2)}, u32[]{:S(2)}) collective-permute-start(f32[96,2304]{1,0:T(8,128)} %get-tuple-element.175), channel_id=1, source_target_pairs={{0,8},{2,10},{4,12},{6,14},{8,0},{10,2},{12,4},{14,6},{16,24},{18,... | collective-permute-start | bytes 2654216 | tf_op jit(solution)/shard_map/ppermute | solution.py:587
  186.3 11.1 %collective-permute-start.21 = (f32[384,768]{1,0:T(8,128)}, f32[384,768]{1,0:T(8,128)S(1)}, u32[]{:S(2)}, u32[]{:S(2)}) collective-permute-start(f32[384,768]{1,0:T(8,128)} %get-tuple-element.123), channel_id=1, source_target_pairs={{0,2},{2,0},{4,6},{6,4},{8,10},{10,8},{12,14},{14,12},{16,18},{18,... | collective-permute-start | bytes 3538952 | tf_op jit(solution)/shard_map/ppermute | solution.py:587
  186.3 11.2 %collective-permute-start.22 = (f32[384,768]{1,0:T(8,128)}, f32[384,768]{1,0:T(8,128)S(1)}, u32[]{:S(2)}, u32[]{:S(2)}) collective-permute-start(f32[384,768]{1,0:T(8,128)} %get-tuple-element.124), channel_id=1, source_target_pairs={{0,2},{2,0},{4,6},{6,4},{8,10},{10,8},{12,14},{14,12},{16,18},{18,... | collective-permute-start | bytes 3538952 | tf_op jit(solution)/shard_map/ppermute | solution.py:587
  197.5 1.7 copy-start.7
  199.2 1.8 copy-start.18
  199.2 8.9 %copy-start = (bf16[1024,768]{1,0:T(8,128)(2,1)S(1)}, bf16[1024,768]{1,0:T(8,128)(2,1)}, u32[]{:S(2)}) copy-start(bf16[1024,768]{1,0:T(8,128)(2,1)} %get-tuple-element.118) | copy-start | bytes 4718596
  201.0 1.2 collective-permute-start.23
  202.2 4.2 %collective-permute-start.24 = (f32[16,768]{1,0:T(8,128)S(1)}, f32[16,768]{1,0:T(8,128)S(1)}, u32[]{:S(2)}, u32[]{:S(2)}) collective-permute-start(f32[16,768]{1,0:T(8,128)S(1)} %add.127), channel_id=1, source_target_pairs={{0,4},{2,6},{4,0},{6,2},{8,12},{10,14},{12,8},{14,10},{16,20},{18,... | collective-permute-start | bytes 147464 | tf_op jit(solution)/shard_map/ppermute | solution.py:587
  203.8 38.7 %collective-permute-start.17 = (f32[512,768]{1,0:T(8,128)}, f32[512,768]{1,0:T(8,128)}, u32[]{:S(2)}, u32[]{:S(2)}) collective-permute-start(f32[512,768]{1,0:T(8,128)} %get-tuple-element.116), channel_id=1, source_target_pairs={{0,1},{1,0},{2,3},{3,2},{4,5},{5,4},{6,7},{7,6},{8,9},{9,8},{10,11... | collective-permute-start | bytes 4718600 | tf_op jit(solution)/shard_map/ppermute | solution.py:584
  206.4 9.1 %copy-start.13 = (f32[192,2304]{1,0:T(8,128)S(1)}, f32[192,2304]{1,0:T(8,128)}, u32[]{:S(2)}) copy-start(f32[192,2304]{1,0:T(8,128)} %get-tuple-element.126) | copy-start | bytes 5308420
  206.4 8.7 %collective-permute-start.25 = (f32[16,768]{1,0:T(8,128)S(1)}, f32[16,768]{1,0:T(8,128)S(1)}, u32[]{:S(2)}, u32[]{:S(2)}) collective-permute-start(f32[16,768]{1,0:T(8,128)S(1)} %add.128), channel_id=1, source_target_pairs={{0,8},{2,10},{4,12},{6,14},{8,0},{10,2},{12,4},{14,6},{16,24},{18,... | collective-permute-start | bytes 147464 | tf_op jit(solution)/shard_map/ppermute | solution.py:587
  211.0 38.9 %collective-permute-start.28 = (f32[192,1536]{1,0:T(8,128)}, f32[192,1536]{1,0:T(8,128)S(1)}, u32[]{:S(2)}, u32[]{:S(2)}) collective-permute-start(f32[192,1536]{1,0:T(8,128)} %get-tuple-element.171), channel_id=1, source_target_pairs={{0,4},{2,6},{4,0},{6,2},{8,12},{10,14},{12,8},{14,10},{16,20},{18,... | collective-permute-start | bytes 3538952 | tf_op jit(solution)/shard_map/ppermute | solution.py:587
  212.4 32.9 %collective-permute-start.33 = (f32[48,2304]{1,0:T(8,128)}, f32[48,2304]{1,0:T(8,128)S(1)}, u32[]{:S(2)}, u32[]{:S(2)}) collective-permute-start(f32[48,2304]{1,0:T(8,128)} %get-tuple-element.128), channel_id=1, source_target_pairs={{0,16},{2,18},{4,20},{6,22},{8,24},{10,26},{12,28},{14,30},{16,0},... | collective-permute-start | bytes 1327112 | tf_op jit(solution)/shard_map/ppermute | solution.py:587
  215.1 20.6 %collective-permute-start.26 = (f32[16,768]{1,0:T(8,128)S(1)}, f32[16,768]{1,0:T(8,128)S(1)}, u32[]{:S(2)}, u32[]{:S(2)}) collective-permute-start(f32[16,768]{1,0:T(8,128)S(1)} %add.129), channel_id=1, source_target_pairs={{0,16},{2,18},{4,20},{6,22},{8,24},{10,26},{12,28},{14,30},{16,0},... | collective-permute-start | bytes 147464 | tf_op jit(solution)/shard_map/ppermute | solution.py:587
  218.0 30.1 %collective-permute-start.31 = (f32[96,2304]{1,0:T(8,128)}, f32[96,2304]{1,0:T(8,128)}, u32[]{:S(2)}, u32[]{:S(2)}) collective-permute-start(f32[96,2304]{1,0:T(8,128)} %get-tuple-element.173), channel_id=1, source_target_pairs={{0,8},{2,10},{4,12},{6,14},{8,0},{10,2},{12,4},{14,6},{16,24},{18,... | collective-permute-start | bytes 2654216 | tf_op jit(solution)/shard_map/ppermute | solution.py:587
  235.7 5.4 %collective-permute-start.27 = (f32[9,768]{1,0:T(8,128)S(1)}, f32[9,768]{1,0:T(8,128)S(1)}, u32[]{:S(2)}, u32[]{:S(2)}) collective-permute-start(f32[9,768]{1,0:T(8,128)S(1)} %pad_maximum_fusion.3), channel_id=1, source_target_pairs={{0,1},{1,0},{2,3},{3,2},{4,5},{5,4},{6,7},{7,6},{8,9},{9,8},{10,11... | collective-permute-start | bytes 82952 | tf_op jit(solution)/shard_map/ppermute | solution.py:584
  242.4 2.9 %copy-start.14 = (f32[48,2304]{1,0:T(8,128)S(1)}, f32[48,2304]{1,0:T(8,128)}, u32[]{:S(2)}) copy-start(f32[48,2304]{1,0:T(8,128)} %get-tuple-element.127) | copy-start | bytes 1327108
  245.3 4.5 %copy-start.4 = (f32[192,1536]{1,0:T(8,128)S(1)}, f32[192,1536]{1,0:T(8,128)}, u32[]{:S(2)}) copy-start(f32[192,1536]{1,0:T(8,128)} %get-tuple-element.170) | copy-start | bytes 3538948
  245.4 4.7 %copy-start.12 = (f32[48,2304]{1,0:T(8,128)}, f32[48,2304]{1,0:T(8,128)S(1)}, u32[]{:S(2)}) copy-start(f32[48,2304]{1,0:T(8,128)S(1)} %add.143) | copy-start | bytes 1327108
  249.2 19.7 %collective-permute-start.32 = (f32[48,2304]{1,0:T(8,128)S(1)}, f32[48,2304]{1,0:T(8,128)S(1)}, u32[]{:S(2)}, u32[]{:S(2)}) collective-permute-start(f32[48,2304]{1,0:T(8,128)S(1)} %slice_add_fusion.10), channel_id=1, source_target_pairs={{0,16},{2,18},{4,20},{6,22},{8,24},{10,26},{12,28},{14,30},{16,0},... | collective-permute-start | bytes 1327112 | tf_op jit(solution)/shard_map/ppermute | solution.py:587
  250.1 25.0 %slice-start = ((f32[48,2304]{1,0:T(8,128)}), f32[48,768]{1,0:T(8,128)S(1)}, s32[]{:S(2)}) async-start(f32[48,2304]{1,0:T(8,128)} %copy-done.12), calls=%async_computation | async-start | bytes 294912 | tf_op jit(solution)/shard_map/slice | solution.py:922
  250.1 22.5 %collective-permute-start.29 = (f32[96,1536]{1,0:T(8,128)S(1)}, f32[96,1536]{1,0:T(8,128)S(1)}, u32[]{:S(2)}, u32[]{:S(2)}) collective-permute-start(f32[96,1536]{1,0:T(8,128)S(1)} %get-tuple-element.177), channel_id=1, source_target_pairs={{0,8},{2,10},{4,12},{6,14},{8,0},{10,2},{12,4},{14,6},{16,24},{18,... | collective-permute-start | bytes 1769480 | tf_op jit(solution)/shard_map/ppermute | solution.py:587
  272.6 14.1 %collective-permute-start.30 = (f32[48,1536]{1,0:T(8,128)S(1)}, f32[48,1536]{1,0:T(8,128)S(1)}, u32[]{:S(2)}, u32[]{:S(2)}) collective-permute-start(f32[48,1536]{1,0:T(8,128)S(1)} %slice_add_fusion.14), channel_id=1, source_target_pairs={{0,16},{2,18},{4,20},{6,22},{8,24},{10,26},{12,28},{14,30},{16,0},... | collective-permute-start | bytes 884744 | tf_op jit(solution)/shard_map/ppermute | solution.py:587
  (2 other events, 1.6 us)

commit v3 on v2

--- a/solution.py
+++ b/solution.py
@@ -14,6 +14,7 @@
 F32 = jnp.float32
 BF16 = jnp.bfloat16
 TILE = 128
+RIDE = 8
 
 
 def dot(left, right):
@@ -340,8 +341,8 @@
 def self_backward(
     slots, order, info, query_own, query_peer, q_w, q_near, q_far, hidden, grad_two, gains, out_w, qkv, lse, mask, cosine, sine, w,
     tok, cross_sums, q_bias, v_bias, in_bias, out_send, mix, ln,
-    keep_out, send_out, sums_out, grads_keep, grads_one, grads_two,
-    q_peer, one, mix_grad, key_grad, value_grad, part, low_out, qkv_out, turned, ordered,
+    keep_out, send_out, grads_keep, grads_one, grads_two,
+    q_peer, one, mix_grad, key_grad, value_grad, part, low_out, qkv_out, turned, ordered, sums_out,
 ):
     count = tok.shape[0]
     local = out_w.shape[0]
@@ -444,8 +445,13 @@
         return carry
 
     lax.fori_loop(0, count // step, finish, 0)
-    terms = ((low_out, mix), (ln, qkv_out))
+    terms = ((low_out, mix), (ln, qkv_out.at[:pairs]), (ln, qkv_out.at[pairs:]))
     fill_grads(order, info[3 + slots], terms, grads_keep, (grads_one, grads_two), turned, ordered)
+    rows, wide = ordered.shape[0] // 2, sums_out.shape[1]
+    grads_keep[rows:, :wide] = sums_out[0:RIDE, :]
+    grads_keep[rows:, wide:] = sums_out[RIDE:, :]
+    grads_one[rows:, :] = sums_out[0:RIDE, :]
+    grads_two[rows:, :] = sums_out[RIDE:, :]
 
 
 def slice_at(place, order):
@@ -453,21 +459,23 @@
     return sum(bit * ((place >> (last - at)) & 1) for at, bit in enumerate(order))
 
 
-def fill_grads(order, me, terms, keep_out, send_outs, turned, ordered):
+def fill_grads(orders, me, terms, keep_out, send_outs, turned, ordered):
     width = turned.shape[0]
     half = width // 2
     share = send_outs[0].shape[1]
     column = 0
-    for left, right in terms:
+    for at_term, (left, right) in enumerate(terms):
         count = left.shape[0]
-        if order is None:
+        if orders is None:
             ordered[:, :count] = left[...].T
         else:
+            order = orders[at_term % len(orders)]
             parts = 1 << len(order)
             slab = width // parts
-            turned[:, :count] = left[...].T
-
-            def move(place, carry, count=count):
+            if at_term == 0 or left is not terms[at_term - 1][0]:
+                turned[:, :count] = left[...].T
+
+            def move(place, carry, count=count, order=order):
                 source = pl.multiple_of((me ^ slice_at(place, order)) * slab, 16)
                 target = pl.multiple_of(place * slab, 16)
                 ordered[pl.ds(target, slab), :count] = turned[pl.ds(source, slab), :count]
@@ -483,9 +491,9 @@
             else:
                 field = right[:, index * wide : (index + 1) * wide]
             field = field.astype(BF16)
-            keep_out[:, column : column + wide] = dot(ordered[:half, :count], field)
+            keep_out[:half, column : column + wide] = dot(ordered[:half, :count], field)
             at = column % share
-            send_outs[column // share][:, at : at + wide] = dot(ordered[half:, :count], field)
+            send_outs[column // share][:half, at : at + wide] = dot(ordered[half:, :count], field)
             column += wide
 
 
@@ -493,7 +501,7 @@
     products = (len(refs) - 7) // 2
     lefts, rights = refs[:products], refs[products : 2 * products]
     keep_out, *send_outs = refs[2 * products : -2]
-    fill_grads(order, info[me_at], zip(lefts, rights), keep_out, send_outs, *refs[-2:])
+    fill_grads(order, info[me_at], tuple(zip(lefts, rights)), keep_out, send_outs, *refs[-2:])
 
 
 def add_halves(pieces, joined, split, *refs):
@@ -613,7 +621,9 @@
     sine = jnp.sin(angles)
 
     bits = [1 << at for at in range(dp_size.bit_length() - 1)]
-    order = bits if slab % 16 == 0 else None
+    far_first = bits[:1] + bits[2:] + bits[1:2]
+    order = [bits] if slab % 16 == 0 else None
+    mixed_order = [bits, bits, far_first] if slab % 16 == 0 else None
 
     def add_sent(name, kept, came, joined=(), split=None):
         rows, total = kept.shape[0] // 2, kept.shape[1]
@@ -642,21 +652,34 @@
             cost_estimate=work(0),
         )(*[value for value in (kept, *came) for _ in range(2)], *joined)
 
-    def sorted_halves(kept, *sent):
-        if order is not None:
+    def sorted_halves(kept, *sent, orders=(bits,)):
+        if slab % 16 == 0:
             return kept, sent
-        value = jnp.concatenate([kept, jnp.concatenate(sent, axis=1)], axis=0)
-        places = jnp.array([slice_at(place, bits) for place in range(dp_size)], jnp.int32) ^ dp_at
-        value = jnp.take(value.reshape(dp_size, slab, -1), places, axis=0).reshape(value.shape)
-        return value[: width // 2], jnp.split(value[width // 2 :], len(sent), axis=1)
+        half = width // 2
+        value = jnp.concatenate([kept[:half], jnp.concatenate([piece[:half] for piece in sent], axis=1)], axis=0)
+        made = []
+        for part, wanted in zip(jnp.split(value, len(orders), axis=1), orders):
+            places = jnp.array([slice_at(place, wanted) for place in range(dp_size)], jnp.int32) ^ dp_at
+            made.append(jnp.take(part.reshape(dp_size, slab, -1), places, axis=0).reshape(part.shape))
+        value = jnp.concatenate(made, axis=1)
+        fresh = jnp.split(value[half:], len(sent), axis=1)
+        sent = [jnp.concatenate([new, old[half:]], axis=0) for new, old in zip(fresh, sent)]
+        return jnp.concatenate([value[:half], kept[half:]], axis=0), sent
+
+    def ride_on(kept, sent, bit):
+        came = across(sent, bit)
+        half = kept.shape[0] // 2
+        far = jnp.concatenate([kept[half:], sent[-RIDE:]], axis=0)
+        return kept[:half] + came[:half], far + came[half:]
 
     def core_halve(halves, gate=None):
         kept, sent = halves
         came = jnp.concatenate([across(piece, 1) for piece in sent], axis=1)
         return merge(kept if gate is None else after(kept, *gate), came)
 
-    def grads_of(total, shares):
-        return (shape((width // 2, total)),) + (shape((width // 2, total // shares)),) * shares
+    def grads_of(total, shares, more=0):
+        rows = width // 2 + more
+        return (shape((rows, total)),) + (shape((rows, total // shares)),) * shares
 
     def turning(most):
         return [pltpu.VMEM((width, most), BF16), pltpu.VMEM((width, most), BF16)]
@@ -790,7 +813,7 @@
         )
     )
     came_mlp = [across(piece, 1) for piece in mlp[1]]
-    *first, late_kept, late_sent = add_sent("add_mlp", mlp[0], came_mlp, split=3 * hidden // 2)
+    first = add_sent("add_mlp", mlp[0], came_mlp)
     (
         grad_two,
         grad_query,
@@ -846,11 +869,11 @@
     store_keep = dot_t(grad_store, own_kv)
     cross = sorted_halves(*cross_halves)
     came_cross = [across(piece, 1) for piece in cross[1]]
-    third = add_sent("add_cross", cross[0], came_cross, (late_kept, late_sent))
+    third = add_sent("add_cross", cross[0], came_cross)
     store_back = swap(after(store_send, third[1]))
 
-    tok_keep, both_send, sums, *self_halves = call(
-        partial(self_backward, slots, order),
+    tok_keep, both_send, *self_halves = call(
+        partial(self_backward, slots, mixed_order),
         "self_backward",
         (info,),
         (
@@ -881,8 +904,7 @@
         (
             shape((count, own_width)),
             shape((count, width)),
-            shape((16, width)),
-            *grads_of(4 * local, 2),
+            *grads_of(4 * local, 2, RIDE),
         ),
         [
             pltpu.VMEM((local, width), BF16),
@@ -894,37 +916,55 @@
             pltpu.VMEM((count, width), BF16),
             pltpu.VMEM((3 * pairs, count, LANES), BF16),
             *turning(count),
+            pltpu.VMEM((2 * RIDE, width), F32),
         ],
         flops=40_000_000_000,
     )
     back = swap(both_send)
+    neighbours_grad = (store_keep + store_back).astype(BF16)
+
+    first = halve(after(first[0], self_halves[0]), first[1], bits[2])
+    third_came = across(third[1], bits[1])
+    third = merge(after(third[0], self_halves[0]), third_came)
+    kept, sent = sorted_halves(*self_halves, orders=(bits, far_first))
+    kept = after(kept, first[1], third[1])
+    half, middle = width // 4, 2 * local
+
+    def ride_core(kept, sent):
+        came = across(sent, 1)
+        return kept[:half] + came[:half], kept[half:] + came[half:]
+
+    def ride_end(kept, sent, order):
+        for bit in order[:-1]:
+            kept, sent = ride_on(kept, sent, bit)
+        came = across(sent, order[-1])
+        return kept + came[:slab], sent[-RIDE:] + came[slab:]
+
+    near_part = ride_core(kept[:, :middle], sent[0])
+    far_part = ride_core(kept[:, middle:], sent[1])
+    third = after(third[0], near_part[1], far_part[1]), third[1]
+    first = after(first[0], near_part[1], far_part[1]), first[1]
+    near_part = ride_on(*near_part, bits[1])
+    far_part = ride_on(*far_part, far_first[1])
+    done = near_part[1], far_part[1]
+    near_part, low_sums = ride_end(*near_part, bits[2:])
+    far_part, high_sums = ride_end(*far_part, far_first[2:])
+    self_grads = jnp.concatenate([near_part, far_part], axis=1)
+    sums = jnp.concatenate([low_sums, high_sums], axis=0)
+
+    back = after(back, *done)
     tokens_grad = (tok_keep + back[:, :own_width]).astype(BF16)
     output = (out_keep + back[:, own_width:]).astype(BF16)
-    neighbours_grad = (store_keep + store_back).astype(BF16)
-
-    first_came = across(first[1], bits[2])
-    third_came = across(third[1], bits[1])
-    fourth = core_halve(sorted_halves(*self_halves), (first_came, third_came, store_back))
-    first = merge(first[0], first_came)
-    third = merge(third[0], third_came)
-    sums, *first = lax.optimization_barrier((sums, *first, fourth[1]))[:3]
 
     def finish(parts, order):
         for bit in order[:-1]:
             parts = halve(*parts, bit)
-        return parts[0] + across(parts[1], order[-1])
+        return after(parts[0], *done) + across(parts[1], order[-1])
 
     mlp_grads = finish(first, bits[3:])
-    third = finish(third, bits[2:])
-    self_grads = finish(fourth, bits[1:])
-    cross_grads = third[:, : 4 * local]
-    mlp_out_w_grad = mlp_grads[:, :hidden]
-    mlp_in_w_grad = jnp.concatenate([mlp_grads[:, hidden:], third[:, 4 * local :]], axis=1)
-
-    bit = 1
-    while bit < dp_size:
-        sums = sums + across(sums, bit)
-        bit *= 2
+    cross_grads = finish(third, bits[2:])
+    mlp_out_w_grad, mlp_in_w_grad = mlp_grads[:, :hidden], mlp_grads[:, hidden:]
+
     shared = 0.5 * sums[2:9]
     shared = jnp.concatenate([sums[0:2], shared], axis=0)
     shared = shared + swap(shared)

time: 289 us -> 275 us (0.952)
  waiting for transfers between devices: 109 us -> 104 us
  other arithmetic: 18.4 us -> 13.4 us
    ppermute x10, waiting for transfers between devices: 49.1 us -> 35.3 us  [swap(): return lax.ppermute(value, 'tp', [(0, 1), (1, 0)])]
    ppermute x24 -> x23, waiting for transfers between devices: 59.6 us -> 68.4 us  [across(): return lax.ppermute(value, 'dp', [(at, at ^ bit) for at in range(dp_size)])]
    add x7 -> x4, other arithmetic: 9.82 us -> 7.2 us  [merge(): return (kept[:half] + arrived[:half], kept[half:] + arrived[half:])]
    unnamed x66 -> x63, local copies, waits for them, and re-layouts: 6.93 us -> 5.25 us
    ppermute x24 -> x23, starting transfers between devices: 18.5 us -> 17.8 us  [across(): return lax.ppermute(value, 'dp', [(at, at ^ bit) for at in range(dp_size)])]
  transfers between devices with their start and end apart: 34 -> 33, of which waited for: 17 -> 15; matrix products, arithmetic and copies ran while one was open for 12% -> 11% of each run, Pallas kernels for 35% -> 37%
where the time goes in v3:
time: 275 us; the launch traced here: 274 us
  waiting for transfers between devices  104 us (38%)
  Pallas kernels  102 us (37%)
  starting transfers between devices  29.8 us (11%)
  local copies, waits for them, and re-layouts  15.3 us (6%)
  other arithmetic  13.4 us (5%)
  matrix products  8.18 us (3%)
    pallas_call x5, Pallas kernels, call(): pl.pallas_call(body, name=name, out_shape=outs, in_specs=scalars(len(smal...  77.9 us
    ppermute x23, waiting for transfers between devices, across(): return lax.ppermute(value, 'dp', [(at, at ^ bit) for at in range(dp_size)])  68.4 us
    ppermute x10, waiting for transfers between devices, swap(): return lax.ppermute(value, 'tp', [(0, 1), (1, 0)])  35.3 us
    ppermute x23, starting transfers between devices, across(): return lax.ppermute(value, 'dp', [(at, at ^ bit) for at in range(dp_size)])  17.8 us
    pallas_call x1, Pallas kernels, per_device(): pl.pallas_call(feed_forward, name='feed_forward', grid=(count // step,),...  13.7 us
    ppermute x10, starting transfers between devices, swap(): return lax.ppermute(value, 'tp', [(0, 1), (1, 0)])  12 us
    pallas_call x2, Pallas kernels, add_sent(): pl.pallas_call(partial(add_halves, len(came), bool(joined), split), name=...  10.4 us
    add x4, other arithmetic, merge(): return (kept[:half] + arrived[:half], kept[half:] + arrived[half:])  7.2 us
  transfers between devices with their start and end apart: 33, of which 15 were waited for; matrix products, arithmetic and copies ran while one was open for 11% of the time, Pallas kernels for 37%

profile of v3, /device:TPU:0, one launch (start us, length us, event | category | flops | bytes accessed | tf_op | source)
XLA Modules:
  0.0 274.2 jit_solution(14059423989120891001)
XLA Ops:
  0.7 1.0 dynamic-slice_convert_fusion.1
  1.7 3.1 %collective-permute-start.1 = (f32[192,768]{1,0:T(8,128)S(1)}, f32[192,768]{1,0:T(8,128)}, u32[]{:S(2)}, u32[]{:S(2)}) collective-permute-start(f32[192,768]{1,0:T(8,128)S(1)} %dynamic-slice_convert_fusion.1), channel_id=1, source_target_pairs={{0,1},{1,0},{2,3},{3,2},{4,5},{5,4},{6,7},{7,6},{8,9},{9,8},{10,11... | collective-permute-start | bytes 1769480 | tf_op jit(solution)/shard_map/ppermute | solution.py:592
  5.7 1.8 multiply_sine_fusion
  7.5 0.6 concatenate.30.info
  8.1 10.6 %self_forward.1 = (bf16[512,768]{1,0:T(8,128)(2,1)}, bf16[9,512,128]{2,1,0:T(8,128)(2,1)}, f32[512,384]{1,0:T(8,128)}, f32[512,128]{1,0:T(8,128)}, f32[512,512]{1,0:T(8,128)}) custom-call(s32[8]{0:T(128)} %concatenate.30.info, bf16[512,768]{1,0:T(8,128)(2,1)} %tok.5, bf16[3,768,384]{2,1,0:T(8,128)(2,1)} %bitcast.39, f32[3,384]{1,0:T(4,128)} %bias.1, ...), custom_call_target="tpu_custom_call" | custom-call | flops 11000000512 | bytes 1 | tf_op jit(solution)/shard_map/self_forward/pallas_call | solution.py:544
  19.3 0.7 copy.49.picks
  21.5 1.6 copy-done.25
  23.0 2.6 fusion.kv
  25.7 12.3 %collective-permute-done.mix_peer = f32[512,384]{1,0:T(8,128)} collective-permute-done((f32[512,384]{1,0:T(8,128)}, f32[512,384]{1,0:T(8,128)}, u32[]{:S(2)}, u32[]{:S(2)}) %collective-permute-start) | collective-permute-done | bytes 786464 | tf_op jit(solution)/shard_map/ppermute | solution.py:592
  38.4 0.8 copy-done.29
  39.2 13.8 %cross_forward.1 = (f32[512,768]{1,0:T(8,128)}, bf16[512,768]{1,0:T(8,128)(2,1)}, bf16[512,384]{1,0:T(8,128)(2,1)}, f32[512,384]{1,0:T(8,128)}, f32[512,128]{1,0:T(8,128)}) custom-call(s32[8]{0:T(128)} %concatenate.30.info, s32[8,2]{1,0:T(8,128)} %copy.49.picks, bf16[512,768]{1,0:T(8,128)(2,1)} %tok.5, f32[512,384]{1,0:T(8,128)} %get-tuple-element.75.mix_own.mix, ...), custom_call_target="tpu_custom_call" | custom-call | flops 14000000000 | bytes 1 | tf_op jit(solution)/shard_map/cross_forward/pallas_call | solution.py:544
  52.9 1.7 collective-permute-start.3
  54.7 0.7 reshape.103.in_b
  56.9 14.4 %collective-permute-done.3.mix_peer = f32[512,384]{1,0:T(8,128)S(1)} collective-permute-done((f32[512,384]{1,0:T(8,128)}, f32[512,384]{1,0:T(8,128)S(1)}, u32[]{:S(2)}, u32[]{:S(2)}) %collective-permute-start.3) | collective-permute-done | bytes 786464 | tf_op jit(solution)/shard_map/ppermute | solution.py:592
  71.3 1.5 collective-permute-start.7
  72.8 13.7 %feed_forward.1 = (f32[512,768]{1,0:T(8,128)}, bf16[512,768]{1,0:T(8,128)(2,1)}, bf16[512,1536]{1,0:T(8,128)(2,1)}, bf16[512,1536]{1,0:T(8,128)(2,1)}, f32[512,3...) custom-call(s32[8]{0:T(128)} %concatenate.30.info, ...), custom_call_target="tpu_custom_call" | custom-call | flops 14000000000 | bytes 1 | tf_op jit(solution)/shard_map/feed_forward/pallas_call | solution.py:756
  86.5 0.9 collective-permute-start.6
  87.4 9.5 %mlp_grads.1 = (f32[384,3072]{1,0:T(8,128)}, f32[384,768]{1,0:T(8,128)}, f32[384,768]{1,0:T(8,128)}, f32[384,768]{1,0:T(8,128)}, f32[384,768]{1,0:T(8,128)}) custom-call(s32[8]{0:T(128)} %concatenate.30.info, bf16[512,768]{1,0:T(8,128)(2,1)} %out_grad.1, bf16[512,768]{1,0:T(8,128)(2,1)} %get-tuple-element.84.refs_1_, ...), custom_call_target="tpu_custom_call" | custom-call | bytes 1 | tf_op jit(solution)/shard_map/mlp_grads/pallas_call | solution.py:544
  97.9 2.0 collective-permute-done.10.refs_6_.refs_7_
  99.9 1.7 collective-permute-done.11.refs_8_.refs_9_
  101.6 1.7 collective-permute-done.8.refs_2_.refs_3_
  103.3 1.8 collective-permute-done.9.refs_4_.refs_5_
  105.1 6.1 %add_mlp.1 = (f32[192,3072]{1,0:T(8,128)}, f32[192,3072]{1,0:T(8,128)}) custom-call(f32[384,3072]{1,0:T(8,128)} %get-tuple-element.87.refs_0_.refs_1_, f32[384,3072]{1,0:T(8,128)} %get-tuple-element.87.refs_0_.refs_1_, f32[384,768]{1,0:T(8,128)} %copy-done.5, f32[384,768]{1,0:T(8,128)} %copy-done.5, f32[384,768]{1,0:T(8,128)} %collective-permute-done.9.refs_4_.refs_5_, ...), custom_call_target="tpu_custom_call" | custom-call | bytes 1 | tf_op jit(solution)/shard_map/add_mlp/pallas_call | solution.py:644
  111.2 1.5 collective-permute-start.16
  112.7 7.7 %collective-permute-done.6.part_peer = f32[512,768]{1,0:T(8,128)} collective-permute-done((f32[512,768]{1,0:T(8,128)}, f32[512,768]{1,0:T(8,128)}, u32[]{:S(2)}, u32[]{:S(2)}) %collective-permute-start.6) | collective-permute-done | bytes 1572896 | tf_op jit(solution)/shard_map/ppermute | solution.py:592
  120.4 21.9 %cross_backward.1 = (f32[512,768]{1,0:T(8,128)}, f32[512,384]{1,0:T(8,128)}, bf16[512,384]{1,0:T(8,128)(2,1)}, bf16[1024,768]{1,0:T(8,128)(2,1)}, f32[8,768]{1,0...) custom-call(s32[8]{0:T(128)} %concatenate.30.info, ...), custom_call_target="tpu_custom_call" | custom-call | flops 16999999488 | bytes 1 | tf_op jit(solution)/shard_map/cross_backward/pallas_call | solution.py:544
  142.9 1.1 collective-permute-start.12
  144.1 3.6 %fusion.4 = f32[1024,384]{1,0:T(8,128)} fusion(bf16[1024,768]{1,0:T(8,128)(2,1)} %get-tuple-element.125, s32[]{:T(128)S(6)} %select_n.40, bf16[768,384]{1,0:T(8,128)(2,1)S(1)} %copy-done.8, bf16[768,384]{1,0:T(8,128)(2,1)S(1)} %copy-done.10), kind=kOutput, calls=%fused_computation.17 | convolution fusion | flops 605159424 | bytes 4325380 | tf_op jit(solution)/shard_map/dot_general | solution.py:25
  147.7 1.0 copy-done.1
  149.1 4.3 %add_cross.1 = (f32[192,1536]{1,0:T(8,128)}, f32[192,1536]{1,0:T(8,128)}) custom-call(f32[384,1536]{1,0:T(8,128)} %get-tuple-element.100.refs_0_.refs_1_, f32[384,1536]{1,0:T(8,128)} %get-tuple-element.100.refs_0_.refs_1_, f32[384,768]{1,0:T(8,128)} %copy-done.1, f32[384,768]{1,0:T(8,128)} %copy-done.1, f32[384,768]{1,0:T(8,128)} %copy-done.2, ...), custom_call_target="tpu_custom_call" | custom-call | bytes 1 | tf_op jit(solution)/shard_map/add_cross/pallas_call | solution.py:644
  153.4 1.5 collective-permute-start.19
  154.9 0.9 collective-permute-start.24
  155.8 9.9 %collective-permute-done.16 = f32[192,3072]{1,0:T(8,128)} collective-permute-done((f32[192,3072]{1,0:T(8,128)}, f32[192,3072]{1,0:T(8,128)}, u32[]{:S(2)}, u32[]{:S(2)}) %collective-permute-start.16) | collective-permute-done | bytes 2359328 | tf_op jit(solution)/shard_map/ppermute | solution.py:595
  165.7 3.7 %slice_add_fusion = (f32[96,3072]{1,0:T(8,128)S(1)}, f32[96,3072]{1,0:T(8,128)}) fusion(f32[192,3072]{1,0:T(8,128)} %collective-permute-done.16, f32[192,3072]{1,0:T(8,128)} %get-tuple-element.104), kind=kLoop, calls=%fused_computation.8 | loop fusion | flops 589824 | bytes 7077888 | tf_op jit(solution)/shard_map/add | solution.py:689
  169.4 1.6 collective-permute-start.18
  171.0 22.2 %self_backward.1 = (f32[512,384]{1,0:T(8,128)}, f32[512,768]{1,0:T(8,128)}, f32[392,1536]{1,0:T(8,128)}, f32[392,768]{1,0:T(8,128)}, f32[392,768]{1,0:T(8,128)}) custom-call(s32[8]{0:T(128)} %concatenate.30.info, bf16[512,384]{1,0:T(8,128)(2,1)} %get-tuple-element.97.query_own, f32[512,384]{1,0:T(8,128)} %collective-permute-done.12.query_peer, ...), custom_call_target="tpu_custom_call" | custom-call | flops 40000000000 | bytes 1 | tf_op jit(solution)/shard_map/self_backward/pallas_call | solution.py:544
  193.7 1.9 slice_add_fusion.5
  196.1 0.6 collective-permute-done.24
  196.7 1.1 collective-permute-start.17
  197.9 1.9 add_convert_fusion.1
  199.8 1.5 slice_add_fusion.4
  201.3 2.6 collective-permute-start.32
  204.1 1.6 collective-permute-start.21
  205.7 1.6 collective-permute-start.23
  207.3 13.5 %collective-permute-done.30 = f32[96,1536]{1,0:T(8,128)S(1)} collective-permute-done((f32[96,1536]{1,0:T(8,128)S(1)}, f32[96,1536]{1,0:T(8,128)S(1)}, u32[]{:S(2)}, u32[]{:S(2)}) %collective-permute-start.30) | collective-permute-done | bytes 589856 | tf_op jit(solution)/shard_map/ppermute | solution.py:595
  221.2 21.9 %collective-permute-done.23 = f32[200,768]{1,0:T(8,128)S(1)} collective-permute-done((f32[200,768]{1,0:T(8,128)S(1)}, f32[200,768]{1,0:T(8,128)S(1)}, u32[]{:S(2)}, u32[]{:S(2)}) %collective-permute-start.23) | collective-permute-done | bytes 614432 | tf_op jit(solution)/shard_map/ppermute | solution.py:595
  243.4 2.9 %collective-permute-start.27 = (f32[104,768]{1,0:T(8,128)S(1)}, f32[104,768]{1,0:T(8,128)S(1)}, u32[]{:S(2)}, u32[]{:S(2)}) collective-permute-start(f32[104,768]{1,0:T(8,128)S(1)} %slice_add_fusion.10), channel_id=1, source_target_pairs={{0,16},{2,18},{4,20},{6,22},{8,24},{10,26},{12,28},{14,30},{16,0},... | collective-permute-start | bytes 958472 | tf_op jit(solution)/shard_map/ppermute | solution.py:595
  246.4 0.8 slice_bitcast_fusion.2
  247.2 1.0 add_convert_fusion.2
  248.3 0.7 slice_bitcast_fusion.3
  249.0 0.7 reshape.108
  249.8 8.6 %collective-permute-done.25 = f32[104,768]{1,0:T(8,128)S(1)} collective-permute-done((f32[104,768]{1,0:T(8,128)S(1)}, f32[104,768]{1,0:T(8,128)S(1)}, u32[]{:S(2)}, u32[]{:S(2)}) %collective-permute-start.25) | collective-permute-done | bytes 319520 | tf_op jit(solution)/shard_map/ppermute | solution.py:595
  258.5 3.4 %collective-permute-done.27 = f32[104,768]{1,0:T(8,128)S(1)} collective-permute-done((f32[104,768]{1,0:T(8,128)S(1)}, f32[104,768]{1,0:T(8,128)S(1)}, u32[]{:S(2)}, u32[]{:S(2)}) %collective-permute-start.27) | collective-permute-done | bytes 319520 | tf_op jit(solution)/shard_map/ppermute | solution.py:595
  261.9 1.6 collective-permute-start.28
  263.4 3.9 %collective-permute-done.26 = f32[56,768]{1,0:T(8,128)S(1)} collective-permute-done((f32[56,768]{1,0:T(8,128)S(1)}, f32[56,768]{1,0:T(8,128)S(1)}, u32[]{:S(2)}, u32[]{:S(2)}) %collective-permute-start.26) | collective-permute-done | bytes 172064 | tf_op jit(solution)/shard_map/ppermute | solution.py:595
  267.4 0.6 slice_bitcast_fusion.4
  268.1 1.4 collective-permute-start.29
  269.5 0.6 fusion.18
  270.1 0.6 slice.376
  270.7 0.7 copy.59
  271.4 0.6 slice.362
  272.3 0.6 slice_reduce_fusion
  272.9 0.6 pad_maximum_fusion.6
  273.6 0.6 pad_maximum_fusion.5
  (136 shorter events, 8.8 us)
Async XLA Ops:
  0.7 6.8 %copy-start.24 = (s32[1,4]{1,0:T(1,128)S(1)}, s32[1,4]{1,0:T(1,128)}, u32[]{:S(2)}) copy-start(s32[1,4]{1,0:T(1,128)} %param.26) | copy-start | bytes 52
  1.7 19.5 %collective-permute-start.1 = (f32[192,768]{1,0:T(8,128)S(1)}, f32[192,768]{1,0:T(8,128)}, u32[]{:S(2)}, u32[]{:S(2)}) collective-permute-start(f32[192,768]{1,0:T(8,128)S(1)} %dynamic-slice_convert_fusion.1), channel_id=1, source_target_pairs={{0,1},{1,0},{2,3},{3,2},{4,5},{5,4},{6,7},{7,6},{8,9},{9,8},{10,11... | collective-permute-start | bytes 1769480 | tf_op jit(solution)/shard_map/ppermute | solution.py:592
  8.1 10.7 %copy-start.12 = (bf16[768,2,384]{2,1,0:T(2,128)(2,1)S(1)}, bf16[768,2,384]{2,1,0:T(2,128)(2,1)}, u32[]{:S(2)}) copy-start(bf16[768,2,384]{2,1,0:T(2,128)(2,1)} %param.36) | copy-start | bytes 3538948
  18.6 0.7 copy-start.23
  18.6 1.4 copy-start.18
  18.6 1.9 copy-start.21
  18.7 2.5 copy-start.22
  18.7 2.5 copy-start.16
  18.7 19.4 %collective-permute-start = (f32[512,384]{1,0:T(8,128)}, f32[512,384]{1,0:T(8,128)}, u32[]{:S(2)}, u32[]{:S(2)}) collective-permute-start(f32[512,384]{1,0:T(8,128)} %get-tuple-element.75.mix_own.mix), channel_id=1, source_target_pairs={{0,1},{1,0},{2,3},{3,2},{4,5},{5,4},{6,7},{7,6},{8,9},{9,8},{10,11... | collective-permute-start | bytes 2359304 | tf_op jit(solution)/shard_map/ppermute | solution.py:592
  21.2 1.8 copy-start.25
  21.2 17.1 %collective-permute-start.2 = (f32[192,768]{1,0:T(8,128)}, f32[192,768]{1,0:T(8,128)S(1)}, u32[]{:S(2)}, u32[]{:S(2)}) collective-permute-start(f32[192,768]{1,0:T(8,128)} %collective-permute-done.1.w_near), channel_id=1, source_target_pairs={{0,2},{2,0},{4,6},{6,4},{8,10},{10,8},{12,14},{14,12},{16,18},{18,... | collective-permute-start | bytes 1769480 | tf_op jit(solution)/shard_map/ppermute | solution.py:595
  21.4 4.3 %copy-start.7 = (bf16[768,384]{1,0:T(8,128)(2,1)}, bf16[768,384]{1,0:T(8,128)(2,1)S(1)}, u32[]{:S(2)}) copy-start(bf16[768,384]{1,0:T(8,128)(2,1)S(1)} %get-tuple-element.186) | copy-start | bytes 1769476
  21.5 4.2 %copy-start.9 = (bf16[768,384]{1,0:T(8,128)(2,1)}, bf16[768,384]{1,0:T(8,128)(2,1)S(1)}, u32[]{:S(2)}) copy-start(bf16[768,384]{1,0:T(8,128)(2,1)S(1)} %get-tuple-element.187) | copy-start | bytes 1769476
  25.7 29.0 %copy-start.17 = (f32[1536]{0:T(1024)S(1)}, f32[1536]{0:T(1024)}, u32[]{:S(2)}) copy-start(f32[1536]{0:T(1024)} %param.41) | copy-start | bytes 18436
  25.7 29.7 %copy-start.19 = (f32[768]{0:T(1024)S(1)}, f32[768]{0:T(1024)}, u32[]{:S(2)}) copy-start(f32[768]{0:T(1024)} %param.39) | copy-start | bytes 9220
  25.7 30.2 %copy-start.20 = (f32[768]{0:T(1024)S(1)}, f32[768]{0:T(1024)}, u32[]{:S(2)}) copy-start(f32[768]{0:T(1024)} %param.43) | copy-start | bytes 9220
  25.7 30.8 %copy-start.15 = (bf16[768,384]{1,0:T(8,128)(2,1)S(1)}, bf16[768,384]{1,0:T(8,128)(2,1)}, u32[]{:S(2)}) copy-start(bf16[768,384]{1,0:T(8,128)(2,1)} %q_w.3) | copy-start | bytes 1769476
  38.1 16.6 %collective-permute-start.4 = (f32[192,768]{1,0:T(8,128)S(1)}, f32[192,768]{1,0:T(8,128)S(1)}, u32[]{:S(2)}, u32[]{:S(2)}) collective-permute-start(f32[192,768]{1,0:T(8,128)S(1)} %dynamic-slice_convert_fusion), channel_id=1, source_target_pairs={{0,1},{1,0},{2,3},{3,2},{4,5},{5,4},{6,7},{7,6},{8,9},{9,8},{10,11... | collective-permute-start | bytes 1769480 | tf_op jit(solution)/shard_map/ppermute | solution.py:592
  38.4 0.8 copy-start.29
  52.9 18.4 %collective-permute-start.3 = (f32[512,384]{1,0:T(8,128)}, f32[512,384]{1,0:T(8,128)S(1)}, u32[]{:S(2)}, u32[]{:S(2)}) collective-permute-start(f32[512,384]{1,0:T(8,128)} %get-tuple-element.77.mix_own.mix), channel_id=1, source_target_pairs={{0,1},{1,0},{2,3},{3,2},{4,5},{5,4},{6,7},{7,6},{8,9},{9,8},{10,11... | collective-permute-start | bytes 2359304 | tf_op jit(solution)/shard_map/ppermute | solution.py:592
  54.7 18.1 %copy-start.28 = (f32[192,768]{1,0:T(8,128)}, f32[192,768]{1,0:T(8,128)S(1)}, u32[]{:S(2)}) copy-start(f32[192,768]{1,0:T(8,128)S(1)} %collective-permute-done.4.w_near) | copy-start | bytes 1769476
  54.7 18.1 %collective-permute-start.5 = (f32[192,768]{1,0:T(8,128)S(1)}, f32[192,768]{1,0:T(8,128)}, u32[]{:S(2)}, u32[]{:S(2)}) collective-permute-start(f32[192,768]{1,0:T(8,128)S(1)} %collective-permute-done.4.w_near), channel_id=1, source_target_pairs={{0,2},{2,0},{4,6},{6,4},{8,10},{10,8},{12,14},{14,12},{16,18},{18,... | collective-permute-start | bytes 1769480 | tf_op jit(solution)/shard_map/ppermute | solution.py:595
  71.3 1.5 copy-start.26
  71.3 16.1 %collective-permute-start.7 = (f32[192,768]{1,0:T(8,128)S(1)}, f32[192,768]{1,0:T(8,128)S(1)}, u32[]{:S(2)}, u32[]{:S(2)}) collective-permute-start(f32[192,768]{1,0:T(8,128)S(1)} %convert_bitcast_fusion), channel_id=1, source_target_pairs={{0,1},{1,0},{2,3},{3,2},{4,5},{5,4},{6,7},{7,6},{8,9},{9,8},{10,11... | collective-permute-start | bytes 1769480 | tf_op jit(solution)/shard_map/ppermute | solution.py:592
  86.5 34.0 %collective-permute-start.6 = (f32[512,768]{1,0:T(8,128)}, f32[512,768]{1,0:T(8,128)}, u32[]{:S(2)}, u32[]{:S(2)}) collective-permute-start(f32[512,768]{1,0:T(8,128)} %get-tuple-element.80.part_own), channel_id=1, source_target_pairs={{0,1},{1,0},{2,3},{3,2},{4,5},{5,4},{6,7},{7,6},{8,9},{9,8},{10,11... | collective-permute-start | bytes 4718600 | tf_op jit(solution)/shard_map/ppermute | solution.py:592
  87.4 9.5 %copy-start.27 = (f32[192,768]{1,0:T(8,128)}, f32[192,768]{1,0:T(8,128)S(1)}, u32[]{:S(2)}) copy-start(f32[192,768]{1,0:T(8,128)S(1)} %collective-permute-done.7.q_near) | copy-start | bytes 1769476
  96.8 3.1 %collective-permute-start.10 = (f32[384,768]{1,0:T(8,128)}, f32[384,768]{1,0:T(8,128)S(1)}, u32[]{:S(2)}, u32[]{:S(2)}) collective-permute-start(f32[384,768]{1,0:T(8,128)} %get-tuple-element.90), channel_id=1, source_target_pairs={{0,2},{2,0},{4,6},{6,4},{8,10},{10,8},{12,14},{14,12},{16,18},{18,... | collective-permute-start | bytes 3538952 | tf_op jit(solution)/shard_map/ppermute | solution.py:595
  96.9 4.7 %collective-permute-start.11 = (f32[384,768]{1,0:T(8,128)}, f32[384,768]{1,0:T(8,128)S(1)}, u32[]{:S(2)}, u32[]{:S(2)}) collective-permute-start(f32[384,768]{1,0:T(8,128)} %get-tuple-element.91), channel_id=1, source_target_pairs={{0,2},{2,0},{4,6},{6,4},{8,10},{10,8},{12,14},{14,12},{16,18},{18,... | collective-permute-start | bytes 3538952 | tf_op jit(solution)/shard_map/ppermute | solution.py:595
  97.4 5.9 %collective-permute-start.8 = (f32[384,768]{1,0:T(8,128)}, f32[384,768]{1,0:T(8,128)S(1)}, u32[]{:S(2)}, u32[]{:S(2)}) collective-permute-start(f32[384,768]{1,0:T(8,128)} %get-tuple-element.88), channel_id=1, source_target_pairs={{0,2},{2,0},{4,6},{6,4},{8,10},{10,8},{12,14},{14,12},{16,18},{18,... | collective-permute-start | bytes 3538952 | tf_op jit(solution)/shard_map/ppermute | solution.py:595
  97.4 7.7 %collective-permute-start.9 = (f32[384,768]{1,0:T(8,128)}, f32[384,768]{1,0:T(8,128)}, u32[]{:S(2)}, u32[]{:S(2)}) collective-permute-start(f32[384,768]{1,0:T(8,128)} %get-tuple-element.89), channel_id=1, source_target_pairs={{0,2},{2,0},{4,6},{6,4},{8,10},{10,8},{12,14},{14,12},{16,18},{18,... | collective-permute-start | bytes 3538952 | tf_op jit(solution)/shard_map/ppermute | solution.py:595
  99.9 5.2 %copy-start.3 = (f32[384,768]{1,0:T(8,128)}, f32[384,768]{1,0:T(8,128)S(1)}, u32[]{:S(2)}) copy-start(f32[384,768]{1,0:T(8,128)S(1)} %collective-permute-done.10.refs_6_.refs_7_) | copy-start | bytes 3538948
  101.6 3.5 %copy-start.4 = (f32[384,768]{1,0:T(8,128)}, f32[384,768]{1,0:T(8,128)S(1)}, u32[]{:S(2)}) copy-start(f32[384,768]{1,0:T(8,128)S(1)} %collective-permute-done.11.refs_8_.refs_9_) | copy-start | bytes 3538948
  103.3 1.8 copy-start.5
  111.2 54.5 %collective-permute-start.16 = (f32[192,3072]{1,0:T(8,128)}, f32[192,3072]{1,0:T(8,128)}, u32[]{:S(2)}, u32[]{:S(2)}) collective-permute-start(f32[192,3072]{1,0:T(8,128)} %get-tuple-element.92), channel_id=1, source_target_pairs={{0,4},{2,6},{4,0},{6,2},{8,12},{10,14},{12,8},{14,10},{16,20},{18,... | collective-permute-start | bytes 7077896 | tf_op jit(solution)/shard_map/ppermute | solution.py:595
  120.4 23.6 %copy-start.8 = (bf16[768,384]{1,0:T(8,128)(2,1)S(1)}, bf16[768,384]{1,0:T(8,128)(2,1)}, u32[]{:S(2)}) copy-start(bf16[768,384]{1,0:T(8,128)(2,1)} %copy-done.7) | copy-start | bytes 1769476
  120.4 23.6 %copy-start.10 = (bf16[768,384]{1,0:T(8,128)(2,1)S(1)}, bf16[768,384]{1,0:T(8,128)(2,1)}, u32[]{:S(2)}) copy-start(bf16[768,384]{1,0:T(8,128)(2,1)} %copy-done.9) | copy-start | bytes 1769476
  142.3 5.4 %collective-permute-start.14 = (f32[384,768]{1,0:T(8,128)}, f32[384,768]{1,0:T(8,128)S(1)}, u32[]{:S(2)}, u32[]{:S(2)}) collective-permute-start(f32[384,768]{1,0:T(8,128)} %get-tuple-element.101), channel_id=1, source_target_pairs={{0,2},{2,0},{4,6},{6,4},{8,10},{10,8},{12,14},{14,12},{16,18},{18,... | collective-permute-start | bytes 3538952 | tf_op jit(solution)/shard_map/ppermute | solution.py:595
  142.4 5.3 %collective-permute-start.15 = (f32[384,768]{1,0:T(8,128)}, f32[384,768]{1,0:T(8,128)S(1)}, u32[]{:S(2)}, u32[]{:S(2)}) collective-permute-start(f32[384,768]{1,0:T(8,128)} %get-tuple-element.102), channel_id=1, source_target_pairs={{0,2},{2,0},{4,6},{6,4},{8,10},{10,8},{12,14},{14,12},{16,18},{18,... | collective-permute-start | bytes 3538952 | tf_op jit(solution)/shard_map/ppermute | solution.py:595
  142.9 28.1 %collective-permute-start.13 = (f32[192,768]{1,0:T(8,128)}, f32[192,768]{1,0:T(8,128)}, u32[]{:S(2)}, u32[]{:S(2)}) collective-permute-start(f32[192,768]{1,0:T(8,128)} %copy-done.27), channel_id=1, source_target_pairs={{0,2},{2,0},{4,6},{6,4},{8,10},{10,8},{12,14},{14,12},{16,18},{18,... | collective-permute-start | bytes 1769480 | tf_op jit(solution)/shard_map/ppermute | solution.py:595
  142.9 28.1 %collective-permute-start.12 = (f32[512,384]{1,0:T(8,128)}, f32[512,384]{1,0:T(8,128)}, u32[]{:S(2)}, u32[]{:S(2)}) collective-permute-start(f32[512,384]{1,0:T(8,128)} %get-tuple-element.98), channel_id=1, source_target_pairs={{0,1},{1,0},{2,3},{3,2},{4,5},{5,4},{6,7},{7,6},{8,9},{9,8},{10,11... | collective-permute-start | bytes 2359304 | tf_op jit(solution)/shard_map/ppermute | solution.py:592
  147.7 1.0 copy-start.1
  147.7 1.4 copy-start.2
  153.4 40.3 %collective-permute-start.19 = (f32[192,1536]{1,0:T(8,128)}, f32[192,1536]{1,0:T(8,128)}, u32[]{:S(2)}, u32[]{:S(2)}) collective-permute-start(f32[192,1536]{1,0:T(8,128)} %get-tuple-element.103), channel_id=1, source_target_pairs={{0,4},{2,6},{4,0},{6,2},{8,12},{10,14},{12,8},{14,10},{16,20},{18,... | collective-permute-start | bytes 3538952 | tf_op jit(solution)/shard_map/ppermute | solution.py:595
  154.9 41.9 %collective-permute-start.24 = (f32[1024,384]{1,0:T(8,128)}, f32[1024,384]{1,0:T(8,128)S(1)}, u32[]{:S(2)}, u32[]{:S(2)}) collective-permute-start(f32[1024,384]{1,0:T(8,128)} %fusion.4), channel_id=1, source_target_pairs={{0,1},{1,0},{2,3},{3,2},{4,5},{5,4},{6,7},{7,6},{8,9},{9,8},{10,11... | collective-permute-start | bytes 4718600 | tf_op jit(solution)/shard_map/ppermute | solution.py:592
  169.4 30.3 %collective-permute-start.18 = (f32[96,3072]{1,0:T(8,128)}, f32[96,3072]{1,0:T(8,128)}, u32[]{:S(2)}, u32[]{:S(2)}) collective-permute-start(f32[96,3072]{1,0:T(8,128)} %get-tuple-element.173), channel_id=1, source_target_pairs={{0,8},{2,10},{4,12},{6,14},{8,0},{10,2},{12,4},{14,6},{16,24},{18,... | collective-permute-start | bytes 3538952 | tf_op jit(solution)/shard_map/ppermute | solution.py:595
  193.1 10.8 %collective-permute-start.20 = (f32[392,768]{1,0:T(8,128)}, f32[392,768]{1,0:T(8,128)S(1)}, u32[]{:S(2)}, u32[]{:S(2)}) collective-permute-start(f32[392,768]{1,0:T(8,128)} %get-tuple-element.121), channel_id=1, source_target_pairs={{0,2},{2,0},{4,6},{6,4},{8,10},{10,8},{12,14},{14,12},{16,18},{18,... | collective-permute-start | bytes 3612680 | tf_op jit(solution)/shard_map/ppermute | solution.py:595
  193.2 4.6 %copy-start = (bf16[1024,768]{1,0:T(8,128)(2,1)S(1)}, bf16[1024,768]{1,0:T(8,128)(2,1)}, u32[]{:S(2)}) copy-start(bf16[1024,768]{1,0:T(8,128)(2,1)} %get-tuple-element.125) | copy-start | bytes 4718596
  193.2 4.6 %copy-start.11 = (bf16[768,384]{1,0:T(8,128)(2,1)S(1)}, bf16[768,384]{1,0:T(8,128)(2,1)}, u32[]{:S(2)}) copy-start(bf16[768,384]{1,0:T(8,128)(2,1)} %copy-done.9) | copy-start | bytes 1769476
  193.2 10.7 %collective-permute-start.22 = (f32[392,768]{1,0:T(8,128)}, f32[392,768]{1,0:T(8,128)S(1)}, u32[]{:S(2)}, u32[]{:S(2)}) collective-permute-start(f32[392,768]{1,0:T(8,128)} %get-tuple-element.122), channel_id=1, source_target_pairs={{0,2},{2,0},{4,6},{6,4},{8,10},{10,8},{12,14},{14,12},{16,18},{18,... | collective-permute-start | bytes 3612680 | tf_op jit(solution)/shard_map/ppermute | solution.py:595
  195.6 25.2 %collective-permute-start.30 = (f32[96,1536]{1,0:T(8,128)S(1)}, f32[96,1536]{1,0:T(8,128)S(1)}, u32[]{:S(2)}, u32[]{:S(2)}) collective-permute-start(f32[96,1536]{1,0:T(8,128)S(1)} %get-tuple-element.181), channel_id=1, source_target_pairs={{0,8},{2,10},{4,12},{6,14},{8,0},{10,2},{12,4},{14,6},{16,24},{18,... | collective-permute-start | bytes 1769480 | tf_op jit(solution)/shard_map/ppermute | solution.py:595
  196.7 50.5 %collective-permute-start.17 = (f32[512,768]{1,0:T(8,128)}, f32[512,768]{1,0:T(8,128)S(1)}, u32[]{:S(2)}, u32[]{:S(2)}) collective-permute-start(f32[512,768]{1,0:T(8,128)} %get-tuple-element.115), channel_id=1, source_target_pairs={{0,1},{1,0},{2,3},{3,2},{4,5},{5,4},{6,7},{7,6},{8,9},{9,8},{10,11... | collective-permute-start | bytes 4718600 | tf_op jit(solution)/shard_map/ppermute | solution.py:592
  199.7 4.2 %copy-start.6 = (f32[392,1536]{1,0:T(8,128)S(1)}, f32[392,1536]{1,0:T(8,128)}, u32[]{:S(2)}) copy-start(f32[392,1536]{1,0:T(8,128)} %get-tuple-element.120) | copy-start | bytes 7225348
  201.3 45.0 %collective-permute-start.32 = (f32[48,3072]{1,0:T(8,128)S(1)}, f32[48,3072]{1,0:T(8,128)S(1)}, u32[]{:S(2)}, u32[]{:S(2)}) collective-permute-start(f32[48,3072]{1,0:T(8,128)S(1)} %get-tuple-element.179), channel_id=1, source_target_pairs={{0,16},{2,18},{4,20},{6,22},{8,24},{10,26},{12,28},{14,30},{16,0},... | collective-permute-start | bytes 1769480 | tf_op jit(solution)/shard_map/ppermute | solution.py:595
  204.1 17.1 %collective-permute-start.21 = (f32[200,768]{1,0:T(8,128)S(1)}, f32[200,768]{1,0:T(8,128)S(1)}, u32[]{:S(2)}, u32[]{:S(2)}) collective-permute-start(f32[200,768]{1,0:T(8,128)S(1)} %get-tuple-element.177), channel_id=1, source_target_pairs={{0,4},{2,6},{4,0},{6,2},{8,12},{10,14},{12,8},{14,10},{16,20},{18,... | collective-permute-start | bytes 1843208 | tf_op jit(solution)/shard_map/ppermute | solution.py:595
  205.7 37.4 %collective-permute-start.23 = (f32[200,768]{1,0:T(8,128)S(1)}, f32[200,768]{1,0:T(8,128)S(1)}, u32[]{:S(2)}, u32[]{:S(2)}) collective-permute-start(f32[200,768]{1,0:T(8,128)S(1)} %get-tuple-element.176), channel_id=1, source_target_pairs={{0,8},{2,10},{4,12},{6,14},{8,0},{10,2},{12,4},{14,6},{16,24},{18,... | collective-permute-start | bytes 1843208 | tf_op jit(solution)/shard_map/ppermute | solution.py:595
  220.9 27.4 %collective-permute-start.31 = (f32[48,1536]{1,0:T(8,128)S(1)}, f32[48,1536]{1,0:T(8,128)S(1)}, u32[]{:S(2)}, u32[]{:S(2)}) collective-permute-start(f32[48,1536]{1,0:T(8,128)S(1)} %get-tuple-element.184), channel_id=1, source_target_pairs={{0,16},{2,18},{4,20},{6,22},{8,24},{10,26},{12,28},{14,30},{16,0},... | collective-permute-start | bytes 884744 | tf_op jit(solution)/shard_map/ppermute | solution.py:595
  243.3 15.1 %collective-permute-start.25 = (f32[104,768]{1,0:T(8,128)S(1)}, f32[104,768]{1,0:T(8,128)S(1)}, u32[]{:S(2)}, u32[]{:S(2)}) collective-permute-start(f32[104,768]{1,0:T(8,128)S(1)} %slice_add_fusion.11), channel_id=1, source_target_pairs={{0,8},{2,10},{4,12},{6,14},{8,0},{10,2},{12,4},{14,6},{16,24},{18,... | collective-permute-start | bytes 958472 | tf_op jit(solution)/shard_map/ppermute | solution.py:595
  243.4 3.8 %copy-start.13 = (f32[512,384]{1,0:T(8,128)S(1)}, f32[512,384]{1,0:T(8,128)}, u32[]{:S(2)}) copy-start(f32[512,384]{1,0:T(8,128)} %get-tuple-element.79) | copy-start | bytes 2359300
  243.4 3.8 %copy-start.14 = (f32[512,384]{1,0:T(8,128)S(1)}, f32[512,384]{1,0:T(8,128)}, u32[]{:S(2)}) copy-start(f32[512,384]{1,0:T(8,128)} %get-tuple-element.124) | copy-start | bytes 2359300
  243.4 18.4 %collective-permute-start.27 = (f32[104,768]{1,0:T(8,128)S(1)}, f32[104,768]{1,0:T(8,128)S(1)}, u32[]{:S(2)}, u32[]{:S(2)}) collective-permute-start(f32[104,768]{1,0:T(8,128)S(1)} %slice_add_fusion.10), channel_id=1, source_target_pairs={{0,16},{2,18},{4,20},{6,22},{8,24},{10,26},{12,28},{14,30},{16,0},... | collective-permute-start | bytes 958472 | tf_op jit(solution)/shard_map/ppermute | solution.py:595
  258.4 8.9 %collective-permute-start.26 = (f32[56,768]{1,0:T(8,128)S(1)}, f32[56,768]{1,0:T(8,128)S(1)}, u32[]{:S(2)}, u32[]{:S(2)}) collective-permute-start(f32[56,768]{1,0:T(8,128)S(1)} %slice_add_fusion.17), channel_id=1, source_target_pairs={{0,16},{2,18},{4,20},{6,22},{8,24},{10,26},{12,28},{14,30},{16,0},... | collective-permute-start | bytes 516104 | tf_op jit(solution)/shard_map/ppermute | solution.py:595
  261.9 6.1 %collective-permute-start.28 = (f32[56,768]{1,0:T(8,128)S(1)}, f32[56,768]{1,0:T(8,128)S(1)}, u32[]{:S(2)}, u32[]{:S(2)}) collective-permute-start(f32[56,768]{1,0:T(8,128)S(1)} %slice_add_fusion.16), channel_id=1, source_target_pairs={{0,4},{2,6},{4,0},{6,2},{8,12},{10,14},{12,8},{14,10},{16,20},{18,... | collective-permute-start | bytes 516104 | tf_op jit(solution)/shard_map/ppermute | solution.py:595
  268.1 4.2 %collective-permute-start.29 = (f32[9,768]{1,0:T(8,128)S(1)}, f32[9,768]{1,0:T(8,128)S(1)}, u32[]{:S(2)}, u32[]{:S(2)}) collective-permute-start(f32[9,768]{1,0:T(8,128)S(1)} %pad_maximum_fusion.3), channel_id=1, source_target_pairs={{0,1},{1,0},{2,3},{3,2},{4,5},{5,4},{6,7},{7,6},{8,9},{9,8},{10,11... | collective-permute-start | bytes 82952 | tf_op jit(solution)/shard_map/ppermute | solution.py:592

commit v4 on v3

--- a/solution.py
+++ b/solution.py
@@ -509,13 +509,14 @@
     outs = refs[2 + 2 * pieces + (2 if joined else 0) :]
     share = came[0].shape[1]
     for side in range(2):
-        for piece in range(pieces):
-            start = piece * share
-            value = kept[side][:, start : start + share] + came[2 * piece + side][...]
+        wide = 3 * LANES
+        for start in range(0, pieces * share, wide):
+            inside = start % share
+            value = kept[side][:, start : start + wide] + came[2 * (start // share) + side][:, inside : inside + wide]
             if start < split:
-                outs[side][:, start : start + share] = value
+                outs[side][:, start : start + wide] = value
             else:
-                outs[2 + side][:, start - split : start - split + share] = value
+                outs[2 + side][:, start - split : start - split + wide] = value
         if joined:
             outs[side][:, pieces * share :] = refs[2 + 2 * pieces + side][...]
 
@@ -621,7 +622,7 @@
     sine = jnp.sin(angles)
 
     bits = [1 << at for at in range(dp_size.bit_length() - 1)]
-    far_first = bits[:1] + bits[2:] + bits[1:2]
+    far_first = bits
     order = [bits] if slab % 16 == 0 else None
     mixed_order = [bits, bits, far_first] if slab % 16 == 0 else None
 
@@ -813,7 +814,7 @@
         )
     )
     came_mlp = [across(piece, 1) for piece in mlp[1]]
-    first = add_sent("add_mlp", mlp[0], came_mlp)
+    *first, late_kept, late_sent = add_sent("add_mlp", mlp[0], came_mlp, split=7 * hidden // 4)
     (
         grad_two,
         grad_query,
@@ -869,7 +870,7 @@
     store_keep = dot_t(grad_store, own_kv)
     cross = sorted_halves(*cross_halves)
     came_cross = [across(piece, 1) for piece in cross[1]]
-    third = add_sent("add_cross", cross[0], came_cross)
+    third = add_sent("add_cross", cross[0], came_cross, (late_kept, late_sent))
     store_back = swap(after(store_send, third[1]))
 
     tok_keep, both_send, *self_halves = call(
@@ -921,7 +922,6 @@
         flops=40_000_000_000,
     )
     back = swap(both_send)
-    neighbours_grad = (store_keep + store_back).astype(BF16)
 
     first = halve(after(first[0], self_halves[0]), first[1], bits[2])
     third_came = across(third[1], bits[1])
@@ -942,6 +942,8 @@
 
     near_part = ride_core(kept[:, :middle], sent[0])
     far_part = ride_core(kept[:, middle:], sent[1])
+    store_back = after(store_back, near_part[1], far_part[1])
+    neighbours_grad = (store_keep + store_back).astype(BF16)
     third = after(third[0], near_part[1], far_part[1]), third[1]
     first = after(first[0], near_part[1], far_part[1]), first[1]
     near_part = ride_on(*near_part, bits[1])
@@ -962,8 +964,10 @@
         return after(parts[0], *done) + across(parts[1], order[-1])
 
     mlp_grads = finish(first, bits[3:])
-    cross_grads = finish(third, bits[2:])
-    mlp_out_w_grad, mlp_in_w_grad = mlp_grads[:, :hidden], mlp_grads[:, hidden:]
+    third = finish(third, bits[2:])
+    cross_grads = third[:, : 4 * local]
+    mlp_out_w_grad = mlp_grads[:, :hidden]
+    mlp_in_w_grad = jnp.concatenate([mlp_grads[:, hidden:], third[:, 4 * local :]], axis=1)
 
     shared = 0.5 * sums[2:9]
     shared = jnp.concatenate([sums[0:2], shared], axis=0)

time: 275 us -> 267 us (0.971)
  waiting for transfers between devices: 104 us -> 96.2 us
    ppermute x23, waiting for transfers between devices: 68.4 us -> 60 us  [across(): return lax.ppermute(value, 'dp', [(at, at ^ bit) for at in range(dp_size)])]
  transfers between devices with their start and end apart: 33 -> 33, of which waited for: 15 -> 18; matrix products, arithmetic and copies ran while one was open for 11% -> 11% of each run, Pallas kernels for 37% -> 38%
where the time goes in v4:
time: 267 us; the launch traced here: 266 us
  Pallas kernels  102 us (38%)
  waiting for transfers between devices  96.2 us (36%)
  starting transfers between devices  28.9 us (11%)
  local copies, waits for them, and re-layouts  15.8 us (6%)
  other arithmetic  13.5 us (5%)
  matrix products  8.02 us (3%)
    pallas_call x5, Pallas kernels, call(): pl.pallas_call(body, name=name, out_shape=outs, in_specs=scalars(len(smal...  77.6 us
    ppermute x23, waiting for transfers between devices, across(): return lax.ppermute(value, 'dp', [(at, at ^ bit) for at in range(dp_size)])  60 us
    ppermute x10, waiting for transfers between devices, swap(): return lax.ppermute(value, 'tp', [(0, 1), (1, 0)])  36.2 us
    ppermute x23, starting transfers between devices, across(): return lax.ppermute(value, 'dp', [(at, at ^ bit) for at in range(dp_size)])  17.3 us
    pallas_call x1, Pallas kernels, per_device(): pl.pallas_call(feed_forward, name='feed_forward', grid=(count // step,),...  13.7 us
    ppermute x10, starting transfers between devices, swap(): return lax.ppermute(value, 'tp', [(0, 1), (1, 0)])  11.6 us
    pallas_call x2, Pallas kernels, add_sent(): pl.pallas_call(partial(add_halves, len(came), bool(joined), split), name=...  10.7 us
    add x4, other arithmetic, merge(): return (kept[:half] + arrived[:half], kept[half:] + arrived[half:])  6.64 us
  transfers between devices with their start and end apart: 33, of which 18 were waited for; matrix products, arithmetic and copies ran while one was open for 11% of the time, Pallas kernels for 38%

profile of v4, /device:TPU:0, one launch (start us, length us, event | category | flops | bytes accessed | tf_op | source)
XLA Modules:
  0.0 266.3 jit_solution(2214778494650255355)
XLA Ops:
  0.7 1.0 dynamic-slice_convert_fusion.1
  1.7 3.1 %collective-permute-start.1 = (f32[192,768]{1,0:T(8,128)S(1)}, f32[192,768]{1,0:T(8,128)}, u32[]{:S(2)}, u32[]{:S(2)}) collective-permute-start(f32[192,768]{1,0:T(8,128)S(1)} %dynamic-slice_convert_fusion.1), channel_id=1, source_target_pairs={{0,1},{1,0},{2,3},{3,2},{4,5},{5,4},{6,7},{7,6},{8,9},{9,8},{10,11... | collective-permute-start | bytes 1769480 | tf_op jit(solution)/shard_map/ppermute | solution.py:593
  5.7 1.8 multiply_sine_fusion
  7.5 1.2 concatenate.33.info
  8.7 10.5 %self_forward.1 = (bf16[512,768]{1,0:T(8,128)(2,1)}, bf16[9,512,128]{2,1,0:T(8,128)(2,1)}, f32[512,384]{1,0:T(8,128)}, f32[512,128]{1,0:T(8,128)}, f32[512,512]{1,0:T(8,128)}) custom-call(s32[8]{0:T(128)} %concatenate.33.info, bf16[512,768]{1,0:T(8,128)(2,1)} %tok.5, bf16[3,768,384]{2,1,0:T(8,128)(2,1)} %bitcast.39, f32[3,384]{1,0:T(4,128)} %bias.1, ...), custom_call_target="tpu_custom_call" | custom-call | flops 11000000512 | bytes 1 | tf_op jit(solution)/shard_map/self_forward/pallas_call | solution.py:545
  19.9 0.7 copy.49.picks
  22.0 1.5 copy-done.24
  23.5 2.6 fusion.kv
  26.1 12.5 %collective-permute-done.mix_peer = f32[512,384]{1,0:T(8,128)} collective-permute-done((f32[512,384]{1,0:T(8,128)}, f32[512,384]{1,0:T(8,128)}, u32[]{:S(2)}, u32[]{:S(2)}) %collective-permute-start) | collective-permute-done | bytes 786464 | tf_op jit(solution)/shard_map/ppermute | solution.py:593
  38.9 0.9 copy-done.28
  39.8 13.8 %cross_forward.1 = (f32[512,768]{1,0:T(8,128)}, bf16[512,768]{1,0:T(8,128)(2,1)}, bf16[512,384]{1,0:T(8,128)(2,1)}, f32[512,384]{1,0:T(8,128)}, f32[512,128]{1,0:T(8,128)}) custom-call(s32[8]{0:T(128)} %concatenate.33.info, s32[8,2]{1,0:T(8,128)} %copy.49.picks, bf16[512,768]{1,0:T(8,128)(2,1)} %tok.5, f32[512,384]{1,0:T(8,128)} %get-tuple-element.78.mix_own.mix, ...), custom_call_target="tpu_custom_call" | custom-call | flops 14000000000 | bytes 1 | tf_op jit(solution)/shard_map/cross_forward/pallas_call | solution.py:545
  53.6 1.7 collective-permute-start.3
  55.3 0.7 reshape.103.in_b
  57.5 14.4 %collective-permute-done.3.mix_peer = f32[512,384]{1,0:T(8,128)S(1)} collective-permute-done((f32[512,384]{1,0:T(8,128)}, f32[512,384]{1,0:T(8,128)S(1)}, u32[]{:S(2)}, u32[]{:S(2)}) %collective-permute-start.3) | collective-permute-done | bytes 786464 | tf_op jit(solution)/shard_map/ppermute | solution.py:593
  71.9 1.5 collective-permute-start.7
  73.4 13.7 %feed_forward.1 = (f32[512,768]{1,0:T(8,128)}, bf16[512,768]{1,0:T(8,128)(2,1)}, bf16[512,1536]{1,0:T(8,128)(2,1)}, bf16[512,1536]{1,0:T(8,128)(2,1)}, f32[512,3...) custom-call(s32[8]{0:T(128)} %concatenate.33.info, ...), custom_call_target="tpu_custom_call" | custom-call | flops 14000000000 | bytes 1 | tf_op jit(solution)/shard_map/feed_forward/pallas_call | solution.py:757
  87.1 0.9 collective-permute-start.6
  87.9 9.4 %mlp_grads.1 = (f32[384,3072]{1,0:T(8,128)}, f32[384,768]{1,0:T(8,128)}, f32[384,768]{1,0:T(8,128)}, f32[384,768]{1,0:T(8,128)}, f32[384,768]{1,0:T(8,128)}) custom-call(s32[8]{0:T(128)} %concatenate.33.info, bf16[512,768]{1,0:T(8,128)(2,1)} %out_grad.1, bf16[512,768]{1,0:T(8,128)(2,1)} %get-tuple-element.87.refs_1_, ...), custom_call_target="tpu_custom_call" | custom-call | bytes 1 | tf_op jit(solution)/shard_map/mlp_grads/pallas_call | solution.py:545
  98.4 2.0 collective-permute-done.10.refs_6_.refs_7_
  100.4 1.7 collective-permute-done.11.refs_8_.refs_9_
  102.1 1.7 collective-permute-done.8.refs_2_.refs_3_
  103.8 1.8 collective-permute-done.9.refs_4_.refs_5_
  105.6 6.1 %add_mlp.1 = (f32[192,2688]{1,0:T(8,128)}, f32[192,2688]{1,0:T(8,128)}, f32[192,384]{1,0:T(8,128)}, f32[192,384]{1,0:T(8,128)}) custom-call(f32[384,3072]{1,0:T(8,128)} %get-tuple-element.90.refs_0_.refs_1_, f32[384,3072]{1,0:T(8,128)} %get-tuple-element.90.refs_0_.refs_1_, f32[384,768]{1,0:T(8,128)} %copy-done.5, f32[384,768]{1,0:T(8,128)} %copy-done.5, ...), custom_call_target="tpu_custom_call" | custom-call | bytes 1 | tf_op jit(solution)/shard_map/add_mlp/pallas_call | solution.py:645
  111.7 1.6 collective-permute-start.16
  113.2 7.8 %collective-permute-done.6.part_peer = f32[512,768]{1,0:T(8,128)} collective-permute-done((f32[512,768]{1,0:T(8,128)}, f32[512,768]{1,0:T(8,128)}, u32[]{:S(2)}, u32[]{:S(2)}) %collective-permute-start.6) | collective-permute-done | bytes 1572896 | tf_op jit(solution)/shard_map/ppermute | solution.py:593
  121.0 21.9 %cross_backward.1 = (f32[512,768]{1,0:T(8,128)}, f32[512,384]{1,0:T(8,128)}, bf16[512,384]{1,0:T(8,128)(2,1)}, bf16[1024,768]{1,0:T(8,128)(2,1)}, f32[8,768]{1,0...) custom-call(s32[8]{0:T(128)} %concatenate.33.info, ...), custom_call_target="tpu_custom_call" | custom-call | flops 16999999488 | bytes 1 | tf_op jit(solution)/shard_map/cross_backward/pallas_call | solution.py:545
  143.5 1.1 collective-permute-start.12
  144.6 3.6 %fusion.4 = f32[1024,384]{1,0:T(8,128)} fusion(bf16[1024,768]{1,0:T(8,128)(2,1)} %get-tuple-element.130, s32[]{:T(128)S(6)} %select_n.40, bf16[768,384]{1,0:T(8,128)(2,1)S(1)} %copy-done.8, bf16[768,384]{1,0:T(8,128)(2,1)S(1)} %copy-done.10), kind=kOutput, calls=%fused_computation.19 | convolution fusion | flops 605159424 | bytes 4325380 | tf_op jit(solution)/shard_map/dot_general | solution.py:25
  148.1 1.0 copy-done.1
  149.5 4.6 %add_cross.1 = (f32[192,1920]{1,0:T(8,128)}, f32[192,1920]{1,0:T(8,128)}) custom-call(f32[384,1536]{1,0:T(8,128)} %get-tuple-element.103.refs_0_.refs_1_, f32[384,1536]{1,0:T(8,128)} %get-tuple-element.103.refs_0_.refs_1_, f32[384,768]{1,0:T(8,128)} %copy-done.1, f32[384,768]{1,0:T(8,128)} %copy-done.1, f32[384,768]{1,0:T(8,128)} %copy-done.2, ...), custom_call_target="tpu_custom_call" | custom-call | bytes 1 | tf_op jit(solution)/shard_map/add_cross/pallas_call | solution.py:645
  154.1 1.5 collective-permute-start.19
  155.6 0.9 collective-permute-start.24
  156.5 3.3 %collective-permute-done.16 = f32[192,2688]{1,0:T(8,128)} collective-permute-done((f32[192,2688]{1,0:T(8,128)}, f32[192,2688]{1,0:T(8,128)}, u32[]{:S(2)}, u32[]{:S(2)}) %collective-permute-start.16) | collective-permute-done | bytes 2064416 | tf_op jit(solution)/shard_map/ppermute | solution.py:596
  159.9 3.3 %slice_add_fusion = (f32[96,2688]{1,0:T(8,128)S(1)}, f32[96,2688]{1,0:T(8,128)}) fusion(f32[192,2688]{1,0:T(8,128)} %collective-permute-done.16, f32[192,2688]{1,0:T(8,128)} %get-tuple-element.109), kind=kLoop, calls=%fused_computation.9 | loop fusion | flops 516096 | bytes 6193152 | tf_op jit(solution)/shard_map/add | solution.py:690
  163.2 1.6 collective-permute-start.18
  164.8 22.1 %self_backward.1 = (f32[512,384]{1,0:T(8,128)}, f32[512,768]{1,0:T(8,128)}, f32[392,1536]{1,0:T(8,128)}, f32[392,768]{1,0:T(8,128)}, f32[392,768]{1,0:T(8,128)}) custom-call(s32[8]{0:T(128)} %concatenate.33.info, bf16[512,384]{1,0:T(8,128)(2,1)} %get-tuple-element.100.query_own, f32[512,384]{1,0:T(8,128)} %collective-permute-done.12.query_peer, ...), custom_call_target="tpu_custom_call" | custom-call | flops 40000000000 | bytes 1 | tf_op jit(solution)/shard_map/self_backward/pallas_call | solution.py:545
  187.5 3.1 %collective-permute-done.19 = f32[192,1920]{1,0:T(8,128)} collective-permute-done((f32[192,1920]{1,0:T(8,128)}, f32[192,1920]{1,0:T(8,128)}, u32[]{:S(2)}, u32[]{:S(2)}) %collective-permute-start.19) | collective-permute-done | bytes 1474592 | tf_op jit(solution)/shard_map/ppermute | solution.py:596
  190.6 1.2 collective-permute-start.17
  191.8 1.9 slice_add_fusion.2
  193.8 1.6 collective-permute-start.30
  195.4 1.3 slice_add_fusion.8
  196.8 2.6 collective-permute-start.32
  199.6 1.6 collective-permute-start.21
  201.7 1.9 add_convert_fusion.1
  203.9 18.4 %collective-permute-done.30 = f32[96,1920]{1,0:T(8,128)S(1)} collective-permute-done((f32[96,1920]{1,0:T(8,128)S(1)}, f32[96,1920]{1,0:T(8,128)S(1)}, u32[]{:S(2)}, u32[]{:S(2)}) %collective-permute-start.30) | collective-permute-done | bytes 737312 | tf_op jit(solution)/shard_map/ppermute | solution.py:596
  222.4 1.7 collective-permute-start.31
  224.1 2.9 %collective-permute-done.23 = f32[200,768]{1,0:T(8,128)S(1)} collective-permute-done((f32[200,768]{1,0:T(8,128)S(1)}, f32[200,768]{1,0:T(8,128)S(1)}, u32[]{:S(2)}, u32[]{:S(2)}) %collective-permute-start.23) | collective-permute-done | bytes 614432 | tf_op jit(solution)/shard_map/ppermute | solution.py:596
  227.2 0.6 collective-permute-start.25
  227.9 1.5 collective-permute-start.27
  229.5 0.7 slice_bitcast_fusion.2
  230.2 0.7 collective-permute-done.17
  231.0 1.0 add_convert_fusion.2
  232.0 8.2 %collective-permute-done.31 = f32[48,1920]{1,0:T(8,128)S(1)} collective-permute-done((f32[48,1920]{1,0:T(8,128)S(1)}, f32[48,1920]{1,0:T(8,128)S(1)}, u32[]{:S(2)}, u32[]{:S(2)}) %collective-permute-start.31) | collective-permute-done | bytes 368672 | tf_op jit(solution)/shard_map/ppermute | solution.py:596
  240.3 0.7 fusion.18
  241.0 0.7 pad_maximum_fusion.2
  241.7 0.7 reshape.108
  242.5 2.2 collective-permute-done.25
  244.8 4.9 %collective-permute-done.27 = f32[104,768]{1,0:T(8,128)S(1)} collective-permute-done((f32[104,768]{1,0:T(8,128)S(1)}, f32[104,768]{1,0:T(8,128)S(1)}, u32[]{:S(2)}, u32[]{:S(2)}) %collective-permute-start.27) | collective-permute-done | bytes 319520 | tf_op jit(solution)/shard_map/ppermute | solution.py:596
  249.8 8.0 %collective-permute-done.26 = f32[56,768]{1,0:T(8,128)S(1)} collective-permute-done((f32[56,768]{1,0:T(8,128)S(1)}, f32[56,768]{1,0:T(8,128)S(1)}, u32[]{:S(2)}, u32[]{:S(2)}) %collective-permute-start.26) | collective-permute-done | bytes 172064 | tf_op jit(solution)/shard_map/ppermute | solution.py:596
  257.8 0.6 slice_bitcast_fusion.4
  258.5 1.6 collective-permute-done.28
  260.2 0.9 collective-permute-start.29
  262.3 0.7 copy.59
  263.6 0.8 collective-permute-done.29
  (136 shorter events, 12.1 us)
Async XLA Ops:
  1.7 20.1 %collective-permute-start.1 = (f32[192,768]{1,0:T(8,128)S(1)}, f32[192,768]{1,0:T(8,128)}, u32[]{:S(2)}, u32[]{:S(2)}) collective-permute-start(f32[192,768]{1,0:T(8,128)S(1)} %dynamic-slice_convert_fusion.1), channel_id=1, source_target_pairs={{0,1},{1,0},{2,3},{3,2},{4,5},{5,4},{6,7},{7,6},{8,9},{9,8},{10,11... | collective-permute-start | bytes 1769480 | tf_op jit(solution)/shard_map/ppermute | solution.py:593
  8.7 10.6 %copy-start.12 = (bf16[768,2,384]{2,1,0:T(2,128)(2,1)S(1)}, bf16[768,2,384]{2,1,0:T(2,128)(2,1)}, u32[]{:S(2)}) copy-start(bf16[768,2,384]{2,1,0:T(2,128)(2,1)} %param.36) | copy-start | bytes 3538948
  19.2 0.7 copy-start.23
  19.2 1.4 copy-start.18
  19.2 1.9 copy-start.21
  19.2 2.5 copy-start.22
  19.2 2.5 copy-start.16
  19.2 19.4 %collective-permute-start = (f32[512,384]{1,0:T(8,128)}, f32[512,384]{1,0:T(8,128)}, u32[]{:S(2)}, u32[]{:S(2)}) collective-permute-start(f32[512,384]{1,0:T(8,128)} %get-tuple-element.78.mix_own.mix), channel_id=1, source_target_pairs={{0,1},{1,0},{2,3},{3,2},{4,5},{5,4},{6,7},{7,6},{8,9},{9,8},{10,11... | collective-permute-start | bytes 2359304 | tf_op jit(solution)/shard_map/ppermute | solution.py:593
  21.7 1.8 copy-start.24
  21.8 17.1 %collective-permute-start.2 = (f32[192,768]{1,0:T(8,128)}, f32[192,768]{1,0:T(8,128)S(1)}, u32[]{:S(2)}, u32[]{:S(2)}) collective-permute-start(f32[192,768]{1,0:T(8,128)} %collective-permute-done.1.w_near), channel_id=1, source_target_pairs={{0,2},{2,0},{4,6},{6,4},{8,10},{10,8},{12,14},{14,12},{16,18},{18,... | collective-permute-start | bytes 1769480 | tf_op jit(solution)/shard_map/ppermute | solution.py:596
  22.0 4.1 %copy-start.7 = (bf16[768,384]{1,0:T(8,128)(2,1)}, bf16[768,384]{1,0:T(8,128)(2,1)S(1)}, u32[]{:S(2)}) copy-start(bf16[768,384]{1,0:T(8,128)(2,1)S(1)} %get-tuple-element.192) | copy-start | bytes 1769476
  22.0 4.1 %copy-start.9 = (bf16[768,384]{1,0:T(8,128)(2,1)}, bf16[768,384]{1,0:T(8,128)(2,1)S(1)}, u32[]{:S(2)}) copy-start(bf16[768,384]{1,0:T(8,128)(2,1)S(1)} %get-tuple-element.193) | copy-start | bytes 1769476
  26.1 29.2 %copy-start.17 = (f32[1536]{0:T(1024)S(1)}, f32[1536]{0:T(1024)}, u32[]{:S(2)}) copy-start(f32[1536]{0:T(1024)} %param.41) | copy-start | bytes 18436
  26.1 29.9 %copy-start.19 = (f32[768]{0:T(1024)S(1)}, f32[768]{0:T(1024)}, u32[]{:S(2)}) copy-start(f32[768]{0:T(1024)} %param.39) | copy-start | bytes 9220
  26.1 30.5 %copy-start.20 = (f32[768]{0:T(1024)S(1)}, f32[768]{0:T(1024)}, u32[]{:S(2)}) copy-start(f32[768]{0:T(1024)} %param.43) | copy-start | bytes 9220
  26.1 31.0 %copy-start.15 = (bf16[768,384]{1,0:T(8,128)(2,1)S(1)}, bf16[768,384]{1,0:T(8,128)(2,1)}, u32[]{:S(2)}) copy-start(bf16[768,384]{1,0:T(8,128)(2,1)} %q_w.3) | copy-start | bytes 1769476
  38.6 16.7 %collective-permute-start.4 = (f32[192,768]{1,0:T(8,128)S(1)}, f32[192,768]{1,0:T(8,128)S(1)}, u32[]{:S(2)}, u32[]{:S(2)}) collective-permute-start(f32[192,768]{1,0:T(8,128)S(1)} %dynamic-slice_convert_fusion), channel_id=1, source_target_pairs={{0,1},{1,0},{2,3},{3,2},{4,5},{5,4},{6,7},{7,6},{8,9},{9,8},{10,11... | collective-permute-start | bytes 1769480 | tf_op jit(solution)/shard_map/ppermute | solution.py:593
  38.9 0.9 copy-start.28
  53.6 18.4 %collective-permute-start.3 = (f32[512,384]{1,0:T(8,128)}, f32[512,384]{1,0:T(8,128)S(1)}, u32[]{:S(2)}, u32[]{:S(2)}) collective-permute-start(f32[512,384]{1,0:T(8,128)} %get-tuple-element.80.mix_own.mix), channel_id=1, source_target_pairs={{0,1},{1,0},{2,3},{3,2},{4,5},{5,4},{6,7},{7,6},{8,9},{9,8},{10,11... | collective-permute-start | bytes 2359304 | tf_op jit(solution)/shard_map/ppermute | solution.py:593
  55.3 18.1 %copy-start.27 = (f32[192,768]{1,0:T(8,128)}, f32[192,768]{1,0:T(8,128)S(1)}, u32[]{:S(2)}) copy-start(f32[192,768]{1,0:T(8,128)S(1)} %collective-permute-done.4.w_near) | copy-start | bytes 1769476
  55.3 18.1 %collective-permute-start.5 = (f32[192,768]{1,0:T(8,128)S(1)}, f32[192,768]{1,0:T(8,128)}, u32[]{:S(2)}, u32[]{:S(2)}) collective-permute-start(f32[192,768]{1,0:T(8,128)S(1)} %collective-permute-done.4.w_near), channel_id=1, source_target_pairs={{0,2},{2,0},{4,6},{6,4},{8,10},{10,8},{12,14},{14,12},{16,18},{18,... | collective-permute-start | bytes 1769480 | tf_op jit(solution)/shard_map/ppermute | solution.py:596
  71.9 1.5 copy-start.25
  71.9 16.0 %collective-permute-start.7 = (f32[192,768]{1,0:T(8,128)S(1)}, f32[192,768]{1,0:T(8,128)S(1)}, u32[]{:S(2)}, u32[]{:S(2)}) collective-permute-start(f32[192,768]{1,0:T(8,128)S(1)} %convert_bitcast_fusion), channel_id=1, source_target_pairs={{0,1},{1,0},{2,3},{3,2},{4,5},{5,4},{6,7},{7,6},{8,9},{9,8},{10,11... | collective-permute-start | bytes 1769480 | tf_op jit(solution)/shard_map/ppermute | solution.py:593
  87.1 34.0 %collective-permute-start.6 = (f32[512,768]{1,0:T(8,128)}, f32[512,768]{1,0:T(8,128)}, u32[]{:S(2)}, u32[]{:S(2)}) collective-permute-start(f32[512,768]{1,0:T(8,128)} %get-tuple-element.83.part_own), channel_id=1, source_target_pairs={{0,1},{1,0},{2,3},{3,2},{4,5},{5,4},{6,7},{7,6},{8,9},{9,8},{10,11... | collective-permute-start | bytes 4718600 | tf_op jit(solution)/shard_map/ppermute | solution.py:593
  87.9 9.4 %copy-start.26 = (f32[192,768]{1,0:T(8,128)}, f32[192,768]{1,0:T(8,128)S(1)}, u32[]{:S(2)}) copy-start(f32[192,768]{1,0:T(8,128)S(1)} %collective-permute-done.7.q_near) | copy-start | bytes 1769476
  97.4 3.1 %collective-permute-start.10 = (f32[384,768]{1,0:T(8,128)}, f32[384,768]{1,0:T(8,128)S(1)}, u32[]{:S(2)}, u32[]{:S(2)}) collective-permute-start(f32[384,768]{1,0:T(8,128)} %get-tuple-element.93), channel_id=1, source_target_pairs={{0,2},{2,0},{4,6},{6,4},{8,10},{10,8},{12,14},{14,12},{16,18},{18,... | collective-permute-start | bytes 3538952 | tf_op jit(solution)/shard_map/ppermute | solution.py:596
  97.4 4.7 %collective-permute-start.11 = (f32[384,768]{1,0:T(8,128)}, f32[384,768]{1,0:T(8,128)S(1)}, u32[]{:S(2)}, u32[]{:S(2)}) collective-permute-start(f32[384,768]{1,0:T(8,128)} %get-tuple-element.94), channel_id=1, source_target_pairs={{0,2},{2,0},{4,6},{6,4},{8,10},{10,8},{12,14},{14,12},{16,18},{18,... | collective-permute-start | bytes 3538952 | tf_op jit(solution)/shard_map/ppermute | solution.py:596
  97.9 5.9 %collective-permute-start.8 = (f32[384,768]{1,0:T(8,128)}, f32[384,768]{1,0:T(8,128)S(1)}, u32[]{:S(2)}, u32[]{:S(2)}) collective-permute-start(f32[384,768]{1,0:T(8,128)} %get-tuple-element.91), channel_id=1, source_target_pairs={{0,2},{2,0},{4,6},{6,4},{8,10},{10,8},{12,14},{14,12},{16,18},{18,... | collective-permute-start | bytes 3538952 | tf_op jit(solution)/shard_map/ppermute | solution.py:596
  97.9 7.7 %collective-permute-start.9 = (f32[384,768]{1,0:T(8,128)}, f32[384,768]{1,0:T(8,128)}, u32[]{:S(2)}, u32[]{:S(2)}) collective-permute-start(f32[384,768]{1,0:T(8,128)} %get-tuple-element.92), channel_id=1, source_target_pairs={{0,2},{2,0},{4,6},{6,4},{8,10},{10,8},{12,14},{14,12},{16,18},{18,... | collective-permute-start | bytes 3538952 | tf_op jit(solution)/shard_map/ppermute | solution.py:596
  100.4 5.2 %copy-start.3 = (f32[384,768]{1,0:T(8,128)}, f32[384,768]{1,0:T(8,128)S(1)}, u32[]{:S(2)}) copy-start(f32[384,768]{1,0:T(8,128)S(1)} %collective-permute-done.10.refs_6_.refs_7_) | copy-start | bytes 3538948
  102.1 3.5 %copy-start.4 = (f32[384,768]{1,0:T(8,128)}, f32[384,768]{1,0:T(8,128)S(1)}, u32[]{:S(2)}) copy-start(f32[384,768]{1,0:T(8,128)S(1)} %collective-permute-done.11.refs_8_.refs_9_) | copy-start | bytes 3538948
  103.8 1.8 copy-start.5
  111.7 48.2 %collective-permute-start.16 = (f32[192,2688]{1,0:T(8,128)}, f32[192,2688]{1,0:T(8,128)}, u32[]{:S(2)}, u32[]{:S(2)}) collective-permute-start(f32[192,2688]{1,0:T(8,128)} %get-tuple-element.95), channel_id=1, source_target_pairs={{0,4},{2,6},{4,0},{6,2},{8,12},{10,14},{12,8},{14,10},{16,20},{18,... | collective-permute-start | bytes 6193160 | tf_op jit(solution)/shard_map/ppermute | solution.py:596
  121.0 23.5 %copy-start.8 = (bf16[768,384]{1,0:T(8,128)(2,1)S(1)}, bf16[768,384]{1,0:T(8,128)(2,1)}, u32[]{:S(2)}) copy-start(bf16[768,384]{1,0:T(8,128)(2,1)} %copy-done.7) | copy-start | bytes 1769476
  121.0 23.5 %copy-start.10 = (bf16[768,384]{1,0:T(8,128)(2,1)S(1)}, bf16[768,384]{1,0:T(8,128)(2,1)}, u32[]{:S(2)}) copy-start(bf16[768,384]{1,0:T(8,128)(2,1)} %copy-done.9) | copy-start | bytes 1769476
  142.9 5.2 %collective-permute-start.14 = (f32[384,768]{1,0:T(8,128)}, f32[384,768]{1,0:T(8,128)S(1)}, u32[]{:S(2)}, u32[]{:S(2)}) collective-permute-start(f32[384,768]{1,0:T(8,128)} %get-tuple-element.104), channel_id=1, source_target_pairs={{0,2},{2,0},{4,6},{6,4},{8,10},{10,8},{12,14},{14,12},{16,18},{18,... | collective-permute-start | bytes 3538952 | tf_op jit(solution)/shard_map/ppermute | solution.py:596
  142.9 5.2 %collective-permute-start.15 = (f32[384,768]{1,0:T(8,128)}, f32[384,768]{1,0:T(8,128)S(1)}, u32[]{:S(2)}, u32[]{:S(2)}) collective-permute-start(f32[384,768]{1,0:T(8,128)} %get-tuple-element.105), channel_id=1, source_target_pairs={{0,2},{2,0},{4,6},{6,4},{8,10},{10,8},{12,14},{14,12},{16,18},{18,... | collective-permute-start | bytes 3538952 | tf_op jit(solution)/shard_map/ppermute | solution.py:596
  143.4 21.4 %collective-permute-start.13 = (f32[192,768]{1,0:T(8,128)}, f32[192,768]{1,0:T(8,128)}, u32[]{:S(2)}, u32[]{:S(2)}) collective-permute-start(f32[192,768]{1,0:T(8,128)} %copy-done.26), channel_id=1, source_target_pairs={{0,2},{2,0},{4,6},{6,4},{8,10},{10,8},{12,14},{14,12},{16,18},{18,... | collective-permute-start | bytes 1769480 | tf_op jit(solution)/shard_map/ppermute | solution.py:596
  143.5 21.3 %collective-permute-start.12 = (f32[512,384]{1,0:T(8,128)}, f32[512,384]{1,0:T(8,128)}, u32[]{:S(2)}, u32[]{:S(2)}) collective-permute-start(f32[512,384]{1,0:T(8,128)} %get-tuple-element.101), channel_id=1, source_target_pairs={{0,1},{1,0},{2,3},{3,2},{4,5},{5,4},{6,7},{7,6},{8,9},{9,8},{10,11... | collective-permute-start | bytes 2359304 | tf_op jit(solution)/shard_map/ppermute | solution.py:593
  148.1 1.0 copy-start.1
  148.1 1.4 copy-start.2
  154.1 36.5 %collective-permute-start.19 = (f32[192,1920]{1,0:T(8,128)}, f32[192,1920]{1,0:T(8,128)}, u32[]{:S(2)}, u32[]{:S(2)}) collective-permute-start(f32[192,1920]{1,0:T(8,128)} %get-tuple-element.108), channel_id=1, source_target_pairs={{0,4},{2,6},{4,0},{6,2},{8,12},{10,14},{12,8},{14,10},{16,20},{18,... | collective-permute-start | bytes 4423688 | tf_op jit(solution)/shard_map/ppermute | solution.py:596
  155.6 45.6 %collective-permute-start.24 = (f32[1024,384]{1,0:T(8,128)}, f32[1024,384]{1,0:T(8,128)S(1)}, u32[]{:S(2)}, u32[]{:S(2)}) collective-permute-start(f32[1024,384]{1,0:T(8,128)} %fusion.4), channel_id=1, source_target_pairs={{0,1},{1,0},{2,3},{3,2},{4,5},{5,4},{6,7},{7,6},{8,9},{9,8},{10,11... | collective-permute-start | bytes 4718600 | tf_op jit(solution)/shard_map/ppermute | solution.py:593
  163.2 30.6 %collective-permute-start.18 = (f32[96,2688]{1,0:T(8,128)}, f32[96,2688]{1,0:T(8,128)}, u32[]{:S(2)}, u32[]{:S(2)}) collective-permute-start(f32[96,2688]{1,0:T(8,128)} %get-tuple-element.179), channel_id=1, source_target_pairs={{0,8},{2,10},{4,12},{6,14},{8,0},{10,2},{12,4},{14,6},{16,24},{18,... | collective-permute-start | bytes 3096584 | tf_op jit(solution)/shard_map/ppermute | solution.py:596
  186.9 9.8 %collective-permute-start.20 = (f32[392,768]{1,0:T(8,128)}, f32[392,768]{1,0:T(8,128)S(1)}, u32[]{:S(2)}, u32[]{:S(2)}) collective-permute-start(f32[392,768]{1,0:T(8,128)} %get-tuple-element.126), channel_id=1, source_target_pairs={{0,2},{2,0},{4,6},{6,4},{8,10},{10,8},{12,14},{14,12},{16,18},{18,... | collective-permute-start | bytes 3612680 | tf_op jit(solution)/shard_map/ppermute | solution.py:596
  187.0 12.4 %collective-permute-start.22 = (f32[392,768]{1,0:T(8,128)}, f32[392,768]{1,0:T(8,128)S(1)}, u32[]{:S(2)}, u32[]{:S(2)}) collective-permute-start(f32[392,768]{1,0:T(8,128)} %get-tuple-element.127), channel_id=1, source_target_pairs={{0,2},{2,0},{4,6},{6,4},{8,10},{10,8},{12,14},{14,12},{16,18},{18,... | collective-permute-start | bytes 3612680 | tf_op jit(solution)/shard_map/ppermute | solution.py:596
  190.6 40.4 %collective-permute-start.17 = (f32[512,768]{1,0:T(8,128)}, f32[512,768]{1,0:T(8,128)S(1)}, u32[]{:S(2)}, u32[]{:S(2)}) collective-permute-start(f32[512,768]{1,0:T(8,128)} %get-tuple-element.120), channel_id=1, source_target_pairs={{0,1},{1,0},{2,3},{3,2},{4,5},{5,4},{6,7},{7,6},{8,9},{9,8},{10,11... | collective-permute-start | bytes 4718600 | tf_op jit(solution)/shard_map/ppermute | solution.py:593
  193.8 5.6 %copy-start.6 = (f32[392,1536]{1,0:T(8,128)S(1)}, f32[392,1536]{1,0:T(8,128)}, u32[]{:S(2)}) copy-start(f32[392,1536]{1,0:T(8,128)} %get-tuple-element.125) | copy-start | bytes 7225348
  193.8 28.5 %collective-permute-start.30 = (f32[96,1920]{1,0:T(8,128)S(1)}, f32[96,1920]{1,0:T(8,128)S(1)}, u32[]{:S(2)}, u32[]{:S(2)}) collective-permute-start(f32[96,1920]{1,0:T(8,128)S(1)} %get-tuple-element.181), channel_id=1, source_target_pairs={{0,8},{2,10},{4,12},{6,14},{8,0},{10,2},{12,4},{14,6},{16,24},{18,... | collective-permute-start | bytes 2211848 | tf_op jit(solution)/shard_map/ppermute | solution.py:596
  196.7 5.0 %copy-start = (bf16[1024,768]{1,0:T(8,128)(2,1)S(1)}, bf16[1024,768]{1,0:T(8,128)(2,1)}, u32[]{:S(2)}) copy-start(bf16[1024,768]{1,0:T(8,128)(2,1)} %get-tuple-element.130) | copy-start | bytes 4718596
  196.8 5.0 %copy-start.11 = (bf16[768,384]{1,0:T(8,128)(2,1)S(1)}, bf16[768,384]{1,0:T(8,128)(2,1)}, u32[]{:S(2)}) copy-start(bf16[768,384]{1,0:T(8,128)(2,1)} %copy-done.9) | copy-start | bytes 1769476
  196.8 32.7 %collective-permute-start.32 = (f32[48,2688]{1,0:T(8,128)S(1)}, f32[48,2688]{1,0:T(8,128)S(1)}, u32[]{:S(2)}, u32[]{:S(2)}) collective-permute-start(f32[48,2688]{1,0:T(8,128)S(1)} %get-tuple-element.187), channel_id=1, source_target_pairs={{0,16},{2,18},{4,20},{6,22},{8,24},{10,26},{12,28},{14,30},{16,0},... | collective-permute-start | bytes 1548296 | tf_op jit(solution)/shard_map/ppermute | solution.py:596
  199.6 24.5 %collective-permute-start.21 = (f32[200,768]{1,0:T(8,128)S(1)}, f32[200,768]{1,0:T(8,128)S(1)}, u32[]{:S(2)}, u32[]{:S(2)}) collective-permute-start(f32[200,768]{1,0:T(8,128)S(1)} %get-tuple-element.185), channel_id=1, source_target_pairs={{0,4},{2,6},{4,0},{6,2},{8,12},{10,14},{12,8},{14,10},{16,20},{18,... | collective-permute-start | bytes 1843208 | tf_op jit(solution)/shard_map/ppermute | solution.py:596
  201.2 25.9 %collective-permute-start.23 = (f32[200,768]{1,0:T(8,128)S(1)}, f32[200,768]{1,0:T(8,128)S(1)}, u32[]{:S(2)}, u32[]{:S(2)}) collective-permute-start(f32[200,768]{1,0:T(8,128)S(1)} %get-tuple-element.184), channel_id=1, source_target_pairs={{0,4},{2,6},{4,0},{6,2},{8,12},{10,14},{12,8},{14,10},{16,20},{18,... | collective-permute-start | bytes 1843208 | tf_op jit(solution)/shard_map/ppermute | solution.py:596
  222.4 17.8 %collective-permute-start.31 = (f32[48,1920]{1,0:T(8,128)S(1)}, f32[48,1920]{1,0:T(8,128)S(1)}, u32[]{:S(2)}, u32[]{:S(2)}) collective-permute-start(f32[48,1920]{1,0:T(8,128)S(1)} %get-tuple-element.190), channel_id=1, source_target_pairs={{0,16},{2,18},{4,20},{6,22},{8,24},{10,26},{12,28},{14,30},{16,0},... | collective-permute-start | bytes 1105928 | tf_op jit(solution)/shard_map/ppermute | solution.py:596
  227.2 3.8 %copy-start.13 = (f32[512,384]{1,0:T(8,128)S(1)}, f32[512,384]{1,0:T(8,128)}, u32[]{:S(2)}) copy-start(f32[512,384]{1,0:T(8,128)} %get-tuple-element.82) | copy-start | bytes 2359300
  227.2 3.8 %copy-start.14 = (f32[512,384]{1,0:T(8,128)S(1)}, f32[512,384]{1,0:T(8,128)}, u32[]{:S(2)}) copy-start(f32[512,384]{1,0:T(8,128)} %get-tuple-element.129) | copy-start | bytes 2359300
  227.2 17.4 %collective-permute-start.25 = (f32[104,768]{1,0:T(8,128)S(1)}, f32[104,768]{1,0:T(8,128)S(1)}, u32[]{:S(2)}, u32[]{:S(2)}) collective-permute-start(f32[104,768]{1,0:T(8,128)S(1)} %slice_add_fusion.13), channel_id=1, source_target_pairs={{0,8},{2,10},{4,12},{6,14},{8,0},{10,2},{12,4},{14,6},{16,24},{18,... | collective-permute-start | bytes 958472 | tf_op jit(solution)/shard_map/ppermute | solution.py:596
  227.9 21.8 %collective-permute-start.27 = (f32[104,768]{1,0:T(8,128)S(1)}, f32[104,768]{1,0:T(8,128)S(1)}, u32[]{:S(2)}, u32[]{:S(2)}) collective-permute-start(f32[104,768]{1,0:T(8,128)S(1)} %slice_add_fusion.12), channel_id=1, source_target_pairs={{0,8},{2,10},{4,12},{6,14},{8,0},{10,2},{12,4},{14,6},{16,24},{18,... | collective-permute-start | bytes 958472 | tf_op jit(solution)/shard_map/ppermute | solution.py:596
  244.7 13.1 %collective-permute-start.26 = (f32[56,768]{1,0:T(8,128)S(1)}, f32[56,768]{1,0:T(8,128)S(1)}, u32[]{:S(2)}, u32[]{:S(2)}) collective-permute-start(f32[56,768]{1,0:T(8,128)S(1)} %slice_add_fusion.17), channel_id=1, source_target_pairs={{0,16},{2,18},{4,20},{6,22},{8,24},{10,26},{12,28},{14,30},{16,0},... | collective-permute-start | bytes 516104 | tf_op jit(solution)/shard_map/ppermute | solution.py:596
  249.7 10.4 %collective-permute-start.28 = (f32[56,768]{1,0:T(8,128)S(1)}, f32[56,768]{1,0:T(8,128)S(1)}, u32[]{:S(2)}, u32[]{:S(2)}) collective-permute-start(f32[56,768]{1,0:T(8,128)S(1)} %slice_add_fusion.16), channel_id=1, source_target_pairs={{0,16},{2,18},{4,20},{6,22},{8,24},{10,26},{12,28},{14,30},{16,0},... | collective-permute-start | bytes 516104 | tf_op jit(solution)/shard_map/ppermute | solution.py:596
  260.2 4.2 %collective-permute-start.29 = (f32[9,768]{1,0:T(8,128)S(1)}, f32[9,768]{1,0:T(8,128)S(1)}, u32[]{:S(2)}, u32[]{:S(2)}) collective-permute-start(f32[9,768]{1,0:T(8,128)S(1)} %pad_maximum_fusion.4), channel_id=1, source_target_pairs={{0,1},{1,0},{2,3},{3,2},{4,5},{5,4},{6,7},{7,6},{8,9},{9,8},{10,11... | collective-permute-start | bytes 82952 | tf_op jit(solution)/shard_map/ppermute | solution.py:593
